TPU v7x, 128 devices: a whole 4x4x4 slice. The times are simulated.
128 devices in a mesh: seq: 32 (over z, y, core), head: 4 (over x).
Axes of the slice: x: 4, y: 4, z: 4, core: 2. Of those that a mesh axis runs over, the one named last changes fastest.
Arguments:
- tokens: bfloat16 [65536, 1024], P(('seq', 'head')), may hold values from -6 to 6
- w_gate_x: bfloat16 [1024, 4096], replicated, may hold values from -0.1875 to 0.1875
- w_bc_dt: bfloat16 [1024, 160], replicated, may hold values from -0.1875 to 0.1875
- conv_x_weight: float32 [4, 2048], P(None, 'head'), may hold values from -0.5 to 0.5
- conv_x_bias: float32 [2048], P('head'), may hold values from -0.5 to 0.5
- conv_bc_weight: float32 [4, 128], replicated, may hold values from -0.5 to 0.5
- conv_bc_bias: float32 [128], replicated, may hold values from -0.5 to 0.5
- dt_bias: float32 [32], P('head'), may hold values from -9 to -1
- a_log: float32 [32], P('head'), may hold values from -4 to 1
- skip_d: float32 [32], P('head'), may hold values from 0.5 to 1.5
- norm_gain: float32 [2048], replicated, may hold values from 0.1 to 1.9
- w_out: bfloat16 [2048, 1024], replicated, may hold values from -0.125 to 0.125
Outputs:
- mixed: bfloat16 [65536, 1024], P(('seq', 'head'))
All inputs are finite; a program needn't handle non-finite values.
Results may differ from a plain program's by a relative error of at most 0.009.
Values may be sent and summed in bfloat16 or wider, within the bound.
No kernel may reach another device: no remote copies, remote signals or barrier semaphores. Data moves between devices by JAX's collectives and lax.ppermute only.
A program may use at most 128 MiB of HBM per device.

v0:
```python
import jax
import jax.numpy as jnp
from jax import lax
from jax.sharding import PartitionSpec as P

HEADS = 32
HEAD_DIM = 64
STATE = 64
GROUP = 256
CONV = 4


epsilon = 1e-05


def from_behind(array, axis, by):
    size = lax.axis_size(axis)
    pairs = [(i, i + by) for i in range(size) if 0 <= i + by < size]
    return lax.ppermute(array, axis, pairs)


def prefix(array, axis, combine, identity):
    size, mine = (lax.axis_size(axis), lax.axis_index(axis))
    everything = jax.tree.map(lambda part: lax.all_gather(part, axis), array)
    start = jax.tree.map(
        lambda part, zero: jnp.broadcast_to(jnp.asarray(zero, part.dtype), part.shape),
        array,
        identity,
    )

    def hop(k, before):
        reached = k < mine
        new = combine(before, jax.tree.map(lambda part: part[k], everything))
        return jax.tree.map(lambda a, b: jnp.where(reached, a, b), new, before)

    return lax.fori_loop(0, size, hop, start)


def causal_taps(padded, weights, biases, count):
    summed = biases + weights[0] * padded[0:count]
    for tap_index in range(1, CONV):
        summed = summed + weights[tap_index] * padded[tap_index : tap_index + count]
    return jax.nn.silu(summed).astype(jnp.bfloat16)


def on_device(
    tokens,
    w_gate_x,
    w_bc_dt,
    conv_x_weight,
    conv_x_bias,
    conv_bc_weight,
    conv_bc_bias,
    dt_bias,
    a_log,
    skip_d,
    norm_gain,
    w_out,
):
    highest = lax.Precision.HIGHEST
    heads_here = dt_bias.shape[0]
    dinner_here = heads_here * HEAD_DIM
    tok_rows = tokens.shape[0]
    gate_all = jnp.dot(tokens, w_gate_x, preferred_element_type=jnp.float32).astype(jnp.bfloat16)
    gate_all = gate_all.reshape(tok_rows, HEADS, 2 * HEAD_DIM)
    bc_dt = jnp.dot(tokens, w_bc_dt, preferred_element_type=jnp.float32).astype(jnp.bfloat16)
    dt_all = bc_dt[:, 2 * STATE :].reshape(tok_rows, HEADS, 1)
    gate_x, dt_raw = (
        lax.all_to_all(gate_all, "head", split_axis=1, concat_axis=0, tiled=True),
        lax.all_to_all(dt_all, "head", split_axis=1, concat_axis=0, tiled=True),
    )
    dt_raw = dt_raw[:, :, 0]
    bc_rows = lax.all_gather(bc_dt[:, : 2 * STATE], "head", axis=0, tiled=True)
    seq_rows = gate_x.shape[0]
    gate_z = gate_x[:, :, :HEAD_DIM]
    x_chan = gate_x[:, :, HEAD_DIM:].reshape(seq_rows, dinner_here)
    conv_input = jnp.concatenate([x_chan, bc_rows], axis=1)
    rim_rows = from_behind(conv_input[seq_rows - (CONV - 1) :], "seq", 1)
    padded = jnp.concatenate([rim_rows, conv_input], axis=0).astype(jnp.float32)
    conv_weights = jnp.concatenate([conv_x_weight, conv_bc_weight], axis=1)
    conv_biases = jnp.concatenate([conv_x_bias, conv_bc_bias], axis=0)
    conved = causal_taps(padded, conv_weights, conv_biases, seq_rows)
    x_heads = conved[:, :dinner_here].astype(jnp.float32).reshape(seq_rows, heads_here, HEAD_DIM)
    b_mat = conved[:, dinner_here : dinner_here + STATE].astype(jnp.float32)
    c_mat = conved[:, dinner_here + STATE :].astype(jnp.float32)
    dt_step = jax.nn.softplus(dt_raw.astype(jnp.float32) + dt_bias)
    log_decay = dt_step * -jnp.exp(a_log)
    x_dt = x_heads * dt_step[:, :, None]
    blocks = seq_rows // GROUP
    decay_blocks = log_decay.reshape(blocks, GROUP, heads_here)
    xdt_blocks = x_dt.reshape(blocks, GROUP, heads_here, HEAD_DIM)
    b_blocks = b_mat.reshape(blocks, GROUP, STATE)
    c_blocks = c_mat.reshape(blocks, GROUP, STATE)
    cumlog = jnp.cumsum(decay_blocks, axis=1)
    scores = jnp.einsum("ktn,ksn->kts", c_blocks, b_blocks, precision=highest)
    by_head = jnp.swapaxes(cumlog, 1, 2)
    gaps = by_head[:, :, :, None] - by_head[:, :, None, :]
    causal = jnp.arange(GROUP)[:, None] >= jnp.arange(GROUP)[None, :]
    decays = jnp.where(causal[None, None], jnp.exp(jnp.minimum(gaps, 0.0)), 0.0)
    mixed = scores[:, None] * decays
    y_intra = jnp.einsum("khts,kshp->kthp", mixed, xdt_blocks, precision=highest)
    block_ends = cumlog[:, -1, :]
    to_end = jnp.exp(block_ends[:, None, :] - cumlog)
    local_states = jnp.einsum(
        "kshp,ksn->khpn", to_end[..., None] * xdt_blocks, b_blocks, precision=highest
    )

    def chain_step(carried, inputs):
        block_decay, fresh = inputs
        return (block_decay[:, None, None] * carried + fresh, carried)

    zero_state = jnp.zeros((heads_here, HEAD_DIM, STATE), jnp.float32)
    device_state, block_starts = lax.scan(
        chain_step, zero_state, (jnp.exp(block_ends), local_states)
    )
    total_log = jnp.sum(block_ends, axis=0)

    def combine(earlier, latter):
        return (earlier[0] + latter[0], earlier[1] * jnp.exp(latter[0])[:, None, None] + latter[1])

    prefix_log, incoming = prefix(
        (total_log, device_state), "seq", combine, (jnp.zeros_like(total_log), zero_state)
    )
    offset = jnp.cumsum(block_ends, axis=0) - block_ends
    start_states = block_starts + jnp.exp(offset)[:, :, None, None] * incoming[None]
    y_state = jnp.exp(cumlog)[..., None] * jnp.einsum(
        "ktn,khpn->kthp", c_blocks, start_states, precision=highest
    )
    y_heads = (y_intra + y_state).reshape(seq_rows, heads_here, HEAD_DIM) + skip_d[
        None, :, None
    ] * x_heads
    gated_out = (
        (y_heads * jax.nn.silu(gate_z.astype(jnp.float32)))
        .astype(jnp.bfloat16)
        .reshape(seq_rows, dinner_here)
    )
    by_token = lax.all_to_all(gated_out, "head", split_axis=0, concat_axis=1, tiled=True)
    gated_f = by_token.astype(jnp.float32)
    mean_sq = jnp.mean(gated_f * gated_f, axis=1, keepdims=True)
    normed = (gated_f * lax.rsqrt(mean_sq + epsilon) * norm_gain).astype(jnp.bfloat16)
    return jnp.dot(normed, w_out, preferred_element_type=jnp.float32).astype(jnp.bfloat16)


def solution(mesh):
    return jax.shard_map(
        on_device,
        mesh=mesh,
        in_specs=(
            P(("seq", "head"), None),
            P(),
            P(),
            P(None, "head"),
            P("head"),
            P(),
            P(),
            P("head"),
            P("head"),
            P("head"),
            P(),
            P(),
        ),
        out_specs=P(("seq", "head"), None),
        check_vma=False,
    )
```

profile of v0, /device:TPU:1, one launch (start us, length us, event | category | flops | bytes accessed | tf_op | source)
XLA Modules:
  0.0 319.8 jit_solution(6159652783522887039)
XLA Ops:
  6.5 1.2 copy-done
  7.8 1.5 convolution_convert_fusion.2
  9.8 0.8 reduce.13
  11.3 4.8 %all-to-all-start.1 = ((bf16[4,2,2048]{2,1,0:T(2,128)(2,1)}), bf16[4,2,2048]{2,1,0:T(2,128)(2,1)S(1)}, u32[]{:S(2)}, u32[]{:S(2)}) async-start(bf16[4,2,2048]{2,1,0:T(2,128)(2,1)} %reshape.184), calls=%async_computation.1 | async-start | bytes 65536 | tf_op jit(solution)/shard_map/all_to_all | solution.py:70
  16.1 8.1 %fusion.28 = bf16[64,32,8,128]{3,2,1,0:T(8,128)(2,1)S(1)} fusion(bf16[512,1024]{1,0:T(8,128)(2,1)S(1)} %copy-done, bf16[1024,4096]{1,0:T(8,128)(2,1)} %param.17), kind=kOutput, calls=%fused_computation.46 | convolution fusion | flops 4297064448 | bytes 13631488 | tf_op jit(solution)/shard_map/dot_general | solution.py:64
  24.3 3.1 copy.123
  27.4 5.0 %all-to-all-start = ((bf16[512,32,128]{2,0,1:T(8,128)(2,1)}), bf16[512,32,128]{2,0,1:T(8,128)(2,1)}, u32[]{:S(2)}, u32[]{:S(2)}) async-start(bf16[512,32,128]{2,0,1:T(8,128)(2,1)} %bitcast.113), calls=%async_computation | async-start | bytes 8388608 | tf_op jit(solution)/shard_map/all_to_all | solution.py:69
  32.7 53.4 %all_gather.15 = bf16[2048,128]{0,1:T(8,128)(2,1)S(1)} all-gather(bf16[512,128]{0,1:T(8,128)(2,1)S(1)} %slice.78), channel_id=1, replica_groups=mesh['seq'=32,'head'=4] {'head'}, dimensions={0}, use_global_device_ids=true | all-gather | bytes 655360 | tf_op jit(solution)/shard_map/all_gather | solution.py:73
  86.2 4.5 %reduce-window.6 = f32[8,8,2,128]{3,1,2,0:T(8,128)S(1)} reduce-window(f32[8,8,2,128]{3,1,2,0:T(8,128)S(1)} %get-tuple-element.196, f32[]{:T(128)} %constant.58.clone.1), window={size=1x1x1x128 pad=0_0x0_0x0_0x127_0}, to_apply=%region_0.1 | reduce-window | flops 2080768 | bytes 131076 | tf_op jit(solution)/shard_map/reduce-window
  91.5 4.9 %copy.73 = bf16[4,512,8,128]{3,2,1,0:T(8,128)(2,1)S(1)} copy(bf16[4,512,8,128]{3,1,2,0:T(8,128)(2,1)} %bitcast.2) | data formatting | bytes 8388608 | tf_op jit(solution)/shard_map/all_to_all | solution.py:69
  96.4 4.0 %fusion.44 = (bf16[2048,8,64]{2,1,0:T(8,128)(2,1)}, bf16[2048,8,64]{2,1,0:T(8,128)(2,1)}) fusion(bf16[2048,8,128]{2,1,0:T(8,128)(2,1)S(1)} %bitcast.109), kind=kLoop, calls=%fused_computation.87 | loop fusion | bytes 8388608 | tf_op jit(solution)/shard_map/slice | solution.py:76
  100.4 4.5 %copy.74 = bf16[2048,8,64]{0,2,1:T(8,128)(2,1)S(1)} copy(bf16[2048,8,64]{2,1,0:T(8,128)(2,1)} %get-tuple-element.198) | data formatting | bytes 4194304 | tf_op jit(solution)/shard_map/slice | solution.py:76
  105.0 7.5 %collective-permute-start = (bf16[3,640]{0,1:T(8,128)(2,1)S(1)}, bf16[3,640]{0,1:T(8,128)(2,1)S(1)}, u32[]{:S(2)}, u32[]{:S(2)}) collective-permute-start(bf16[3,640]{0,1:T(8,128)(2,1)S(1)} %pad_maximum_fusion), channel_id=1, source_target_pairs={{0,4},{4,8},{8,12},{12,16},{16,20},{20,24},{24,28},{28,32},{32,36}... | collective-permute-start | bytes 11528 | tf_op jit(solution)/shard_map/ppermute | solution.py:19
  112.6 2.0 collective-permute-done
  114.6 1.1 maximum_convert_fusion
  115.8 5.2 %multiply_convert_fusion = bf16[2048,640]{0,1:T(8,128)(2,1)S(1)} fusion(f32[2051,640]{0,1:T(8,128)S(1)} %maximum_convert_fusion, f32[640]{0:T(1024)S(1)} %get-tuple-element.169, f32[640]{0:T(1024)S(1)} %get-tuple-element.170, f32[640]{0:T(1024)S(1)} %get-tuple-element.171, f32[640]{0:T(1024)S(1)} %get-tuple-element.168, f32[640]{0:T(1024)S(1)} %pad_maximum_fusion.1), kind=kLoop, calls=%fused_computation.29 | loop fusion | flops 17039360 | bytes 23605760 | tf_op jit(solution)/shard_map/convert_element_type | solution.py:43
  121.6 2.0 copy.102
  124.1 2.5 broadcast_multiply_fusion
  126.6 3.0 fusion.24
  129.6 6.8 %while.27 = (s32[]{:T(128)}, f32[8,64,64]{2,1,0:T(8,128)S(1)}, f32[8,8,64,64]{3,2,1,0:T(8,128)}, f32[8,8]{1,0:T(8,128)S(1)}, f32[8,8,64,64]{3,2,1,0:T(8,128)S(1)}, /*index=5*/s32[]{:T(128)}, s32[]{:T(128)}) while((s32[]{:T(128)}, f32[8,64,64]{2,1,0:T(8,128)S(1)}, f32[8,8,64,64]{3,2,1,0:T(8,128)}, f32[8,8]{1,0:T(8,128)S(1)}, ...), condition=%wide.region_3.4_spmd.clone, body=%wide.region_2.3_spmd.clone.sunk | while | flops 131075 | bytes 786636 | solution.py:113
  132.2 0.7 bitcast_dynamic-update-slice_fusion.2
  138.7 65.6 %all-reduce = f32[256]{0:T(256)S(1)} all-reduce(f32[256]{0:T(256)S(1)} %dynamic-update-slice), channel_id=2, replica_groups=mesh['seq'=32,'head'=4] {'seq'}, use_global_device_ids=true, to_apply=%add | all-reduce | flops 256 | bytes 2048
  204.5 4.5 %copy.97 = bf16[2048,8,64]{0,2,1:T(8,128)(2,1)S(1)} copy(bf16[2048,8,64]{2,1,0:T(8,128)(2,1)} %get-tuple-element.199) | data formatting | bytes 4194304
  209.5 22.5 %fusion.2 = f32[8,8,64,256]{3,2,1,0:T(8,128)} fusion(f32[8,8,256]{2,1,0:T(8,128)S(1)} %add_bitcast_fusion.1, f32[8,256,256]{2,1,0:T(8,128)S(1)} %fusion.33, pred[256,256]{1,0:T(8,128)(4,1)S(1)} %iota_compare_fusion, f32[8,256,8,64]{1,0,3,2:T(8,128)} %get-tuple-element.195), kind=kOutput, calls=%fused_computation.7 | convolution fusion | flops 3238002688 | bytes 10616832 | tf_op jit(solution)/shard_map/khts,kshp->kthp/dot_general | solution.py:101
  232.0 35.1 %while.28 = (s32[]{:T(128)}, f32[8,64,64]{2,1,0:T(8,128)S(1)}, s32[]{:T(128)}, f32[32,8]{1,0:T(8,128)S(1)}, f32[32,8,64,64]{3,2,1,0:T(8,128)}, /*index=5*/s32[]{:T(128)}, s32[]{:T(128)}) while((s32[]{:T(128)}, f32[8,64,64]{2,1,0:T(8,128)S(1)}, s32[]{:T(128)}, f32[32,8]{1,0:T(8,128)S(1)}, f32[32,8,64,64]{3,2,1,0:T(8,128)}, ...), condition=%wide.region_7.8_spmd.clone, body=%wide.region_6.7_spmd.clone.sunk | while | flops 131076 | bytes 393425 | solution.py:36
  232.0 1.1 fusion.55
  233.1 1.1 fusion.55
  234.2 1.1 fusion.55
  235.3 1.1 fusion.55
  236.4 1.1 fusion.55
  237.5 1.1 fusion.55
  238.6 1.1 fusion.55
  239.7 1.1 fusion.55
  240.8 1.1 fusion.55
  241.9 1.1 fusion.55
  243.0 1.1 fusion.55
  244.1 1.1 fusion.55
  245.2 1.1 fusion.55
  246.3 1.1 fusion.55
  247.4 1.1 fusion.55
  248.5 1.1 fusion.55
  249.6 1.1 fusion.55
  250.7 1.1 fusion.55
  251.8 1.1 fusion.55
  252.9 1.1 fusion.55
  254.0 1.1 fusion.55
  255.1 1.1 fusion.55
  256.2 1.1 fusion.55
  257.3 1.1 fusion.55
  258.4 1.1 fusion.55
  259.5 1.1 fusion.55
  260.6 1.1 fusion.55
  261.7 1.1 fusion.55
  262.8 1.1 fusion.55
  263.9 1.1 fusion.55
  265.0 1.1 fusion.55
  266.1 1.1 fusion.55
  267.2 4.9 %fusion.23 = f32[8,8,8,8,256]{4,3,2,1,0:T(8,128)S(1)} fusion(f32[8,8,64,256]{3,2,1,0:T(8,128)} %fusion.2, f32[8,8,64,64]{3,2,1,0:T(8,128)} %get-tuple-element.127, f32[8,256,8]{1,2,0:T(8,128)S(1)} %get-tuple-element.192, f32[8,64,64]{2,1,0:T(8,128)S(1)} %get-tuple-element.129, f32[8,8]{1,0:T(8,128)S(1)} %get-tuple-element.202, ...), kind=kOutput, calls=%fused_computation.39 | convolution fusion | flops 807927808 | bytes 9896192 | tf_op jit(solution)/shard_map/ktn,khpn->kthp/dot_general | solution.py:126
  272.7 1.5 copy-done.3
  274.2 2.9 fusion.27
  277.1 3.3 %all_to_all.35 = bf16[4,512,512]{1,0,2:T(4,128)(2,1)S(1)} reshape(bf16[2048,8,64]{0,2,1:T(8,128)(2,1)} %fusion.27) | data formatting | bytes 4194304 | tf_op jit(solution)/shard_map/all_to_all | solution.py:137
  280.9 26.5 %all_to_all.40 = bf16[4,512,512]{1,2,0:T(8,128)(2,1)S(1)} all-to-all(bf16[4,512,512]{1,2,0:T(8,128)(2,1)S(1)} %copy.88), channel_id=1, replica_groups=mesh['seq'=32,'head'=4] {'head'}, dimensions={0} | all-to-all | bytes 4194304 | tf_op jit(solution)/shard_map/all_to_all | solution.py:137
  308.5 1.1 copy-done.12
  309.6 3.4 %convolution_convert_fusion.1 = bf16[512,1024]{1,0:T(8,128)(2,1)} fusion(bf16[512,2048]{0,1:T(8,128)(2,1)S(1)} %fusion.22, bf16[2048,1024]{1,0:T(8,128)(2,1)S(1)} %copy-done.12), kind=kOutput, calls=%fused_computation.52 | convolution fusion | flops 2148007936 | bytes 7340032 | tf_op jit(solution)/shard_map/dot_general | solution.py:141
  (132 shorter events, 14.1 us)
Async XLA Ops:
  6.5 1.2 copy-start
  11.3 16.1 %all-to-all-start.1 = ((bf16[4,2,2048]{2,1,0:T(2,128)(2,1)}), bf16[4,2,2048]{2,1,0:T(2,128)(2,1)S(1)}, u32[]{:S(2)}, u32[]{:S(2)}) async-start(bf16[4,2,2048]{2,1,0:T(2,128)(2,1)} %reshape.184), calls=%async_computation.1 | async-start | bytes 65536 | tf_op jit(solution)/shard_map/all_to_all | solution.py:70
  27.4 5.1 %copy-start.6 = (f32[4,512]{1,0:T(4,128)S(1)}, f32[4,512]{1,0:T(4,128)}, u32[]{:S(2)}) copy-start(f32[4,512]{1,0:T(4,128)} %param.19) | copy-start | bytes 24580
  27.4 5.2 %copy-start.7 = (f32[4,128]{1,0:T(4,128)S(1)}, f32[4,128]{1,0:T(4,128)}, u32[]{:S(2)}) copy-start(f32[4,128]{1,0:T(4,128)} %param.21) | copy-start | bytes 6148
  27.4 5.2 %copy-start.8 = (f32[512]{0:T(512)S(1)}, f32[512]{0:T(512)}, u32[]{:S(2)}) copy-start(f32[512]{0:T(512)} %param.20) | copy-start | bytes 6148
  27.4 5.2 %copy-start.11 = (f32[128]{0:T(128)S(1)}, f32[128]{0:T(128)}, u32[]{:S(2)}) copy-start(f32[128]{0:T(128)} %param.22) | copy-start | bytes 1540
  27.4 58.6 %copy-start.13 = (f32[8]{0:T(128)S(1)}, f32[8]{0:T(128)}, u32[]{:S(2)}) copy-start(f32[8]{0:T(128)} %param.24) | copy-start | bytes 100
  27.4 58.7 %copy-start.9 = (f32[8]{0:T(128)S(1)}, f32[8]{0:T(128)}, u32[]{:S(2)}) copy-start(f32[8]{0:T(128)} %param.23) | copy-start | bytes 100
  27.4 64.1 %all-to-all-start = ((bf16[512,32,128]{2,0,1:T(8,128)(2,1)}), bf16[512,32,128]{2,0,1:T(8,128)(2,1)}, u32[]{:S(2)}, u32[]{:S(2)}) async-start(bf16[512,32,128]{2,0,1:T(8,128)(2,1)} %bitcast.113), calls=%async_computation | async-start | bytes 8388608 | tf_op jit(solution)/shard_map/all_to_all | solution.py:69
  32.4 199.6 %all-gather.4.cloned.1.call-start = ((), (), s32[]{:S(2)}) async-start(), calls=%async_computation.3 | async-start | bytes 8650752 | tf_op jit(solution)/shard_map/all_gather | solution.py:24
  105.0 9.6 %collective-permute-start = (bf16[3,640]{0,1:T(8,128)(2,1)S(1)}, bf16[3,640]{0,1:T(8,128)(2,1)S(1)}, u32[]{:S(2)}, u32[]{:S(2)}) collective-permute-start(bf16[3,640]{0,1:T(8,128)(2,1)S(1)} %pad_maximum_fusion), channel_id=1, source_target_pairs={{0,4},{4,8},{8,12},{12,16},{16,20},{20,24},{24,28},{28,32},{32,36}... | collective-permute-start | bytes 11528 | tf_op jit(solution)/shard_map/ppermute | solution.py:19
  121.6 2.5 copy-start.2
  129.6 7.6 %copy-start.14 = (u32[128]{0:T(128)S(1)}, u32[128]{0:T(128)}, u32[]{:S(2)}) copy-start(u32[128]{0:T(128)} %constant.66) | copy-start | bytes 1540
  136.4 0.7 copy-start.4
  272.0 2.2 copy-start.3
  272.1 2.2 copy-start.10
  280.9 27.0 %copy-start.5 = (f32[2048]{0:T(1024)S(1)}, f32[2048]{0:T(1024)}, u32[]{:S(2)}) copy-start(f32[2048]{0:T(1024)} %param.26) | copy-start | bytes 24580
  307.4 2.2 copy-start.12
  307.9 5.0 %copy-start.1 = (bf16[512,1024]{1,0:T(8,128)(2,1)S(1)}, bf16[512,1024]{1,0:T(8,128)(2,1)}, u32[]{:S(2)}) copy-start(bf16[512,1024]{1,0:T(8,128)(2,1)} %param.16) | copy-start | bytes 3145732
Sparse Core Ops, SparseCore 0:
  137.3 55.1 all-gather.3
where the time goes:
time: 323 us; the launch traced here: 320 us
  blocking collectives  145 us (45%)
  other arithmetic  59.8 us (19%)
  matrix products  43.9 us (14%)
  local copies, waits for them, and re-layouts  35.4 us (11%)
  starting transfers between devices  17.4 us (5%)
  between operations  14.5 us (4%)
    unnamed x1, blocking collectives  65.6 us
    all_gather x1, blocking collectives, on_device(): bc_rows = lax.all_gather(bc_dt[:, :2 * STATE], 'head', axis=0, tiled=True)  53.4 us
    select_n x32, other arithmetic, hop(): return jax.tree.map(lambda a, b: jnp.where(reached, a, b), new, before)  33.7 us
    all_to_all x1, blocking collectives, on_device(): lax.all_to_all(gated_out, 'head', split_axis=0, concat_axis=1, tiled=True)  26.5 us
    dot_general x1, matrix products, on_device(): jnp.einsum('khts,kshp->kthp', mixed, xdt_blocks, precision=highest)  22.5 us
    unnamed x42, local copies, waits for them, and re-layouts  13.7 us
    slice x2, local copies, waits for them, and re-layouts, on_device(): x_chan = gate_x[:, :, HEAD_DIM:].reshape(seq_rows, dinner_here)  8.44 us
    dot_general x1, matrix products, on_device(): jnp.dot(tokens, w_gate_x, preferred_element_type=jnp.float32)  8.12 us
  transfers between devices with their start and end apart: 4, of which 1 were waited for; matrix products, arithmetic and copies ran while one was open for 14% of the time, Pallas kernels for 0%

commit v1 on v0

v1 whole, which is shorter than its diff:
```python
import functools

import jax
import jax.numpy as jnp
from jax import lax
from jax.experimental import pallas as pl
from jax.experimental.pallas import tpu as pltpu
from jax.sharding import PartitionSpec as P

HEADS = 32
HEAD_DIM = 64
STATE = 64
CONV = 4
DINNER = HEADS * HEAD_DIM
BC = 2 * STATE
SUB = 128
EPSILON = 1e-05
BOTH = ("seq", "head")
F32 = jnp.float32
BF16 = jnp.bfloat16
LIMIT = 56 * 1024 * 1024


def params(steps=1):
    return pltpu.CompilerParams(
        dimension_semantics=("arbitrary",) * steps, vmem_limit_bytes=LIMIT
    )


def silu(v):
    half = 0.5 * v
    return half + half * jnp.tanh(half)


def hi_lo(v, axis):
    hi = v.astype(BF16)
    lo = (v - hi.astype(F32)).astype(BF16)
    return jnp.concatenate([hi, lo], axis=axis)


def dot(a, b):
    return jnp.dot(a, b, preferred_element_type=F32)


def one_hot(first_channel, width):
    row = lax.broadcasted_iota(jnp.int32, (2 * HEADS, width), 0)
    chan = lax.broadcasted_iota(jnp.int32, (2 * HEADS, width), 1) + first_channel
    return ((row % HEADS) == (chan // HEAD_DIM)).astype(F32).astype(BF16)


def project_kernel(tok_ref, w_ref, wbc_ref, x_ref, z_ref, tail_ref, bc_ref, dt_ref):
    j = pl.program_id(0)
    width = x_ref.shape[1]
    rows = tok_ref.shape[0]

    @pl.when(j == 0)
    def _():
        small = dot(tok_ref[...], wbc_ref[...])
        bc = small[:, :BC]
        bc_ref[...] = bc.astype(BF16)
        dt_ref[...] = small[:, BC:].astype(BF16).astype(F32)
        tail_ref[:, DINNER:] = bc[rows - 8 :].astype(BF16)

    full = dot(tok_ref[...], w_ref[...])
    lane = lax.broadcasted_iota(jnp.int32, (1, 128), 1) < HEAD_DIM
    for pair in range(width // 128):
        a = full[:, pair * 256 : pair * 256 + 128]
        b = full[:, pair * 256 + 128 : pair * 256 + 256]
        cols = slice(pair * 128, pair * 128 + 128)
        z_ref[:, cols] = jnp.where(lane, a, pltpu.roll(b, HEAD_DIM, 1)).astype(BF16)
        x = jnp.where(lane, pltpu.roll(a, HEAD_DIM, 1), b).astype(BF16)
        x_ref[:, cols] = x
        start = pl.multiple_of(j * width + pair * 128, 128)
        tail_ref[:, pl.ds(start, 128)] = x[rows - 8 :]


def project(tokens, w_gate_x, w_bc_dt):
    rows, depth = tokens.shape
    width = 256
    return pl.pallas_call(
        project_kernel,
        grid=(DINNER // width,),
        in_specs=[
            pl.BlockSpec((rows, depth), lambda j: (0, 0)),
            pl.BlockSpec((depth, 2 * width), lambda j: (0, j)),
            pl.BlockSpec(w_bc_dt.shape, lambda j: (0, 0)),
        ],
        out_specs=[
            pl.BlockSpec((rows, width), lambda j: (0, j)),
            pl.BlockSpec((rows, width), lambda j: (0, j)),
            pl.BlockSpec((8, DINNER + BC), lambda j: (0, 0)),
            pl.BlockSpec((rows, BC), lambda j: (0, 0)),
            pl.BlockSpec((rows, HEADS), lambda j: (0, 0)),
        ],
        out_shape=[
            jax.ShapeDtypeStruct((rows, DINNER), BF16),
            jax.ShapeDtypeStruct((rows, DINNER), BF16),
            jax.ShapeDtypeStruct((8, DINNER + BC), BF16),
            jax.ShapeDtypeStruct((rows, BC), BF16),
            jax.ShapeDtypeStruct((rows, HEADS), F32),
        ],
        compiler_params=params(),
        name="project",
    )(tokens, w_gate_x, w_bc_dt)


def taps(buf_ref, start, count, weights, bias):
    summed = bias
    for k in range(CONV):
        summed = summed + weights[k : k + 1] * buf_ref[pl.ds(start + 5 + k, count), :]
    return silu(summed)


def state_kernel(
    x_ref, halo_ref, bc_ref, dtraw_ref, par_ref, parall_ref, wbc_ref, bbc_ref,
    xc_ref, bcout_ref, dt_ref, cum_ref, slab_ref,
    buf, bcbuf, wgt, bt,
):
    g = pl.program_id(0)
    rows, width = x_ref.shape

    @pl.when(g == 0)
    def _():
        dt_bias = jnp.sum(parall_ref[:, 6, :HEADS], axis=0, keepdims=True)
        a_log = jnp.sum(parall_ref[:, 7, :HEADS], axis=0, keepdims=True)
        raw = dtraw_ref[...] + dt_bias
        step = jnp.maximum(raw, 0.0) + jnp.log1p(jnp.exp(-jnp.abs(raw)))
        decay = step * -jnp.exp(a_log)
        r = lax.broadcasted_iota(jnp.int32, (SUB, SUB), 0)
        c = lax.broadcasted_iota(jnp.int32, (SUB, SUB), 1)
        ones = (r >= c).astype(F32)
        before = jnp.zeros((1, HEADS), F32)
        parts = []
        for k in range(rows // SUB):
            part = before + jnp.dot(
                ones, decay[k * SUB : (k + 1) * SUB],
                precision=lax.Precision.HIGHEST, preferred_element_type=F32,
            )
            before = part[SUB - 1 : SUB]
            parts.append(part)
        cum = jnp.concatenate(parts, axis=0)
        dt_ref[...] = step
        cum_ref[...] = cum
        wgt[0:rows] = hi_lo(step * jnp.exp(before - cum), 1)
        total = hi_lo(jnp.exp(before), 1)
        zero = jnp.zeros((1, HEADS), BF16)
        wgt[rows : rows + 8] = jnp.concatenate(
            [
                jnp.concatenate([total[:, :HEADS], zero], axis=1),
                jnp.concatenate([zero, total[:, HEADS:]], axis=1),
                jnp.zeros((6, 2 * HEADS), BF16),
            ],
            axis=0,
        )
        bcbuf[0:8] = halo_ref[:, DINNER:].astype(F32)
        bcbuf[8 : 8 + rows] = bc_ref[...].astype(F32)
        conved = taps(bcbuf, 0, rows, wbc_ref[...], bbc_ref[...])
        bcout_ref[...] = conved.astype(BF16)
        bt[...] = conved.T[:STATE].astype(BF16)

    start = pl.multiple_of(g * width, width)
    buf[0:8] = halo_ref[:, pl.ds(start, width)].astype(F32)
    buf[8 : 8 + rows] = x_ref[...].astype(F32)
    spread = dot(wgt[...], one_hot(g * width, width))
    state = jnp.zeros((STATE, width), F32)
    for k in range(rows // SUB):
        here = slice(k * SUB, (k + 1) * SUB)
        xc = taps(buf, k * SUB, SUB, par_ref[0, 0:4], par_ref[0, 4:5]).astype(BF16)
        xc_ref[here] = xc
        weighted = (xc.astype(F32) * spread[here]).astype(BF16)
        state = state + dot(bt[:, here], weighted)
    extra = spread[rows : rows + 8]
    for c in range(width // 128):
        cols = slice(c * 128, c * 128 + 128)
        for r in range(STATE // 8):
            slab_ref[r, c, 0:8] = state[r * 8 : r * 8 + 8, cols].astype(BF16)
            slab_ref[r, c, 8:16] = extra[:, cols].astype(BF16)


def local_state(x, halo, bc, dt_raw, packed, conv_bc_weight, conv_bc_bias):
    rows = x.shape[0]
    width = 256
    per = packed.shape[2] // width

    def whole(a):
        return pl.BlockSpec(a.shape, lambda g: (0,) * a.ndim)

    return pl.pallas_call(
        state_kernel,
        grid=(DINNER // width,),
        in_specs=[
            pl.BlockSpec((rows, width), lambda g: (0, g)),
            whole(halo),
            whole(bc),
            whole(dt_raw),
            pl.BlockSpec((1, 8, width), lambda g: (g // per, 0, g % per)),
            whole(packed),
            whole(conv_bc_weight),
            whole(conv_bc_bias),
        ],
        out_specs=[
            pl.BlockSpec((rows, width), lambda g: (0, g)),
            pl.BlockSpec((rows, BC), lambda g: (0, 0)),
            pl.BlockSpec((rows, HEADS), lambda g: (0, 0)),
            pl.BlockSpec((rows, HEADS), lambda g: (0, 0)),
            pl.BlockSpec((STATE // 8, width // 128, 16, 128), lambda g: (0, g, 0, 0)),
        ],
        out_shape=[
            jax.ShapeDtypeStruct((rows, DINNER), BF16),
            jax.ShapeDtypeStruct((rows, BC), BF16),
            jax.ShapeDtypeStruct((rows, HEADS), F32),
            jax.ShapeDtypeStruct((rows, HEADS), F32),
            jax.ShapeDtypeStruct((STATE // 8, DINNER // 128, 16, 128), BF16),
        ],
        scratch_shapes=[
            pltpu.VMEM((rows + 8, width), F32),
            pltpu.VMEM((rows + 8, BC), F32),
            pltpu.VMEM((rows + 8, 2 * HEADS), BF16),
            pltpu.VMEM((STATE, rows), BF16),
        ],
        compiler_params=params(),
        name="local_state",
    )(x, halo, bc, dt_raw, packed, packed, conv_bc_weight, conv_bc_bias)


def intra_kernel(
    base, xc_ref, z_ref, bc_ref, dt_ref, cum_ref, par_ref,
    own_ref, scale_ref,
    scores, rowlog, bt, wgt,
):
    g = pl.program_id(0)
    rows, width = xc_ref.shape
    blocks = rows // SUB
    heads = width // HEAD_DIM

    @pl.when(g == 0)
    def _():
        bt[...] = bc_ref[...].astype(F32).T[:STATE].astype(BF16)
        for k in range(blocks):
            here = slice(k * SUB, (k + 1) * SUB)
            scores[here] = dot(bc_ref[here, STATE:], bt[:, here])
        cum = cum_ref[...]
        step = dt_ref[...]
        by_row = (cum - jnp.log(step)).T
        for group in range(HEADS // heads):
            rowlog[group, 0:heads] = by_row[group * heads : (group + 1) * heads]
        starts, ends = [], []
        before = jnp.zeros((1, HEADS), F32)
        for k in range(blocks):
            here = slice(k * SUB, (k + 1) * SUB)
            starts.append(jnp.broadcast_to(before, (SUB, HEADS)))
            before = cum[(k + 1) * SUB - 1 : (k + 1) * SUB]
            ends.append(jnp.broadcast_to(before, (SUB, HEADS)))
        starts = jnp.concatenate(starts, axis=0)
        ends = jnp.concatenate(ends, axis=0)
        wgt[0:rows] = hi_lo(step * jnp.exp(ends - cum), 1)
        wgt[rows : 2 * rows] = hi_lo(jnp.exp(cum - starts), 1)
        wgt[2 * rows : 3 * rows] = hi_lo(jnp.exp(cum), 1)

    first = base + g * width
    spread = one_hot(first, width)
    first_head = (base // width + g) * heads
    r = lax.broadcasted_iota(jnp.int32, (SUB, SUB), 0)
    c = lax.broadcasted_iota(jnp.int32, (SUB, SUB), 1)
    causal = r >= c
    lane = lax.broadcasted_iota(jnp.int32, (1, HEADS), 1)
    skip = par_ref[0, 5:6]
    state = jnp.zeros((STATE, width), F32)
    for k in range(blocks):
        here = slice(k * SUB, (k + 1) * SUB)
        xc = xc_ref[here]
        pieces = []
        for h in range(heads):
            head = first_head + h
            col = jnp.sum(
                jnp.where(lane == head, cum_ref[here], 0.0), axis=1, keepdims=True
            )
            row = rowlog[base // width + g, h : h + 1, here]
            decay = jnp.exp(jnp.where(causal, col - row, -jnp.inf))
            mixed = (scores[here] * decay).astype(BF16)
            pieces.append(dot(mixed, xc[:, h * HEAD_DIM : (h + 1) * HEAD_DIM]))
        y = jnp.concatenate(pieces, axis=1)
        xf = xc.astype(F32)
        grow = dot(wgt[rows + k * SUB : rows + (k + 1) * SUB], spread)
        if k > 0:
            y = y + grow * dot(bc_ref[here, STATE:], state.astype(BF16))
        if k + 1 < blocks:
            shrink = dot(wgt[here], spread)
            fresh = dot(bt[:, here], (xf * shrink).astype(BF16))
            state = state * grow[SUB - 1 : SUB] + fresh
        gate = silu(z_ref[here].astype(F32))
        own_ref[here] = (y + skip * xf) * gate
        full = dot(wgt[2 * rows + k * SUB : 2 * rows + (k + 1) * SUB], spread)
        scale_ref[here] = (full * gate).astype(BF16)


def intra(half, halves, xc, z, bc, dt, cum, packed):
    rows = xc.shape[0]
    width = 256
    span = DINNER // halves
    steps = span // width
    per = packed.shape[2] // width

    def whole(a):
        return pl.BlockSpec(a.shape, lambda g: (0,) * a.ndim)

    return pl.pallas_call(
        functools.partial(intra_kernel, half * span),
        grid=(steps,),
        in_specs=[
            pl.BlockSpec((rows, width), lambda g: (0, g + half * steps)),
            pl.BlockSpec((rows, width), lambda g: (0, g + half * steps)),
            whole(bc),
            whole(dt),
            whole(cum),
            pl.BlockSpec(
                (1, 8, width),
                lambda g: ((g + half * steps) // per, 0, (g + half * steps) % per),
            ),
        ],
        out_specs=[
            pl.BlockSpec((rows, width), lambda g: (0, g)),
            pl.BlockSpec((rows, width), lambda g: (0, g)),
        ],
        out_shape=[
            jax.ShapeDtypeStruct((rows, span), F32),
            jax.ShapeDtypeStruct((rows, span), BF16),
        ],
        scratch_shapes=[
            pltpu.VMEM((rows, SUB), F32),
            pltpu.VMEM((DINNER // width, 8, rows), F32),
            pltpu.VMEM((STATE, rows), BF16),
            pltpu.VMEM((3 * rows, 2 * HEADS), BF16),
        ],
        compiler_params=params(),
        name="intra",
    )(xc, z, bc, dt, cum, packed)


def scan_kernel(in_ref, out_ref):
    count = in_ref.shape[0]
    state = jnp.zeros((8, 128), F32)
    for q in range(count):
        out_ref[q] = state.astype(BF16)
        slab = in_ref[q].astype(F32)
        state = state * (slab[8:9] + slab[9:10]) + slab[0:8]


def scan_devices(slabs):
    count = slabs.shape[0]
    return pl.pallas_call(
        scan_kernel,
        out_shape=jax.ShapeDtypeStruct((count, 8, 128), BF16),
        compiler_params=params(0),
        name="scan_devices",
    )(slabs)


def finish_kernel(c_ref, slab_ref, own0, own1, scale0, scale1, gain_ref, w_ref,
                  out_ref, acc, squares):
    g = pl.program_id(0)
    last = pl.num_programs(0) - 1
    half = pl.num_programs(0) // 2
    columns = slab_ref.shape[1]
    slabs = [
        slab_ref[:, c].astype(F32).reshape(STATE, 128).astype(BF16)
        for c in range(columns)
    ]
    carried = dot(c_ref[:, STATE:], jnp.concatenate(slabs, axis=1))

    def step(own_ref, scale_ref):
        gated = (own_ref[...] + scale_ref[...].astype(F32) * carried).astype(BF16)
        gated = gated.astype(F32)
        part = jnp.sum(gated * gated, axis=1, keepdims=True)
        product = dot((gated * gain_ref[...]).astype(BF16), w_ref[...])

        @pl.when(g == 0)
        def _():
            acc[...] = product
            squares[...] = part

        @pl.when(g > 0)
        def _():
            acc[...] += product
            squares[...] += part

    @pl.when(g < half)
    def _():
        step(own0, scale0)

    @pl.when(g >= half)
    def _():
        step(own1, scale1)

    @pl.when(g == last)
    def _():
        scale = lax.rsqrt(squares[...] * (1.0 / DINNER) + EPSILON)
        out_ref[...] = (acc[...] * scale).astype(BF16)


def finish(bc, slabs, owns, scales, norm_gain, w_out):
    rows = bc.shape[0]
    width = 512
    steps = DINNER // width
    half = steps // 2
    columns = w_out.shape[1]

    def first(g):
        return (0, jnp.minimum(g, half - 1))

    def second(g):
        return (0, jnp.maximum(g - half, 0))

    return pl.pallas_call(
        finish_kernel,
        grid=(steps,),
        in_specs=[
            pl.BlockSpec(bc.shape, lambda g: (0, 0)),
            pl.BlockSpec((STATE // 8, width // 128, 8, 128), lambda g: (0, g, 0, 0)),
            pl.BlockSpec((rows, width), first),
            pl.BlockSpec((rows, width), second),
            pl.BlockSpec((rows, width), first),
            pl.BlockSpec((rows, width), second),
            pl.BlockSpec((1, width), lambda g: (0, g)),
            pl.BlockSpec((width, columns), lambda g: (g, 0)),
        ],
        out_specs=pl.BlockSpec((rows, columns), lambda g: (0, 0)),
        out_shape=jax.ShapeDtypeStruct((rows, columns), BF16),
        scratch_shapes=[pltpu.VMEM((rows, columns), F32), pltpu.VMEM((rows, 1), F32)],
        compiler_params=params(),
        name="finish",
    )(bc, slabs, owns[0], owns[1], scales[0], scales[1], norm_gain, w_out)


def gather_params(conv_x_weight, conv_x_bias, dt_bias, a_log, skip_d):
    n = lax.axis_size("head")
    me = lax.axis_index("head")
    wide = conv_x_bias.shape[0]
    here = dt_bias.shape[0]
    mine = (jnp.arange(wide) // here) == me
    packed = jnp.concatenate(
        [
            conv_x_weight,
            conv_x_bias[None],
            jnp.repeat(skip_d, HEAD_DIM)[None],
            jnp.where(mine, jnp.tile(dt_bias, wide // here), 0.0)[None],
            jnp.where(mine, jnp.tile(a_log, wide // here), 0.0)[None],
        ],
        axis=0,
    )
    ring = [packed]
    for k in range(1, n):
        pairs = [(i, (i - k) % n) for i in range(n)]
        ring.append(lax.ppermute(packed, "head", pairs))
    twice = jnp.stack(ring + ring[: n - 1])
    return lax.dynamic_slice_in_dim(twice, (n - me) % n, n, axis=0)


def on_device(
    tokens, w_gate_x, w_bc_dt, conv_x_weight, conv_x_bias, conv_bc_weight,
    conv_bc_bias, dt_bias, a_log, skip_d, norm_gain, w_out,
):
    devices = lax.axis_size("seq") * lax.axis_size("head")
    packed = gather_params(conv_x_weight, conv_x_bias, dt_bias, a_log, skip_d)
    x, z, tail, bc_raw, dt_raw = project(tokens, w_gate_x, w_bc_dt)
    halo = lax.ppermute(tail, BOTH, [(i, i + 1) for i in range(devices - 1)])
    xc, bc, dt, cum, slabs = local_state(
        x, halo, bc_raw, dt_raw, packed, conv_bc_weight, conv_bc_bias[None]
    )
    slabs = slabs.reshape(devices, 16, 128)
    by_owner = lax.all_to_all(slabs, BOTH, 0, 0, tiled=True)
    own0, scale0 = intra(0, 2, xc, z, bc, dt, cum, packed)
    incoming = scan_devices(by_owner)
    back = lax.all_to_all(incoming, BOTH, 0, 0, tiled=True)
    xc, incoming = lax.optimization_barrier((xc, incoming))
    own1, scale1 = intra(1, 2, xc, z, bc, dt, cum, packed)
    back = back.reshape(STATE // 8, DINNER // 128, 8, 128)
    return finish(bc, back, (own0, own1), (scale0, scale1), norm_gain[None], w_out)


def solution(mesh):
    return jax.shard_map(
        on_device,
        mesh=mesh,
        in_specs=(
            P(BOTH, None),
            P(),
            P(),
            P(None, "head"),
            P("head"),
            P(),
            P(),
            P("head"),
            P("head"),
            P("head"),
            P(),
            P(),
        ),
        out_specs=P(BOTH, None),
        check_vma=False,
    )
```

time: 323 us -> 96.6 us (0.30)
  blocking collectives: 145 us -> 23.8 us
  other arithmetic: 59.8 us -> 0.01 us
  Pallas kernels: 0 us -> 50.1 us
  matrix products: 43.9 us -> 0 us
  local copies, waits for them, and re-layouts: 35.4 us -> 6.96 us
  between operations: 14.5 us -> 0.14 us
  starting transfers between devices: 17.4 us -> 11.7 us
    unnamed x1 -> x0, blocking collectives: 65.6 us -> none
    all_gather x1 -> x0, blocking collectives: 53.4 us -> none  [on_device(): bc_rows = lax.all_gather(bc_dt[:, :2 * STATE], 'head', axis=0, tiled=True)]
    pallas_call x0 -> x6, Pallas kernels: none -> 50.1 us  [the longest x2 17.7 us: intra(): pl.pallas_call(functools.partial(intra_kernel, half * span), grid=(steps,...]
    dot_general x7 -> x0, matrix products: 43.9 us -> none  [the longest x1 22.5 us: on_device(): jnp.einsum('khts,kshp->kthp', mixed, xdt_blocks, precision=highest)]
    select_n x32 -> x1, other arithmetic: 33.7 us -> 0.01 us  [gather_params(): jnp.where(mine, jnp.tile(a_log, wide // here), 0.0)[None]]
    unnamed x42 -> x11, local copies, waits for them, and re-layouts: 13.7 us -> 3.3 us
    convert_element_type x5 -> x0, other arithmetic: 10.3 us -> none  [the longest x1 5.21 us: causal_taps(): return jax.nn.silu(summed).astype(jnp.bfloat16)]
    slice x7 -> x0, local copies, waits for them, and re-layouts: 8.76 us -> none  [the longest x2 8.44 us: on_device(): x_chan = gate_x[:, :, HEAD_DIM:].reshape(seq_rows, dinner_here)]
  transfers between devices with their start and end apart: 4 -> 5, of which waited for: 1 -> 1; matrix products, arithmetic and copies ran while one was open for 14% -> 3% of each run, Pallas kernels for 0% -> 31%
where the time goes in v1:
time: 96.6 us; the launch traced here: 95.8 us
  Pallas kernels  50.1 us (52%)
  blocking collectives  23.8 us (25%)
  starting transfers between devices  11.7 us (12%)
  local copies, waits for them, and re-layouts  6.96 us (7%)
  waiting for transfers between devices  3.02 us (3%)
    all_to_all x1, blocking collectives, on_device(): by_owner = lax.all_to_all(slabs, BOTH, 0, 0, tiled=True)  23.8 us
    pallas_call x2, Pallas kernels, intra(): pl.pallas_call(functools.partial(intra_kernel, half * span), grid=(steps,...  17.7 us
    pallas_call x1, Pallas kernels, project(): pl.pallas_call(project_kernel, grid=(DINNER // width,), in_specs=[pl.Bloc...  11.6 us
    pallas_call x1, Pallas kernels, local_state(): pl.pallas_call(state_kernel, grid=(DINNER // width,), in_specs=[pl.BlockS...  9.8 us
    pallas_call x1, Pallas kernels, finish(): pl.pallas_call(finish_kernel, grid=(steps,), in_specs=[pl.BlockSpec(bc.sh...  9.04 us
    ppermute x3, starting transfers between devices, gather_params(): ring.append(lax.ppermute(packed, 'head', pairs))  4.5 us
    all_to_all x1, starting transfers between devices, on_device(): back = lax.all_to_all(incoming, BOTH, 0, 0, tiled=True)  3.8 us
    ppermute x1, starting transfers between devices, on_device(): halo = lax.ppermute(tail, BOTH, [(i, i + 1) for i in range(devices - 1)])  3.42 us
  transfers between devices with their start and end apart: 5, of which 1 were waited for; matrix products, arithmetic and copies ran while one was open for 3% of the time, Pallas kernels for 31%

profile of v1, /device:TPU:1, one launch (start us, length us, event | category | flops | bytes accessed | tf_op | source)
XLA Modules:
  0.0 95.8 jit_solution(9044775317401167018)
XLA Ops:
  0.0 0.7 tile.20
  0.7 0.1 tile.21
  0.8 0.7 tile.8
  1.4 0.1 tile.9
  1.5 0.7 broadcast_in_dim.20
  2.2 0.1 broadcast_in_dim_reshape.3
  2.3 0.7 concatenate.3
  3.0 3.4 %collective-permute-start.1 = (f32[8,512]{1,0:T(8,128)S(1)}, f32[8,512]{1,0:T(8,128)S(1)}, u32[]{:S(2)}, u32[]{:S(2)}) collective-permute-start(f32[8,512]{1,0:T(8,128)S(1)} %concatenate.3), channel_id=1, source_target_pairs={{0,3},{1,0},{2,1},{3,2},{4,7},{5,4},{6,5},{7,6},{8,11},{9,8},{10,9... | collective-permute-start | bytes 49160 | tf_op jit(solution)/shard_map/ppermute | solution.py:454
  6.4 0.5 collective-permute-start.2
  6.9 0.6 collective-permute-start.3
  7.5 2.0 %copy.14.wbc_ref = bf16[1024,160]{1,0:T(8,128)(2,1)} copy(bf16[1024,160]{0,1:T(8,128)(2,1)} %param.14) | data formatting | bytes 655360 | tf_op args[2]
  9.5 11.6 %project.1 = (bf16[512,2048]{1,0:T(8,128)(2,1)}, bf16[512,2048]{1,0:T(8,128)(2,1)}, bf16[8,2176]{1,0:T(8,128)(2,1)}, bf16[512,128]{1,0:T(8,128)(2,1)}, f32[512,32]{1,0:T(8,128)}) custom-call(bf16[512,1024]{1,0:T(8,128)(2,1)} %tok_ref.1, bf16[1024,4096]{1,0:T(8,128)(2,1)} %w_ref.2, bf16[1024,160]{1,0:T(8,128)(2,1)} %copy.14.wbc_ref), custom_call_target="tpu_custom_call" | custom-call | tf_op jit(solution)/shard_map/project/pallas_call | solution.py:80
  21.1 3.4 %collective-permute-start = (bf16[8,2176]{1,0:T(8,128)(2,1)}, bf16[8,2176]{1,0:T(8,128)(2,1)S(1)}, u32[]{:S(2)}, u32[]{:S(2)}) collective-permute-start(bf16[8,2176]{1,0:T(8,128)(2,1)} %get-tuple-element.21), channel_id=1, source_target_pairs={{0,1},{1,2},{2,3},{3,4},{4,5},{5,6},{6,7},{7,8},{8,9},{9,10},{10,1... | collective-permute-start | bytes 104456 | tf_op jit(solution)/shard_map/ppermute | solution.py:466
  24.5 0.0 collective-permute-done.1
  24.5 0.0 collective-permute-done.2
  24.6 0.0 collective-permute-done.3
  24.6 0.6 constant_dynamic-slice_fusion.par_ref.parall_ref
  25.3 3.0 %collective-permute-done.halo_ref = bf16[8,2176]{1,0:T(8,128)(2,1)S(1)} collective-permute-done((bf16[8,2176]{1,0:T(8,128)(2,1)}, bf16[8,2176]{1,0:T(8,128)(2,1)S(1)}, u32[]{:S(2)}, u32[]{:S(2)}) %collective-permute-start) | collective-permute-done | bytes 34848 | tf_op jit(solution)/shard_map/ppermute | solution.py:466
  28.3 0.0 copy-start.1
  28.3 0.6 copy-done.1
  28.9 9.8 %local_state.1 = (bf16[512,2048]{1,0:T(8,128)(2,1)}, bf16[512,128]{1,0:T(8,128)(2,1)}, f32[512,32]{1,0:T(8,128)}, f32[512,32]{1,0:T(8,128)}, bf16[8,16,16,128]{3,2,1,0:T(8,128)(2,1)}) custom-call(bf16[512,2048]{1,0:T(8,128)(2,1)} %get-tuple-element.20.x_ref, bf16[8,2176]{1,0:T(8,128)(2,1)} %copy-done.1, bf16[512,128]{1,0:T(8,128)(2,1)} %get-tuple-element.22.bc_ref, ...), custom_call_target="tpu_custom_call" | custom-call | tf_op jit(solution)/shard_map/local_state/pallas_call | solution.py:188
  38.7 23.8 %all_to_all.10.in_ref = bf16[128,16,128]{2,1,0:T(8,128)(2,1)} all-to-all(bf16[128,16,128]{2,1,0:T(8,128)(2,1)} %bitcast.17), channel_id=1, replica_groups=mesh['seq'=32,'head'=4] {'seq','head'}, dimensions={0} | all-to-all | bytes 1048576 | tf_op jit(solution)/shard_map/all_to_all | solution.py:471
  62.5 2.0 %scan_devices.1 = bf16[128,8,128]{2,1,0:T(8,128)(2,1)} custom-call(bf16[128,16,128]{2,1,0:T(8,128)(2,1)} %all_to_all.10.in_ref), custom_call_target="tpu_custom_call" | custom-call | tf_op jit(solution)/shard_map/scan_devices/pallas_call | solution.py:351
  64.5 3.8 %all-to-all-start.1 = ((bf16[128,8,128]{2,1,0:T(8,128)(2,1)}), bf16[128,8,128]{2,1,0:T(8,128)(2,1)S(1)}, u32[]{:S(2)}, u32[]{:S(2)}) async-start(bf16[128,8,128]{2,1,0:T(8,128)(2,1)} %scan_devices.1), calls=%async_computation.1 | async-start | bytes 524288 | tf_op jit(solution)/shard_map/all_to_all | solution.py:474
  68.3 8.9 %intra.2 = (f32[512,1024]{1,0:T(8,128)}, bf16[512,1024]{1,0:T(8,128)(2,1)}) custom-call(bf16[512,2048]{1,0:T(8,128)(2,1)} %get-tuple-element.31.xc_ref, bf16[512,2048]{1,0:T(8,128)(2,1)} %get-tuple-element.27.z_ref, bf16[512,128]{1,0:T(8,128)(2,1)} %get-tuple-element.24.bc_ref.c_ref, f32[512,32]{1,0:T(8,128)} %get-tuple-element.28.dt_ref, ...), custom_call_target="tpu_custom_call" | custom-call | tf_op jit(solution)/shard_map/intra/pallas_call | solution.py:307
  77.1 8.9 %intra.3 = (f32[512,1024]{1,0:T(8,128)}, bf16[512,1024]{1,0:T(8,128)(2,1)}) custom-call(bf16[512,2048]{1,0:T(8,128)(2,1)} %get-tuple-element.31.xc_ref, bf16[512,2048]{1,0:T(8,128)(2,1)} %get-tuple-element.27.z_ref, bf16[512,128]{1,0:T(8,128)(2,1)} %get-tuple-element.24.bc_ref.c_ref, f32[512,32]{1,0:T(8,128)} %get-tuple-element.28.dt_ref, ...), custom_call_target="tpu_custom_call" | custom-call | tf_op jit(solution)/shard_map/intra/pallas_call | solution.py:307
  86.0 0.0 all-to-all-done.1
  86.0 0.0 copy-start
  86.0 0.7 copy-done
  86.7 9.0 %finish.1 = bf16[512,1024]{1,0:T(8,128)(2,1)} custom-call(bf16[512,128]{1,0:T(8,128)(2,1)} %get-tuple-element.24.bc_ref.c_ref, bf16[8,16,8,128]{3,2,1,0:T(8,128)(2,1)} %bitcast.16, f32[512,1024]{1,0:T(8,128)} %get-tuple-element.30.own0, f32[512,1024]{1,0:T(8,128)} %get-tuple-element.32.own1, bf16[512,1024]{1,0:T(8,128)(2,1)} %get-tuple-element.33.scale0, ...), custom_call_target="tpu_custom_call" | custom-call | tf_op jit(solution)/shard_map/finish/pallas_call | solution.py:414
  (8 shorter events, 0.0 us)
Async XLA Ops:
  3.0 21.5 %collective-permute-start.1 = (f32[8,512]{1,0:T(8,128)S(1)}, f32[8,512]{1,0:T(8,128)S(1)}, u32[]{:S(2)}, u32[]{:S(2)}) collective-permute-start(f32[8,512]{1,0:T(8,128)S(1)} %concatenate.3), channel_id=1, source_target_pairs={{0,3},{1,0},{2,1},{3,2},{4,7},{5,4},{6,5},{7,6},{8,11},{9,8},{10,9... | collective-permute-start | bytes 49160 | tf_op jit(solution)/shard_map/ppermute | solution.py:454
  6.4 18.1 %collective-permute-start.2 = (f32[8,512]{1,0:T(8,128)S(1)}, f32[8,512]{1,0:T(8,128)S(1)}, u32[]{:S(2)}, u32[]{:S(2)}) collective-permute-start(f32[8,512]{1,0:T(8,128)S(1)} %concatenate.3), channel_id=1, source_target_pairs={{0,2},{1,3},{2,0},{3,1},{4,6},{5,7},{6,4},{7,5},{8,10},{9,11},{10,... | collective-permute-start | bytes 49160 | tf_op jit(solution)/shard_map/ppermute | solution.py:454
  6.9 17.6 %collective-permute-start.3 = (f32[8,512]{1,0:T(8,128)S(1)}, f32[8,512]{1,0:T(8,128)S(1)}, u32[]{:S(2)}, u32[]{:S(2)}) collective-permute-start(f32[8,512]{1,0:T(8,128)S(1)} %concatenate.3), channel_id=1, source_target_pairs={{0,1},{1,2},{2,3},{3,0},{4,5},{5,6},{6,7},{7,4},{8,9},{9,10},{10,1... | collective-permute-start | bytes 49160 | tf_op jit(solution)/shard_map/ppermute | solution.py:454
  21.1 7.2 %collective-permute-start = (bf16[8,2176]{1,0:T(8,128)(2,1)}, bf16[8,2176]{1,0:T(8,128)(2,1)S(1)}, u32[]{:S(2)}, u32[]{:S(2)}) collective-permute-start(bf16[8,2176]{1,0:T(8,128)(2,1)} %get-tuple-element.21), channel_id=1, source_target_pairs={{0,1},{1,2},{2,3},{3,4},{4,5},{5,6},{6,7},{7,8},{8,9},{9,10},{10,1... | collective-permute-start | bytes 104456 | tf_op jit(solution)/shard_map/ppermute | solution.py:466
  28.3 0.6 copy-start.1
  64.5 21.5 %all-to-all-start.1 = ((bf16[128,8,128]{2,1,0:T(8,128)(2,1)}), bf16[128,8,128]{2,1,0:T(8,128)(2,1)S(1)}, u32[]{:S(2)}, u32[]{:S(2)}) async-start(bf16[128,8,128]{2,1,0:T(8,128)(2,1)} %scan_devices.1), calls=%async_computation.1 | async-start | bytes 524288 | tf_op jit(solution)/shard_map/all_to_all | solution.py:474
  86.0 0.7 copy-start

commit v2 on v1

--- a/solution.py
+++ b/solution.py
@@ -14,6 +14,7 @@
 DINNER = HEADS * HEAD_DIM
 BC = 2 * STATE
 SUB = 128
+PAD = 16
 EPSILON = 1e-05
 BOTH = ("seq", "head")
 F32 = jnp.float32
@@ -48,84 +49,93 @@
     return ((row % HEADS) == (chan // HEAD_DIM)).astype(F32).astype(BF16)
 
 
-def project_kernel(tok_ref, w_ref, wbc_ref, x_ref, z_ref, tail_ref, bc_ref, dt_ref):
-    j = pl.program_id(0)
-    width = x_ref.shape[1]
-    rows = tok_ref.shape[0]
-
-    @pl.when(j == 0)
-    def _():
-        small = dot(tok_ref[...], wbc_ref[...])
-        bc = small[:, :BC]
-        bc_ref[...] = bc.astype(BF16)
-        dt_ref[...] = small[:, BC:].astype(BF16).astype(F32)
-        tail_ref[:, DINNER:] = bc[rows - 8 :].astype(BF16)
-
-    full = dot(tok_ref[...], w_ref[...])
-    lane = lax.broadcasted_iota(jnp.int32, (1, 128), 1) < HEAD_DIM
-    for pair in range(width // 128):
-        a = full[:, pair * 256 : pair * 256 + 128]
-        b = full[:, pair * 256 + 128 : pair * 256 + 256]
-        cols = slice(pair * 128, pair * 128 + 128)
-        z_ref[:, cols] = jnp.where(lane, a, pltpu.roll(b, HEAD_DIM, 1)).astype(BF16)
-        x = jnp.where(lane, pltpu.roll(a, HEAD_DIM, 1), b).astype(BF16)
-        x_ref[:, cols] = x
-        start = pl.multiple_of(j * width + pair * 128, 128)
-        tail_ref[:, pl.ds(start, 128)] = x[rows - 8 :]
-
-
-def project(tokens, w_gate_x, w_bc_dt):
+def pack_kernel(w_ref, b_ref, dt_ref, a_ref, skip_ref, tok_ref, out_ref, tail_ref):
+    out_ref[...] = jnp.zeros_like(out_ref)
+    out_ref[0:CONV] = w_ref[...]
+    out_ref[CONV : CONV + 1] = b_ref[...]
+    here = dt_ref.shape[1]
+    for row, ref in ((5, dt_ref), (6, a_ref), (7, skip_ref)):
+        out_ref[row : row + 1, 0:here] = ref[...]
+    tail_ref[...] = tok_ref[...]
+
+
+def pack(weight, bias, dt_bias, a_log, skip_d, tokens):
     rows, depth = tokens.shape
-    width = 256
+    small = (weight, bias[None], dt_bias[None], a_log[None], skip_d[None])
+
+    def whole(a):
+        return pl.BlockSpec(a.shape, lambda g: (0, 0))
+
     return pl.pallas_call(
-        project_kernel,
-        grid=(DINNER // width,),
-        in_specs=[
-            pl.BlockSpec((rows, depth), lambda j: (0, 0)),
-            pl.BlockSpec((depth, 2 * width), lambda j: (0, j)),
-            pl.BlockSpec(w_bc_dt.shape, lambda j: (0, 0)),
-        ],
+        pack_kernel,
+        grid=(1,),
+        in_specs=[whole(a) for a in small]
+        + [pl.BlockSpec((8, depth), lambda g: (rows // 8 - 1, 0))],
         out_specs=[
-            pl.BlockSpec((rows, width), lambda j: (0, j)),
-            pl.BlockSpec((rows, width), lambda j: (0, j)),
-            pl.BlockSpec((8, DINNER + BC), lambda j: (0, 0)),
-            pl.BlockSpec((rows, BC), lambda j: (0, 0)),
-            pl.BlockSpec((rows, HEADS), lambda j: (0, 0)),
+            pl.BlockSpec((8, weight.shape[1]), lambda g: (0, 0)),
+            pl.BlockSpec((8, depth), lambda g: (0, 0)),
         ],
         out_shape=[
-            jax.ShapeDtypeStruct((rows, DINNER), BF16),
-            jax.ShapeDtypeStruct((rows, DINNER), BF16),
-            jax.ShapeDtypeStruct((8, DINNER + BC), BF16),
-            jax.ShapeDtypeStruct((rows, BC), BF16),
-            jax.ShapeDtypeStruct((rows, HEADS), F32),
+            jax.ShapeDtypeStruct((8, weight.shape[1]), F32),
+            jax.ShapeDtypeStruct((8, depth), BF16),
         ],
         compiler_params=params(),
-        name="project",
-    )(tokens, w_gate_x, w_bc_dt)
+        name="pack",
+    )(*small, tokens)
+
+
+def half_lanes(w, which):
+    parts = []
+    for pair in range(w.shape[1] // 256):
+        for k in range(2):
+            at = pair * 256 + k * 128 + which * HEAD_DIM
+            parts.append(w[:, at : at + HEAD_DIM])
+    return jnp.concatenate(parts, axis=1)
 
 
 def taps(buf_ref, start, count, weights, bias):
     summed = bias
     for k in range(CONV):
-        summed = summed + weights[k : k + 1] * buf_ref[pl.ds(start + 5 + k, count), :]
+        at = start + PAD - CONV + 1 + k
+        summed = summed + weights[k : k + 1] * buf_ref[pl.ds(at, count), :]
     return silu(summed)
 
 
 def state_kernel(
-    x_ref, halo_ref, bc_ref, dtraw_ref, par_ref, parall_ref, wbc_ref, bbc_ref,
-    xc_ref, bcout_ref, dt_ref, cum_ref, slab_ref,
-    buf, bcbuf, wgt, bt,
+    me_ref, tok_ref, halo_ref, w_ref, wsmall_ref, p0, p1, p2, p3, wbc_ref, bbc_ref,
+    xc_ref, bcout_ref, dt_ref, cum_ref, skip_ref, slab_ref,
+    tok, buf, bcbuf, wgt, bt, par,
 ):
     g = pl.program_id(0)
-    rows, width = x_ref.shape
+    rows = tok_ref.shape[0]
+    width = xc_ref.shape[1]
+    wide = p0.shape[1]
+    blocks = par.shape[0]
+    each = HEADS // blocks
 
     @pl.when(g == 0)
     def _():
-        dt_bias = jnp.sum(parall_ref[:, 6, :HEADS], axis=0, keepdims=True)
-        a_log = jnp.sum(parall_ref[:, 7, :HEADS], axis=0, keepdims=True)
-        raw = dtraw_ref[...] + dt_bias
+        tok[0 : PAD - 8] = jnp.zeros((PAD - 8, tok.shape[1]), BF16)
+        tok[PAD - 8 : PAD] = halo_ref[...]
+        tok[PAD:] = tok_ref[...]
+        for k, piece in enumerate((p0, p1, p2, p3)):
+            owner = lax.rem(me_ref[0] + k, blocks)
+            par[owner] = piece[...]
+        lane = lax.broadcasted_iota(jnp.int32, (8, 128), 1)
+        heads = jnp.zeros((8, 128), F32)
+        for k in range(blocks):
+            block = par[k, :, 0:128]
+            moved = block if k == 0 else pltpu.roll(block, each * k, 1)
+            heads = jnp.where(lane // each == k, moved, heads)
+        heads = heads[:, :HEADS]
+        small = lax.dot_general(
+            tok[...], wsmall_ref[...], (((1,), (1,)), ((), ())),
+            preferred_element_type=F32,
+        )
+        small = small.astype(BF16).astype(F32)
+        raw = small[PAD:, BC:] + heads[5:6]
         step = jnp.maximum(raw, 0.0) + jnp.log1p(jnp.exp(-jnp.abs(raw)))
-        decay = step * -jnp.exp(a_log)
+        decay = step * -jnp.exp(heads[6:7])
         r = lax.broadcasted_iota(jnp.int32, (SUB, SUB), 0)
         c = lax.broadcasted_iota(jnp.int32, (SUB, SUB), 1)
         ones = (r >= c).astype(F32)
@@ -143,33 +153,36 @@
         cum_ref[...] = cum
         wgt[0:rows] = hi_lo(step * jnp.exp(before - cum), 1)
         total = hi_lo(jnp.exp(before), 1)
+        skips = hi_lo(heads[7:8], 1)
         zero = jnp.zeros((1, HEADS), BF16)
         wgt[rows : rows + 8] = jnp.concatenate(
             [
                 jnp.concatenate([total[:, :HEADS], zero], axis=1),
                 jnp.concatenate([zero, total[:, HEADS:]], axis=1),
-                jnp.zeros((6, 2 * HEADS), BF16),
+                skips,
+                jnp.zeros((5, 2 * HEADS), BF16),
             ],
             axis=0,
         )
-        bcbuf[0:8] = halo_ref[:, DINNER:].astype(F32)
-        bcbuf[8 : 8 + rows] = bc_ref[...].astype(F32)
+        bcbuf[...] = small[:, :BC]
         conved = taps(bcbuf, 0, rows, wbc_ref[...], bbc_ref[...])
         bcout_ref[...] = conved.astype(BF16)
         bt[...] = conved.T[:STATE].astype(BF16)
 
-    start = pl.multiple_of(g * width, width)
-    buf[0:8] = halo_ref[:, pl.ds(start, width)].astype(F32)
-    buf[8 : 8 + rows] = x_ref[...].astype(F32)
+    buf[...] = dot(tok[...], half_lanes(w_ref[...], 1)).astype(BF16).astype(F32)
     spread = dot(wgt[...], one_hot(g * width, width))
+    per = wide // width
+    at = pl.multiple_of(lax.rem(g, per) * width, width)
+    mine = par[g // per, :, pl.ds(at, width)]
     state = jnp.zeros((STATE, width), F32)
     for k in range(rows // SUB):
         here = slice(k * SUB, (k + 1) * SUB)
-        xc = taps(buf, k * SUB, SUB, par_ref[0, 0:4], par_ref[0, 4:5]).astype(BF16)
+        xc = taps(buf, k * SUB, SUB, mine[0:CONV], mine[CONV : CONV + 1]).astype(BF16)
         xc_ref[here] = xc
         weighted = (xc.astype(F32) * spread[here]).astype(BF16)
         state = state + dot(bt[:, here], weighted)
     extra = spread[rows : rows + 8]
+    skip_ref[...] = extra
     for c in range(width // 128):
         cols = slice(c * 128, c * 128 + 128)
         for r in range(STATE // 8):
@@ -177,10 +190,9 @@
             slab_ref[r, c, 8:16] = extra[:, cols].astype(BF16)
 
 
-def local_state(x, halo, bc, dt_raw, packed, conv_bc_weight, conv_bc_bias):
-    rows = x.shape[0]
+def local_state(me, tokens, halo, w_gate_x, w_small, pieces, conv_w, conv_b):
+    rows, depth = tokens.shape
     width = 256
-    per = packed.shape[2] // width
 
     def whole(a):
         return pl.BlockSpec(a.shape, lambda g: (0,) * a.ndim)
@@ -189,20 +201,21 @@
         state_kernel,
         grid=(DINNER // width,),
         in_specs=[
-            pl.BlockSpec((rows, width), lambda g: (0, g)),
+            pl.BlockSpec(memory_space=pltpu.SMEM),
+            whole(tokens),
             whole(halo),
-            whole(bc),
-            whole(dt_raw),
-            pl.BlockSpec((1, 8, width), lambda g: (g // per, 0, g % per)),
-            whole(packed),
-            whole(conv_bc_weight),
-            whole(conv_bc_bias),
+            pl.BlockSpec((depth, 2 * width), lambda g: (0, g)),
+            whole(w_small),
+            *(whole(p) for p in pieces),
+            whole(conv_w),
+            whole(conv_b),
         ],
         out_specs=[
             pl.BlockSpec((rows, width), lambda g: (0, g)),
             pl.BlockSpec((rows, BC), lambda g: (0, 0)),
             pl.BlockSpec((rows, HEADS), lambda g: (0, 0)),
             pl.BlockSpec((rows, HEADS), lambda g: (0, 0)),
+            pl.BlockSpec((8, width), lambda g: (0, g)),
             pl.BlockSpec((STATE // 8, width // 128, 16, 128), lambda g: (0, g, 0, 0)),
         ],
         out_shape=[
@@ -210,21 +223,24 @@
             jax.ShapeDtypeStruct((rows, BC), BF16),
             jax.ShapeDtypeStruct((rows, HEADS), F32),
             jax.ShapeDtypeStruct((rows, HEADS), F32),
+            jax.ShapeDtypeStruct((8, DINNER), F32),
             jax.ShapeDtypeStruct((STATE // 8, DINNER // 128, 16, 128), BF16),
         ],
         scratch_shapes=[
-            pltpu.VMEM((rows + 8, width), F32),
-            pltpu.VMEM((rows + 8, BC), F32),
+            pltpu.VMEM((PAD + rows, depth), BF16),
+            pltpu.VMEM((PAD + rows, width), F32),
+            pltpu.VMEM((PAD + rows, BC), F32),
             pltpu.VMEM((rows + 8, 2 * HEADS), BF16),
             pltpu.VMEM((STATE, rows), BF16),
+            pltpu.VMEM((len(pieces), 8, DINNER // len(pieces)), F32),
         ],
         compiler_params=params(),
         name="local_state",
-    )(x, halo, bc, dt_raw, packed, packed, conv_bc_weight, conv_bc_bias)
+    )(me, tokens, halo, w_gate_x, w_small, *pieces, conv_w, conv_b)
 
 
 def intra_kernel(
-    base, xc_ref, z_ref, bc_ref, dt_ref, cum_ref, par_ref,
+    base, xc_ref, tok_ref, w_ref, bc_ref, dt_ref, cum_ref, par_ref,
     own_ref, scale_ref,
     scores, rowlog, bt, wgt,
 ):
@@ -264,7 +280,8 @@
     c = lax.broadcasted_iota(jnp.int32, (SUB, SUB), 1)
     causal = r >= c
     lane = lax.broadcasted_iota(jnp.int32, (1, HEADS), 1)
-    skip = par_ref[0, 5:6]
+    skip = par_ref[2:3]
+    z = dot(tok_ref[...], half_lanes(w_ref[...], 0)).astype(BF16).astype(F32)
     state = jnp.zeros((STATE, width), F32)
     for k in range(blocks):
         here = slice(k * SUB, (k + 1) * SUB)
@@ -288,19 +305,18 @@
             shrink = dot(wgt[here], spread)
             fresh = dot(bt[:, here], (xf * shrink).astype(BF16))
             state = state * grow[SUB - 1 : SUB] + fresh
-        gate = silu(z_ref[here].astype(F32))
+        gate = silu(z[here])
         own_ref[here] = (y + skip * xf) * gate
         full = dot(wgt[2 * rows + k * SUB : 2 * rows + (k + 1) * SUB], spread)
         scale_ref[here] = (full * gate).astype(BF16)
 
 
-def intra(half, halves, xc, z, bc, dt, cum, packed):
+def intra(half, halves, xc, tokens, w_gate_x, bc, dt, cum, skips):
     rows = xc.shape[0]
+    depth = tokens.shape[1]
     width = 256
     span = DINNER // halves
     steps = span // width
-    per = packed.shape[2] // width
-
     def whole(a):
         return pl.BlockSpec(a.shape, lambda g: (0,) * a.ndim)
 
@@ -309,14 +325,12 @@
         grid=(steps,),
         in_specs=[
             pl.BlockSpec((rows, width), lambda g: (0, g + half * steps)),
-            pl.BlockSpec((rows, width), lambda g: (0, g + half * steps)),
+            whole(tokens),
+            pl.BlockSpec((depth, 2 * width), lambda g: (0, g + half * steps)),
             whole(bc),
             whole(dt),
             whole(cum),
-            pl.BlockSpec(
-                (1, 8, width),
-                lambda g: ((g + half * steps) // per, 0, (g + half * steps) % per),
-            ),
+            pl.BlockSpec((8, width), lambda g: (0, g + half * steps)),
         ],
         out_specs=[
             pl.BlockSpec((rows, width), lambda g: (0, g)),
@@ -334,7 +348,7 @@
         ],
         compiler_params=params(),
         name="intra",
-    )(xc, z, bc, dt, cum, packed)
+    )(xc, tokens, w_gate_x, bc, dt, cum, skips)
 
 
 def scan_kernel(in_ref, out_ref):
@@ -432,48 +446,32 @@
     )(bc, slabs, owns[0], owns[1], scales[0], scales[1], norm_gain, w_out)
 
 
-def gather_params(conv_x_weight, conv_x_bias, dt_bias, a_log, skip_d):
-    n = lax.axis_size("head")
-    me = lax.axis_index("head")
-    wide = conv_x_bias.shape[0]
-    here = dt_bias.shape[0]
-    mine = (jnp.arange(wide) // here) == me
-    packed = jnp.concatenate(
-        [
-            conv_x_weight,
-            conv_x_bias[None],
-            jnp.repeat(skip_d, HEAD_DIM)[None],
-            jnp.where(mine, jnp.tile(dt_bias, wide // here), 0.0)[None],
-            jnp.where(mine, jnp.tile(a_log, wide // here), 0.0)[None],
-        ],
-        axis=0,
-    )
-    ring = [packed]
-    for k in range(1, n):
-        pairs = [(i, (i - k) % n) for i in range(n)]
-        ring.append(lax.ppermute(packed, "head", pairs))
-    twice = jnp.stack(ring + ring[: n - 1])
-    return lax.dynamic_slice_in_dim(twice, (n - me) % n, n, axis=0)
-
-
 def on_device(
     tokens, w_gate_x, w_bc_dt, conv_x_weight, conv_x_bias, conv_bc_weight,
     conv_bc_bias, dt_bias, a_log, skip_d, norm_gain, w_out,
 ):
-    devices = lax.axis_size("seq") * lax.axis_size("head")
-    packed = gather_params(conv_x_weight, conv_x_bias, dt_bias, a_log, skip_d)
-    x, z, tail, bc_raw, dt_raw = project(tokens, w_gate_x, w_bc_dt)
+    n = lax.axis_size("head")
+    devices = lax.axis_size("seq") * n
+    me = lax.axis_index("head")[None]
+    packed, tail = pack(conv_x_weight, conv_x_bias, dt_bias, a_log, skip_d, tokens)
     halo = lax.ppermute(tail, BOTH, [(i, i + 1) for i in range(devices - 1)])
-    xc, bc, dt, cum, slabs = local_state(
-        x, halo, bc_raw, dt_raw, packed, conv_bc_weight, conv_bc_bias[None]
+    pieces = [packed]
+    for k in range(1, n):
+        pairs = [(i, (i - k) % n) for i in range(n)]
+        pieces.append(lax.ppermute(packed, "head", pairs))
+    xc, bc, dt, cum, skips, slabs = local_state(
+        me, tokens, halo, w_gate_x, w_bc_dt.T, pieces,
+        conv_bc_weight, conv_bc_bias[None],
     )
     slabs = slabs.reshape(devices, 16, 128)
     by_owner = lax.all_to_all(slabs, BOTH, 0, 0, tiled=True)
-    own0, scale0 = intra(0, 2, xc, z, bc, dt, cum, packed)
+    rest = (tokens, w_gate_x, bc, dt, cum, skips)
+    own0, scale0 = intra(0, 2, xc, *rest)
+    by_owner, own0 = lax.optimization_barrier((by_owner, own0))
     incoming = scan_devices(by_owner)
     back = lax.all_to_all(incoming, BOTH, 0, 0, tiled=True)
     xc, incoming = lax.optimization_barrier((xc, incoming))
-    own1, scale1 = intra(1, 2, xc, z, bc, dt, cum, packed)
+    own1, scale1 = intra(1, 2, xc, *rest)
     back = back.reshape(STATE // 8, DINNER // 128, 8, 128)
     return finish(bc, back, (own0, own1), (scale0, scale1), norm_gain[None], w_out)
 

time: 96.6 us -> 83.6 us (0.87)
  blocking collectives: 23.8 us -> 0 us
  starting transfers between devices: 11.7 us -> 26.1 us
  local copies, waits for them, and re-layouts: 6.96 us -> 2.08 us
  waiting for transfers between devices: 3.02 us -> 6.69 us
  Pallas kernels: 50.1 us -> 48.3 us
    all_to_all x1 -> x0, blocking collectives: 23.8 us -> none  [on_device(): by_owner = lax.all_to_all(slabs, BOTH, 0, 0, tiled=True)]
    all_to_all x0 -> x1, starting transfers between devices: none -> 11 us  [on_device(): by_owner = lax.all_to_all(slabs, BOTH, 0, 0, tiled=True)]
    pallas_call x1, Pallas kernels: 11.6 us -> 1.41 us  [pack(): pl.pallas_call(pack_kernel, grid=(1,), in_specs=[whole(a) for a in small]...]
    pallas_call x1, Pallas kernels: 9.8 us -> 14.2 us  [local_state(): pl.pallas_call(state_kernel, grid=(DINNER // width,), in_specs=[pl.BlockS...]
    pallas_call x2, Pallas kernels: 17.7 us -> 21.6 us  [intra(): pl.pallas_call(functools.partial(intra_kernel, half * span), grid=(steps,...]
    all_to_all x0 -> x1, waiting for transfers between devices: none -> 3.2 us  [on_device(): by_owner = lax.all_to_all(slabs, BOTH, 0, 0, tiled=True)]
    ppermute x1, waiting for transfers between devices: 3.01 us -> 0.01 us  [on_device(): halo = lax.ppermute(tail, BOTH, [(i, i + 1) for i in range(devices - 1)])]
    ppermute x3, waiting for transfers between devices: 0.01 us -> 2.93 us  [on_device(): pieces.append(lax.ppermute(packed, 'head', pairs))]
  transfers between devices with their start and end apart: 5 -> 6, of which waited for: 1 -> 4; matrix products, arithmetic and copies ran while one was open for 3% -> 0% of each run, Pallas kernels for 31% -> 26%
where the time goes in v2:
time: 83.6 us; the launch traced here: 83.2 us
  Pallas kernels  48.3 us (58%)
  starting transfers between devices  26.1 us (31%)
  waiting for transfers between devices  6.69 us (8%)
  local copies, waits for them, and re-layouts  2.08 us (2%)
    pallas_call x2, Pallas kernels, intra(): pl.pallas_call(functools.partial(intra_kernel, half * span), grid=(steps,...  21.6 us
    pallas_call x1, Pallas kernels, local_state(): pl.pallas_call(state_kernel, grid=(DINNER // width,), in_specs=[pl.BlockS...  14.2 us
    all_to_all x1, starting transfers between devices, on_device(): by_owner = lax.all_to_all(slabs, BOTH, 0, 0, tiled=True)  11 us
    pallas_call x1, Pallas kernels, finish(): pl.pallas_call(finish_kernel, grid=(steps,), in_specs=[pl.BlockSpec(bc.sh...  9.04 us
    all_to_all x1, starting transfers between devices, on_device(): back = lax.all_to_all(incoming, BOTH, 0, 0, tiled=True)  6.56 us
    ppermute x3, starting transfers between devices, on_device(): pieces.append(lax.ppermute(packed, 'head', pairs))  4.59 us
    ppermute x1, starting transfers between devices, on_device(): halo = lax.ppermute(tail, BOTH, [(i, i + 1) for i in range(devices - 1)])  3.94 us
    all_to_all x1, waiting for transfers between devices, on_device(): by_owner = lax.all_to_all(slabs, BOTH, 0, 0, tiled=True)  3.2 us
  transfers between devices with their start and end apart: 6, of which 4 were waited for; matrix products, arithmetic and copies ran while one was open for 0% of the time, Pallas kernels for 26%

profile of v2, /device:TPU:1, one launch (start us, length us, event | category | flops | bytes accessed | tf_op | source)
XLA Modules:
  0.0 83.2 jit_solution(17655871977196631265)
XLA Ops:
  0.0 1.4 %pack.1 = (f32[8,512]{1,0:T(8,128)}, bf16[8,1024]{1,0:T(8,128)(2,1)}) custom-call(f32[4,512]{1,0:T(4,128)} %w_ref.5, f32[1,512]{1,0:T(1,128)} %bitcast.14, f32[1,8]{1,0:T(1,128)} %bitcast.15, f32[1,8]{1,0:T(1,128)} %bitcast.16, f32[1,8]{1,0:T(1,128)} %bitcast.17, bf16[512,1024]{1,0:T(8,128)(2,1)} %tok_ref.7), custom_call_target="tpu_custom_call" | custom-call | tf_op jit(solution)/shard_map/pack/pallas_call | solution.py:69
  1.4 3.9 %collective-permute-start = (bf16[8,1024]{1,0:T(8,128)(2,1)}, bf16[8,1024]{1,0:T(8,128)(2,1)S(1)}, u32[]{:S(2)}, u32[]{:S(2)}) collective-permute-start(bf16[8,1024]{1,0:T(8,128)(2,1)} %get-tuple-element.20), channel_id=1, source_target_pairs={{0,1},{1,2},{2,3},{3,4},{4,5},{5,6},{6,7},{7,8},{8,9},{9,10},{10,1... | collective-permute-start | bytes 49160 | tf_op jit(solution)/shard_map/ppermute | solution.py:457
  5.4 1.3 %collective-permute-start.3 = (f32[8,512]{1,0:T(8,128)}, f32[8,512]{1,0:T(8,128)S(1)}, u32[]{:S(2)}, u32[]{:S(2)}) collective-permute-start(f32[8,512]{1,0:T(8,128)} %get-tuple-element.21.p0), channel_id=1, source_target_pairs={{0,1},{1,2},{2,3},{3,0},{4,5},{5,6},{6,7},{7,4},{8,9},{9,10},{10,1... | collective-permute-start | bytes 49160 | tf_op jit(solution)/shard_map/ppermute | solution.py:461
  6.6 3.0 %collective-permute-start.2 = (f32[8,512]{1,0:T(8,128)}, f32[8,512]{1,0:T(8,128)S(1)}, u32[]{:S(2)}, u32[]{:S(2)}) collective-permute-start(f32[8,512]{1,0:T(8,128)} %get-tuple-element.21.p0), channel_id=1, source_target_pairs={{0,2},{1,3},{2,0},{3,1},{4,6},{5,7},{6,4},{7,5},{8,10},{9,11},{10,... | collective-permute-start | bytes 49160 | tf_op jit(solution)/shard_map/ppermute | solution.py:461
  9.7 0.3 collective-permute-start.1
  10.0 0.0 collective-permute-done.halo_ref
  10.0 0.0 copy-start.2
  10.0 0.0 collective-permute-done.3.p3
  10.0 0.0 copy-start.3
  10.0 1.2 %collective-permute-done.2.p2 = f32[8,512]{1,0:T(8,128)S(1)} collective-permute-done((f32[8,512]{1,0:T(8,128)}, f32[8,512]{1,0:T(8,128)S(1)}, u32[]{:S(2)}, u32[]{:S(2)}) %collective-permute-start.2) | collective-permute-done | bytes 16416 | tf_op jit(solution)/shard_map/ppermute | solution.py:461
  11.2 0.0 copy-start.4
  11.2 1.7 %collective-permute-done.1.p1 = f32[8,512]{1,0:T(8,128)S(1)} collective-permute-done((f32[8,512]{1,0:T(8,128)}, f32[8,512]{1,0:T(8,128)S(1)}, u32[]{:S(2)}, u32[]{:S(2)}) %collective-permute-start.1) | collective-permute-done | bytes 16416 | tf_op jit(solution)/shard_map/ppermute | solution.py:461
  12.9 0.0 copy-start.5
  12.9 0.0 copy-done.2
  12.9 0.0 copy-done.3
  12.9 0.0 copy-done.4
  12.9 0.6 copy-done.5
  13.5 14.2 %local_state.1 = (bf16[512,2048]{1,0:T(8,128)(2,1)}, bf16[512,128]{1,0:T(8,128)(2,1)}, f32[512,32]{1,0:T(8,128)}, f32[512,32]{1,0:T(8,128)}, f32[8,2048]{1,0:T(8,128)}, /*index=5*/bf16[8,16,16,128]{3,2,1,0:T(8,128)(2,1)}) custom-call(s32[1]{0:T(128)} %bitcast.me_ref, bf16[512,1024]{1,0:T(8,128)(2,1)} %tok_ref.7, bf16[8,1024]{1,0:T(8,128)(2,1)} %copy-done.2, ...), custom_call_target="tpu_custom_call" | custom-call | tf_op jit(solution)/shard_map/local_state/pallas_call | solution.py:200
  27.7 11.0 %all-to-all-start = ((bf16[128,16,128]{2,1,0:T(8,128)(2,1)}), bf16[128,16,128]{2,1,0:T(8,128)(2,1)S(1)}, u32[]{:S(2)}, u32[]{:S(2)}) async-start(bf16[128,16,128]{2,1,0:T(8,128)(2,1)} %bitcast.11), calls=%async_computation | async-start | bytes 1048576 | tf_op jit(solution)/shard_map/all_to_all | solution.py:467
  38.7 10.8 %intra.2 = (f32[512,1024]{1,0:T(8,128)}, bf16[512,1024]{1,0:T(8,128)(2,1)}) custom-call(bf16[512,2048]{1,0:T(8,128)(2,1)} %get-tuple-element.31.xc_ref, bf16[512,1024]{1,0:T(8,128)(2,1)} %tok_ref.7, bf16[1024,4096]{1,0:T(8,128)(2,1)} %w_ref.8, bf16[512,128]{1,0:T(8,128)(2,1)} %get-tuple-element.22.bc_ref.c_ref, f32[512,32]{1,0:T(8,128)} %get-tuple-element.25.dt_ref, ...), custom_call_target="tpu_custom_call" | custom-call | tf_op jit(solution)/shard_map/intra/pallas_call | solution.py:323
  49.5 3.2 %all-to-all-done.in_ref = bf16[128,16,128]{2,1,0:T(8,128)(2,1)S(1)} async-done(((bf16[128,16,128]{2,1,0:T(8,128)(2,1)}), bf16[128,16,128]{2,1,0:T(8,128)(2,1)S(1)}, u32[]{:S(2)}, u32[]{:S(2)}) %all-to-all-start) | async-done | bytes 524320 | tf_op jit(solution)/shard_map/all_to_all | solution.py:467
  52.7 0.0 copy-start
  52.7 0.8 copy-done
  53.5 2.0 %scan_devices.1 = bf16[128,8,128]{2,1,0:T(8,128)(2,1)} custom-call(bf16[128,16,128]{2,1,0:T(8,128)(2,1)} %copy-done), custom_call_target="tpu_custom_call" | custom-call | tf_op jit(solution)/shard_map/scan_devices/pallas_call | solution.py:365
  55.5 6.6 %all-to-all-start.1 = ((bf16[128,8,128]{2,1,0:T(8,128)(2,1)}), bf16[128,8,128]{2,1,0:T(8,128)(2,1)S(1)}, u32[]{:S(2)}, u32[]{:S(2)}) async-start(bf16[128,8,128]{2,1,0:T(8,128)(2,1)} %scan_devices.1), calls=%async_computation.1 | async-start | bytes 524288 | tf_op jit(solution)/shard_map/all_to_all | solution.py:472
  62.1 10.8 %intra.3 = (f32[512,1024]{1,0:T(8,128)}, bf16[512,1024]{1,0:T(8,128)(2,1)}) custom-call(bf16[512,2048]{1,0:T(8,128)(2,1)} %get-tuple-element.31.xc_ref, bf16[512,1024]{1,0:T(8,128)(2,1)} %tok_ref.7, bf16[1024,4096]{1,0:T(8,128)(2,1)} %w_ref.8, bf16[512,128]{1,0:T(8,128)(2,1)} %get-tuple-element.22.bc_ref.c_ref, f32[512,32]{1,0:T(8,128)} %get-tuple-element.25.dt_ref, ...), custom_call_target="tpu_custom_call" | custom-call | tf_op jit(solution)/shard_map/intra/pallas_call | solution.py:323
  72.9 0.6 all-to-all-done.1
  73.4 0.0 copy-start.1
  73.4 0.7 copy-done.1
  74.1 9.0 %finish.1 = bf16[512,1024]{1,0:T(8,128)(2,1)} custom-call(bf16[512,128]{1,0:T(8,128)(2,1)} %get-tuple-element.22.bc_ref.c_ref, bf16[8,16,8,128]{3,2,1,0:T(8,128)(2,1)} %bitcast.10, f32[512,1024]{1,0:T(8,128)} %get-tuple-element.30.own0, f32[512,1024]{1,0:T(8,128)} %get-tuple-element.32.own1, bf16[512,1024]{1,0:T(8,128)(2,1)} %get-tuple-element.33.scale0, ...), custom_call_target="tpu_custom_call" | custom-call | tf_op jit(solution)/shard_map/finish/pallas_call | solution.py:428
Async XLA Ops:
  1.4 8.5 %collective-permute-start = (bf16[8,1024]{1,0:T(8,128)(2,1)}, bf16[8,1024]{1,0:T(8,128)(2,1)S(1)}, u32[]{:S(2)}, u32[]{:S(2)}) collective-permute-start(bf16[8,1024]{1,0:T(8,128)(2,1)} %get-tuple-element.20), channel_id=1, source_target_pairs={{0,1},{1,2},{2,3},{3,4},{4,5},{5,6},{6,7},{7,8},{8,9},{9,10},{10,1... | collective-permute-start | bytes 49160 | tf_op jit(solution)/shard_map/ppermute | solution.py:457
  5.4 4.6 %collective-permute-start.3 = (f32[8,512]{1,0:T(8,128)}, f32[8,512]{1,0:T(8,128)S(1)}, u32[]{:S(2)}, u32[]{:S(2)}) collective-permute-start(f32[8,512]{1,0:T(8,128)} %get-tuple-element.21.p0), channel_id=1, source_target_pairs={{0,1},{1,2},{2,3},{3,0},{4,5},{5,6},{6,7},{7,4},{8,9},{9,10},{10,1... | collective-permute-start | bytes 49160 | tf_op jit(solution)/shard_map/ppermute | solution.py:461
  6.6 4.5 %collective-permute-start.2 = (f32[8,512]{1,0:T(8,128)}, f32[8,512]{1,0:T(8,128)S(1)}, u32[]{:S(2)}, u32[]{:S(2)}) collective-permute-start(f32[8,512]{1,0:T(8,128)} %get-tuple-element.21.p0), channel_id=1, source_target_pairs={{0,2},{1,3},{2,0},{3,1},{4,6},{5,7},{6,4},{7,5},{8,10},{9,11},{10,... | collective-permute-start | bytes 49160 | tf_op jit(solution)/shard_map/ppermute | solution.py:461
  9.7 3.3 %collective-permute-start.1 = (f32[8,512]{1,0:T(8,128)}, f32[8,512]{1,0:T(8,128)S(1)}, u32[]{:S(2)}, u32[]{:S(2)}) collective-permute-start(f32[8,512]{1,0:T(8,128)} %get-tuple-element.21.p0), channel_id=1, source_target_pairs={{0,3},{1,0},{2,1},{3,2},{4,7},{5,4},{6,5},{7,6},{8,11},{9,8},{10,9... | collective-permute-start | bytes 49160 | tf_op jit(solution)/shard_map/ppermute | solution.py:461
  10.0 3.0 %copy-start.2 = (bf16[8,1024]{1,0:T(8,128)(2,1)}, bf16[8,1024]{1,0:T(8,128)(2,1)S(1)}, u32[]{:S(2)}) copy-start(bf16[8,1024]{1,0:T(8,128)(2,1)S(1)} %collective-permute-done.halo_ref) | copy-start | bytes 49156
  10.0 3.0 %copy-start.3 = (f32[8,512]{1,0:T(8,128)}, f32[8,512]{1,0:T(8,128)S(1)}, u32[]{:S(2)}) copy-start(f32[8,512]{1,0:T(8,128)S(1)} %collective-permute-done.3.p3) | copy-start | bytes 49156
  11.2 1.8 %copy-start.4 = (f32[8,512]{1,0:T(8,128)}, f32[8,512]{1,0:T(8,128)S(1)}, u32[]{:S(2)}) copy-start(f32[8,512]{1,0:T(8,128)S(1)} %collective-permute-done.2.p2) | copy-start | bytes 49156
  12.9 0.6 copy-start.5
  27.7 25.0 %all-to-all-start = ((bf16[128,16,128]{2,1,0:T(8,128)(2,1)}), bf16[128,16,128]{2,1,0:T(8,128)(2,1)S(1)}, u32[]{:S(2)}, u32[]{:S(2)}) async-start(bf16[128,16,128]{2,1,0:T(8,128)(2,1)} %bitcast.11), calls=%async_computation | async-start | bytes 1048576 | tf_op jit(solution)/shard_map/all_to_all | solution.py:467
  52.7 0.8 copy-start
  55.5 17.9 %all-to-all-start.1 = ((bf16[128,8,128]{2,1,0:T(8,128)(2,1)}), bf16[128,8,128]{2,1,0:T(8,128)(2,1)S(1)}, u32[]{:S(2)}, u32[]{:S(2)}) async-start(bf16[128,8,128]{2,1,0:T(8,128)(2,1)} %scan_devices.1), calls=%async_computation.1 | async-start | bytes 524288 | tf_op jit(solution)/shard_map/all_to_all | solution.py:472
  73.4 0.7 copy-start.1

commit v3 on v0

v3 whole, which is shorter than its diff:
```python
import functools

import jax
import jax.numpy as jnp
from jax import lax
from jax.experimental import pallas as pl
from jax.experimental.pallas import tpu as pltpu
from jax.sharding import Mesh
from jax.sharding import PartitionSpec as P

HEADS = 32
HEAD_DIM = 64
STATE = 64
CONV = 4
DINNER = HEADS * HEAD_DIM
BC = 2 * STATE
SUB = 128
PAD = 16
EPSILON = 1e-05
FAR = "chips"
NEAR = ("row", "core", "head")
BOTH = (FAR, *NEAR)
WIDTH = 256
OWNED = 128
TOGETHER = 1
SPLIT = (2, 4, 2)
F32 = jnp.float32
BF16 = jnp.bfloat16
OWN = jnp.float32
LIMIT = 60 * 1024 * 1024
LOG2E = 1.4426950408889634
FAR_AWAY = pl.BlockSpec(memory_space=pltpu.HBM)


def params(steps=1):
    return pltpu.CompilerParams(
        dimension_semantics=("arbitrary",) * steps, vmem_limit_bytes=LIMIT
    )


def silu(v):
    half = 0.5 * v
    return half + half * jnp.tanh(half)


def hi_lo(v, axis):
    hi = v.astype(BF16)
    lo = (v - hi.astype(F32)).astype(BF16)
    return jnp.concatenate([hi, lo], axis=axis)


def dot(a, b):
    return jnp.dot(a, b, preferred_element_type=F32)


def split3(v):
    hi = v.astype(BF16)
    rest = v - hi.astype(F32)
    mid = rest.astype(BF16)
    return [hi, mid, (rest - mid.astype(F32)).astype(BF16)]


def call(kernel, args, outs, scratch, name, far=(), far_out=(), scalars=()):
    specs = [pl.BlockSpec(memory_space=pltpu.SMEM)] * len(scalars)
    specs += [FAR_AWAY if i in far else pl.BlockSpec() for i in range(len(args))]
    return pl.pallas_call(
        kernel,
        in_specs=specs,
        out_specs=[FAR_AWAY if i in far_out else pl.BlockSpec() for i in range(len(outs))],
        out_shape=[jax.ShapeDtypeStruct(shape, dtype) for shape, dtype in outs],
        scratch_shapes=scratch,
        compiler_params=params(0),
        name=name,
    )(*scalars, *args)


def start(source, target, sem):
    copy = pltpu.make_async_copy(source, target, sem)
    copy.start()
    return copy


def on_chip(array):
    return pltpu.with_memory_space_constraint(array, pltpu.VMEM)


def place(r):
    return r // 8 + SUB // 8 * (r % 8)


def reorder(back=False):
    r = lax.broadcasted_iota(jnp.int32, (SUB, SUB), 1 if back else 0)
    c = lax.broadcasted_iota(jnp.int32, (SUB, SUB), 0 if back else 1)
    return (place(r) == c).astype(F32).astype(BF16)


def one_hot(first_channel, width):
    row = lax.broadcasted_iota(jnp.int32, (2 * HEADS, width), 0)
    chan = lax.broadcasted_iota(jnp.int32, (2 * HEADS, width), 1) + first_channel
    return ((row % HEADS) == (chan // HEAD_DIM)).astype(F32).astype(BF16)


def pack_kernel(w_ref, b_ref, dt_ref, a_ref, skip_ref, tok_ref, out_ref, tail_ref):
    out_ref[...] = jnp.zeros_like(out_ref)
    here = dt_ref.shape[1]
    for k in range(out_ref.shape[0]):
        out_ref[k, 0:CONV] = w_ref[...]
        out_ref[k, CONV : CONV + 1] = b_ref[...]
        for row, ref in ((5, dt_ref), (6, a_ref), (7, skip_ref)):
            out_ref[k, row : row + 1, 0:here] = ref[...]
    tail_ref[...] = tok_ref[...]


def pack(weight, bias, dt_bias, a_log, skip_d, tokens, copies):
    rows, depth = tokens.shape
    small = (weight, bias[None], dt_bias[None], a_log[None], skip_d[None])

    def whole(a):
        return pl.BlockSpec(a.shape, lambda g: (0, 0))

    return pl.pallas_call(
        pack_kernel,
        grid=(1,),
        in_specs=[whole(a) for a in small]
        + [pl.BlockSpec((8, depth), lambda g: (rows // 8 - 1, 0))],
        out_specs=[
            pl.BlockSpec((copies, 8, weight.shape[1]), lambda g: (0, 0, 0)),
            pl.BlockSpec((8, depth), lambda g: (0, 0)),
        ],
        out_shape=[
            jax.ShapeDtypeStruct((copies, 8, weight.shape[1]), F32),
            jax.ShapeDtypeStruct((8, depth), BF16),
        ],
        compiler_params=params(),
        name="pack",
    )(*small, tokens)


def half_lanes(w, which):
    parts = []
    for k in range(w.shape[1] // 128):
        at = k * 128 + which * HEAD_DIM
        parts.append(w[:, at : at + HEAD_DIM])
    return jnp.concatenate(parts, axis=1)


def convolve(x, weights, bias):
    first = lax.broadcasted_iota(jnp.int32, (8, 1), 0) == 0
    results = []
    for k in range((x.shape[0] - PAD) // SUB):
        at = PAD + k * SUB
        rows = x[at : at + SUB]
        edge = []
        for m in range(1, CONV):
            own = x[at + SUB - 8 * m : at + SUB - 8 * m + 8]
            last = PAD - m if k == 0 else at - 8 * m + 7
            edge.insert(0, jnp.where(first, x[last : last + 1], pltpu.roll(own, 1, 0)))
        summed = bias + weights[CONV - 1 : CONV] * rows
        for m in range(1, CONV):
            moved = jnp.concatenate(edge[CONV - 1 - m :] + [rows[: SUB - 8 * m]], axis=0)
            summed = summed + weights[CONV - 1 - m : CONV - m] * moved
        results.append(silu(summed))
    return results


def state_kernel(
    tok_hbm, halo_ref, w_hbm, wsmall_hbm, par, wbc_ref, bbc_ref,
    xc_hbm, z_hbm, bc_hbm, dt_hbm, cum_hbm, skip_hbm, slab_ref,
    raw, tok, w_ref, wsmall, xc_ref, z_ref, bc_ref, dt_ref, cum_ref, skip_ref,
    wgt, bt, in_sem, out_sem,
):
    rows = tok_hbm.shape[0]
    groups = DINNER // WIDTH
    half = DINNER
    fetch_tok = start(tok_hbm, raw, in_sem.at[0])
    fetch_small = start(wsmall_hbm, wsmall, in_sem.at[1])
    fetch_w = [
        start(w_hbm.at[:, i * half : (i + 1) * half], w_ref.at[i], in_sem.at[2 + i])
        for i in range(2)
    ]
    tok[0 : PAD - 8] = jnp.zeros((PAD - 8, tok.shape[1]), BF16)
    tok[PAD - 8 : PAD] = halo_ref[...]
    fetch_tok.wait()
    order = reorder()
    for k in range(rows // SUB):
        here = slice(k * SUB, (k + 1) * SUB)
        tok[PAD + k * SUB : PAD + (k + 1) * SUB] = dot(order, raw[here]).astype(BF16)
    fetch_small.wait()
    begin(tok, wsmall, par, wbc_ref, bbc_ref, bc_ref, dt_ref, cum_ref, wgt, bt)
    sends = [
        start(bc_ref, bc_hbm, out_sem.at[0]),
        start(dt_ref, dt_hbm, out_sem.at[1]),
        start(cum_ref, cum_hbm, out_sem.at[2]),
    ]

    def project(g):
        at = 2 * g * WIDTH % half
        both = dot(tok[...], w_ref[2 * g * WIDTH // half, :, at : at + 2 * WIDTH])
        both = both.astype(BF16)
        z_ref[:, g * WIDTH : (g + 1) * WIDTH] = half_lanes(both[PAD:], 0)
        return half_lanes(both, 1).astype(F32)

    wide = par.shape[2]
    for part in range(2):
        fetch_w[part].wait()
        mine_groups = range(part * groups // 2, (part + 1) * groups // 2)
        ahead = project(mine_groups[0])
        for g in mine_groups:
            x = ahead
            if g + 1 in mine_groups:
                ahead = project(g + 1)
            cols = slice(g * WIDTH, (g + 1) * WIDTH)
            spread = dot(wgt[...], one_hot(g * WIDTH, WIDTH))
            at = g * WIDTH % wide
            mine = par[g * WIDTH // wide, :, at : at + WIDTH]
            blocks = convolve(x, mine[0:CONV], mine[CONV : CONV + 1])
            xc = jnp.concatenate([block.astype(BF16) for block in blocks], axis=0)
            xc_ref[:, cols] = xc
            weighted = (xc.astype(F32) * spread[:rows]).astype(BF16)
            state = dot(bt[...], weighted)
            extra = spread[rows : rows + 8]
            skip_ref[:, cols] = extra
            for i in range(WIDTH // OWNED):
                own = slice(i * OWNED, (i + 1) * OWNED)
                owner = g * WIDTH // OWNED + i
                slab_ref[owner, 0:STATE] = state[:, own].astype(BF16)
                slab_ref[owner, STATE : STATE + 8] = extra[:, own].astype(BF16)
        cols = slice(part * DINNER // 2, (part + 1) * DINNER // 2)
        for k, (ref, hbm) in enumerate(((xc_ref, xc_hbm), (z_ref, z_hbm))):
            sends.append(
                start(ref.at[:, cols], hbm.at[:, cols], out_sem.at[3 + 2 * part + k])
            )
    sends.append(start(skip_ref, skip_hbm, out_sem.at[7]))
    for copy in sends:
        copy.wait()


def begin(tok, wsmall_ref, par, wbc_ref, bbc_ref, bc_ref, dt_ref, cum_ref, wgt, bt):
    rows = dt_ref.shape[0]
    blocks = par.shape[0]
    each = HEADS // blocks
    lane = lax.broadcasted_iota(jnp.int32, (8, 128), 1)
    heads = jnp.zeros((8, 128), F32)
    for k in range(blocks):
        block = par[k, :, 0:128]
        moved = block if k == 0 else pltpu.roll(block, each * k, 1)
        heads = jnp.where(lane // each == k, moved, heads)
    heads = heads[:, :HEADS]
    small = lax.dot_general(
        tok[...], wsmall_ref[...], (((1,), (1,)), ((), ())),
        preferred_element_type=F32,
    )
    small = small.astype(BF16).astype(F32)
    raw = small[PAD:, BC:] + heads[5:6]
    step = jnp.maximum(raw, 0.0) + jnp.log1p(jnp.exp(-jnp.abs(raw)))
    decay = step * -jnp.exp(heads[6:7])
    r = lax.broadcasted_iota(jnp.int32, (SUB, SUB), 0)
    c = lax.broadcasted_iota(jnp.int32, (SUB, SUB), 1)
    ones = (place(r) >= place(c)).astype(F32).astype(BF16)
    before = jnp.zeros((1, HEADS), F32)
    parts = []
    for k in range(rows // SUB):
        three = jnp.concatenate(split3(decay[k * SUB : (k + 1) * SUB]), axis=1)
        sums = dot(ones, three)
        part = before + (
            sums[:, :HEADS] + sums[:, HEADS : 2 * HEADS] + sums[:, 2 * HEADS :]
        )
        before = part[SUB - 1 : SUB]
        parts.append(part)
    cum = jnp.concatenate(parts, axis=0)
    dt_ref[...] = step
    cum_ref[...] = cum
    wgt[0:rows] = hi_lo(step * jnp.exp(before - cum), 1)
    total = hi_lo(jnp.exp(before), 1)
    zero = jnp.zeros((1, HEADS), BF16)
    wgt[rows : rows + 8] = jnp.concatenate(
        [
            jnp.concatenate([total[:, :HEADS], zero], axis=1),
            jnp.concatenate([zero, total[:, HEADS:]], axis=1),
            hi_lo(heads[7:8], 1),
            jnp.zeros((5, 2 * HEADS), BF16),
        ],
        axis=0,
    )
    conved = jnp.concatenate(
        convolve(small[:, :BC], wbc_ref[...], bbc_ref[...]), axis=0
    )
    bc_ref[...] = conved.astype(BF16)
    bt[...] = conved.T[:STATE].astype(BF16)


def local_state(tokens, halo, w_gate_x, w_small, packed, conv_w, conv_b):
    rows, depth = tokens.shape
    outs = [
        ((rows, DINNER), BF16),
        ((rows, DINNER), BF16),
        ((rows, BC), BF16),
        ((rows, HEADS), F32),
        ((rows, HEADS), F32),
        ((8, DINNER), F32),
    ]
    return call(
        state_kernel,
        [tokens, on_chip(halo), w_gate_x, w_small, on_chip(packed), conv_w, conv_b],
        outs + [((DINNER // OWNED, STATE + 8, OWNED), BF16)],
        [
            pltpu.VMEM((rows, depth), BF16),
            pltpu.VMEM((PAD + rows, depth), BF16),
            pltpu.VMEM((2, depth, DINNER), BF16),
            pltpu.VMEM(w_small.shape, BF16),
            *(pltpu.VMEM(shape, dtype) for shape, dtype in outs),
            pltpu.VMEM((rows + 8, 2 * HEADS), BF16),
            pltpu.VMEM((STATE, rows), BF16),
            pltpu.SemaphoreType.DMA((4,)),
            pltpu.SemaphoreType.DMA((8,)),
        ],
        "local_state",
        far=(0, 2, 3),
        far_out=range(6),
    )


def prepare(bc_ref, dt_ref, cum_ref, scores, left, rowlog, bt, wgt):
    rows = bc_ref.shape[0]
    heads = WIDTH // HEAD_DIM
    bt[...] = bc_ref[...].astype(F32).T[:STATE].astype(BF16)
    for k in range(rows // SUB):
        here = slice(k * SUB, (k + 1) * SUB)
        scores[here] = dot(bc_ref[here, STATE:], bt[:, here])
    cum = cum_ref[...]
    step = dt_ref[...]
    ones = jnp.ones((rows, HEADS), BF16)
    left[...] = jnp.concatenate(split3(cum * LOG2E) + [ones], axis=1)
    by_row = (jnp.log(jnp.maximum(step, 1e-37)) - cum) * LOG2E
    by_row = jnp.concatenate([p.astype(F32) for p in split3(by_row)] + [cum], axis=1).T
    for g in range(HEADS // heads):
        for p in range(3):
            first = p * HEADS + g * heads
            rowlog[g, p, 0:heads] = by_row[first : first + heads]
    starts, ends = [], []
    before = jnp.zeros((1, HEADS), F32)
    for k in range(rows // SUB):
        starts.append(jnp.broadcast_to(before, (SUB, HEADS)))
        before = cum[(k + 1) * SUB - 1 : (k + 1) * SUB]
        ends.append(jnp.broadcast_to(before, (SUB, HEADS)))
    starts = jnp.concatenate(starts, axis=0)
    ends = jnp.concatenate(ends, axis=0)
    wgt[0:rows] = hi_lo(step * jnp.exp(ends - cum), 1)
    wgt[rows : 2 * rows] = hi_lo(jnp.exp(cum - starts), 1)
    wgt[2 * rows : 3 * rows] = hi_lo(jnp.exp(cum), 1)


def intra_kernel(
    first_group, xc_ref, z_ref, bc_ref, dt_ref, cum_ref, skip_ref,
    own_ref, scale_ref, scores, left, rowlog, bt, wgt,
):
    rows = xc_ref.shape[0]
    blocks = rows // SUB
    heads = WIDTH // HEAD_DIM
    together = xc_ref.shape[1] // WIDTH

    @pl.when(pl.program_id(0) == 0)
    def _():
        prepare(bc_ref, dt_ref, cum_ref, scores, left, rowlog, bt, wgt)

    r = lax.broadcasted_iota(jnp.int32, (SUB, heads * SUB), 0)
    c = lax.broadcasted_iota(jnp.int32, (SUB, heads * SUB), 1)
    causal = place(r) >= place(c % SUB)
    low = lax.broadcasted_iota(jnp.int32, (1, 128), 1) < HEAD_DIM
    pr = lax.broadcasted_iota(jnp.int32, (3 * HEADS, heads * SUB), 0)
    pc = lax.broadcasted_iota(jnp.int32, (3 * HEADS, heads * SUB), 1)
    for i in range(together):
        g = first_group + pl.program_id(0) * together + i
        mine = slice(i * WIDTH, (i + 1) * WIDTH)
        spread = one_hot(g * WIDTH, WIDTH)
        pick = (pr % HEADS == g * heads + pc // SUB).astype(F32).astype(BF16)
        skip = skip_ref[2:3, mine]
        state = jnp.zeros((STATE, WIDTH), F32)
        for k in range(blocks):
            here = slice(k * SUB, (k + 1) * SUB)
            xc = xc_ref[here, mine]
            late = jnp.concatenate(
                [
                    jnp.concatenate(
                        [rowlog[g, p, h : h + 1, here] for h in range(heads)], axis=1
                    )
                    for p in range(3)
                ]
                + [jnp.zeros((HEADS - 3, heads * SUB), F32)],
                axis=0,
            ).astype(BF16)
            gaps = dot(left[here], jnp.concatenate([pick, late], axis=0))
            decay = jnp.exp2(jnp.where(causal, gaps, -jnp.inf))
            score = scores[here]
            pieces = []
            for pair in range(heads // 2):
                both = [
                    (score * decay[:, h * SUB : (h + 1) * SUB]).astype(BF16)
                    for h in (2 * pair, 2 * pair + 1)
                ]
                x = xc[:, pair * 128 : pair * 128 + 128]
                none = jnp.zeros_like(x)
                right = jnp.concatenate(
                    [jnp.where(low, x, none), jnp.where(low, none, x)], axis=0
                )
                pieces.append(dot(jnp.concatenate(both, axis=1), right))
            y = jnp.concatenate(pieces, axis=1)
            xf = xc.astype(F32)
            grow = dot(wgt[rows + k * SUB : rows + (k + 1) * SUB], spread)
            if k > 0:
                y = y + grow * dot(bc_ref[here, STATE:], state.astype(BF16))
            if k + 1 < blocks:
                shrink = dot(wgt[here], spread)
                fresh = dot(bt[:, here], (xf * shrink).astype(BF16))
                state = state * grow[SUB - 1 : SUB] + fresh
            gate = silu(z_ref[here, mine].astype(F32))
            own_ref[here, mine] = ((y + skip * xf) * gate).astype(own_ref.dtype)
            full = dot(wgt[2 * rows + k * SUB : 2 * rows + (k + 1) * SUB], spread)
            scale_ref[here, mine] = (full * gate).astype(BF16)


def intra(first_group, groups, xc, z, bc, dt, cum, skips):
    rows = xc.shape[0]
    together = TOGETHER
    group = first_group // together
    wide = together * WIDTH

    def whole(a):
        return pl.BlockSpec(a.shape, lambda i: (0,) * a.ndim)

    return pl.pallas_call(
        functools.partial(intra_kernel, first_group),
        grid=(groups // together,),
        in_specs=[
            pl.BlockSpec((rows, wide), lambda i: (0, i + group)),
            pl.BlockSpec((rows, wide), lambda i: (0, i + group)),
            whole(bc),
            whole(dt),
            whole(cum),
            pl.BlockSpec((8, wide), lambda i: (0, i + group)),
        ],
        out_specs=[
            pl.BlockSpec((rows, wide), lambda i: (0, i)),
            pl.BlockSpec((rows, wide), lambda i: (0, i)),
        ],
        out_shape=[
            jax.ShapeDtypeStruct((rows, groups * WIDTH), OWN),
            jax.ShapeDtypeStruct((rows, groups * WIDTH), BF16),
        ],
        scratch_shapes=[
            pltpu.VMEM((rows, SUB), F32),
            pltpu.VMEM((rows, 4 * HEADS), BF16),
            pltpu.VMEM((DINNER // WIDTH, 3, 8, rows), F32),
            pltpu.VMEM((STATE, rows), BF16),
            pltpu.VMEM((3 * rows, 2 * HEADS), BF16),
        ],
        compiler_params=params(),
        name="intra",
    )(xc, z, bc, dt, cum, skips)


def through(state, slab):
    slab = slab.astype(F32)
    total = slab[STATE : STATE + 1] + slab[STATE + 1 : STATE + 2]
    return state * total + slab[0:STATE], total


def fold_kernel(in_ref, out_ref):
    state = jnp.zeros((STATE, OWNED), F32)
    whole = jnp.ones((1, OWNED), F32)
    for q in range(in_ref.shape[0]):
        state, total = through(state, in_ref[q])
        whole = whole * total
    hi = whole.astype(BF16).astype(F32)
    row = lax.broadcasted_iota(jnp.int32, (8, OWNED), 0)
    tail = jnp.where(row == 0, hi, jnp.where(row == 1, whole - hi, 0.0))
    state = state.astype(BF16)
    tail = tail.astype(BF16)
    for b in range(out_ref.shape[0]):
        out_ref[b, 0:STATE] = state
        out_ref[b, STATE:] = tail


def fold(near, blocks):
    out = ((blocks, *near.shape[1:]), BF16)
    return call(fold_kernel, [on_chip(near)], [out], [], "fold")[0]


def unfold_kernel(me_ref, near_ref, far_ref, out_ref):
    def earlier(b, state):
        return through(state, far_ref[b])[0]

    state = jnp.zeros((STATE, OWNED), F32)
    state = lax.fori_loop(0, me_ref[0], earlier, state)
    for q in range(near_ref.shape[0]):
        out_ref[q] = state.astype(BF16)
        state, _ = through(state, near_ref[q])


def unfold(me, near, far):
    count = near.shape[0]
    out = ((count, STATE, OWNED), BF16)
    operands = [on_chip(near), on_chip(far)]
    return call(unfold_kernel, operands, [out], [], "unfold", scalars=(me,))[0]


def finish_kernel(parts, c_ref, in_ref, gain_ref, w_hbm, *refs):
    own_hbm, scale_hbm = refs[:parts], refs[parts : 2 * parts]
    out_ref, w_ref, own_all, scale_all, acc, in_sem, w_sem = refs[2 * parts :]
    rows = c_ref.shape[0]
    halves = 2
    span = DINNER // halves
    fetches = []
    fetch_w = []
    for k in range(halves):
        fetches.append([])
        at = 0
        for p in range(parts):
            low, high = max(at, k * span), min(at + own_hbm[p].shape[1], (k + 1) * span)
            if low < high:
                there, here = slice(low - at, high - at), slice(low, high)
                for i, (hbm, ref) in enumerate(
                    ((own_hbm[p], own_all), (scale_hbm[p], scale_all))
                ):
                    source, target = hbm.at[:, there], ref.at[:, here]
                    fetches[k].append(start(source, target, in_sem.at[k, p, i]))
            at += own_hbm[p].shape[1]
        part = slice(k * span, (k + 1) * span)
        fetch_w.append(start(w_hbm.at[part], w_ref.at[part], w_sem.at[k]))
    total = jnp.zeros((rows, 128), F32)

    def gate(k, total):
        sides = []
        for g in range(k * span // WIDTH, (k + 1) * span // WIDTH):
            cols = slice(g * WIDTH, (g + 1) * WIDTH)
            slabs = [in_ref[2 * g], in_ref[2 * g + 1]]
            carried = dot(c_ref[:, STATE:], jnp.concatenate(slabs, axis=1))
            gated = own_all[:, cols] + scale_all[:, cols].astype(F32) * carried
            gated = gated.astype(BF16).astype(F32)
            square = gated * gated
            total = total + square[:, :128] + square[:, 128:]
            sides.append((gated * gain_ref[:, cols]).astype(BF16))
        return jnp.concatenate(sides, axis=1), total

    for copy in fetches[0]:
        copy.wait()
    left, total = gate(0, total)
    for copy in fetches[1] + fetch_w[:1]:
        copy.wait()
    acc[...] = dot(left, w_ref[:span])
    right, total = gate(1, total)
    fetch_w[1].wait()
    mean = jnp.sum(total, axis=1, keepdims=True) * (1.0 / DINNER)
    product = (acc[...] + dot(right, w_ref[span:])) * lax.rsqrt(mean + EPSILON)
    product = product.astype(BF16)
    order = reorder(back=True)
    for k in range(rows // SUB):
        here = slice(k * SUB, (k + 1) * SUB)
        out_ref[here] = dot(order, product[here]).astype(BF16)


def finish(bc, incoming, owns, scales, norm_gain, w_out):
    rows = bc.shape[0]
    columns = w_out.shape[1]
    parts = len(owns)
    return call(
        functools.partial(finish_kernel, parts),
        [bc, on_chip(incoming), norm_gain, w_out, *owns, *scales],
        [((rows, columns), BF16)],
        [
            pltpu.VMEM(w_out.shape, BF16),
            pltpu.VMEM((rows, DINNER), F32),
            pltpu.VMEM((rows, DINNER), BF16),
            pltpu.VMEM((rows, columns), F32),
            pltpu.SemaphoreType.DMA((2, parts, 2)),
            pltpu.SemaphoreType.DMA((2,)),
        ],
        "finish",
        far=range(3, 4 + 2 * parts),
    )[0]


def on_device(
    tokens, w_gate_x, w_bc_dt, conv_x_weight, conv_x_bias, conv_bc_weight,
    conv_bc_bias, dt_bias, a_log, skip_d, norm_gain, w_out,
):
    n = lax.axis_size("head")
    blocks = lax.axis_size(FAR)
    devices = blocks * lax.axis_size(NEAR)
    my_block = lax.axis_index(FAR)[None]
    packed, tail = pack(conv_x_weight, conv_x_bias, dt_bias, a_log, skip_d, tokens, n)
    packed = lax.all_to_all(packed, "head", 0, 0, tiled=True)
    halo = lax.ppermute(tail, BOTH, [(i, i + 1) for i in range(devices - 1)])
    xc, z, bc, dt, cum, skips, slabs = local_state(
        tokens, halo, w_gate_x, w_bc_dt.T, packed, conv_bc_weight, conv_bc_bias[None]
    )
    near = lax.all_to_all(slabs, NEAR, 0, 0, tiled=True)
    rest = (bc, dt, cum, skips)
    first, second, third = SPLIT
    own0, scale0 = intra(0, first, xc, z, *rest)
    near, own0 = lax.optimization_barrier((near, own0))
    copies = fold(near, blocks)
    far = lax.all_to_all(copies, FAR, 0, 0, tiled=True)
    z, copies = lax.optimization_barrier((z, copies))
    own1, scale1 = intra(first, second, xc, z, *rest)
    far, own1 = lax.optimization_barrier((far, own1))
    incoming = unfold(my_block, near, far)
    back = lax.all_to_all(incoming, NEAR, 0, 0, tiled=True)
    z, incoming = lax.optimization_barrier((z, incoming))
    own2, scale2 = intra(first + second, third, xc, z, *rest)
    owns, scales = (own0, own1, own2), (scale0, scale1, scale2)
    return finish(bc, back, owns, scales, norm_gain[None], w_out)


def solution(mesh):
    seq, head = mesh.devices.shape
    split = Mesh(mesh.devices.reshape(seq // 4, 2, 2, head), BOTH)
    return jax.shard_map(
        on_device,
        mesh=split,
        in_specs=(
            P(BOTH, None),
            P(),
            P(),
            P(None, "head"),
            P("head"),
            P(),
            P(),
            P("head"),
            P("head"),
            P("head"),
            P(),
            P(),
        ),
        out_specs=P(BOTH, None),
        check_vma=False,
    )
```

time: 323 us -> 79 us (0.24)
  blocking collectives: 145 us -> 0 us
  other arithmetic: 59.8 us -> 0 us
  Pallas kernels: 0 us -> 46.1 us
  matrix products: 43.9 us -> 0 us
  local copies, waits for them, and re-layouts: 35.4 us -> 0 us
  between operations: 14.5 us -> 0.19 us
  starting transfers between devices: 17.4 us -> 25.3 us
  waiting for transfers between devices: 2.01 us -> 6.73 us
    unnamed x1 -> x0, blocking collectives: 65.6 us -> none
    all_gather x1 -> x0, blocking collectives: 53.4 us -> none  [on_device(): bc_rows = lax.all_gather(bc_dt[:, :2 * STATE], 'head', axis=0, tiled=True)]
    pallas_call x0 -> x8, Pallas kernels: none -> 46.1 us  [the longest x4 23.6 us: call(): pl.pallas_call(kernel, in_specs=specs, out_specs=[FAR_AWAY if i in far_ou...]
    dot_general x7 -> x0, matrix products: 43.9 us -> none  [the longest x1 22.5 us: on_device(): jnp.einsum('khts,kshp->kthp', mixed, xdt_blocks, precision=highest)]
    select_n x32 -> x0, other arithmetic: 33.7 us -> none  [hop(): return jax.tree.map(lambda a, b: jnp.where(reached, a, b), new, before)]
    all_to_all x1 -> x0, blocking collectives: 26.5 us -> none  [on_device(): lax.all_to_all(gated_out, 'head', split_axis=0, concat_axis=1, tiled=True)]
    unnamed x42 -> x0, local copies, waits for them, and re-layouts: 13.7 us -> none
    all_to_all x2 -> x4, starting transfers between devices: 9.84 us -> 21.9 us  [the longest x1 7.37 us: on_device(): far = lax.all_to_all(copies, FAR, 0, 0, tiled=True)]
  transfers between devices with their start and end apart: 4 -> 5, of which waited for: 1 -> 3; matrix products, arithmetic and copies ran while one was open for 14% -> 0% of each run, Pallas kernels for 0% -> 27%
where the time goes in v3:
time: 79 us; the launch traced here: 78.3 us
  Pallas kernels  46.1 us (58%)
  starting transfers between devices  25.3 us (32%)
  waiting for transfers between devices  6.73 us (9%)
    pallas_call x4, Pallas kernels, call(): pl.pallas_call(kernel, in_specs=specs, out_specs=[FAR_AWAY if i in far_ou...  23.6 us
    pallas_call x3, Pallas kernels, intra(): pl.pallas_call(functools.partial(intra_kernel, first_group), grid=(groups...  21.1 us
    all_to_all x1, starting transfers between devices, on_device(): far = lax.all_to_all(copies, FAR, 0, 0, tiled=True)  7.37 us
    all_to_all x1, starting transfers between devices, on_device(): near = lax.all_to_all(slabs, NEAR, 0, 0, tiled=True)  5.31 us
    all_to_all x1, starting transfers between devices, on_device(): packed = lax.all_to_all(packed, 'head', 0, 0, tiled=True)  4.84 us
    all_to_all x1, starting transfers between devices, on_device(): back = lax.all_to_all(incoming, NEAR, 0, 0, tiled=True)  4.43 us
    ppermute x1, waiting for transfers between devices, on_device(): halo = lax.ppermute(tail, BOTH, [(i, i + 1) for i in range(devices - 1)])  3.95 us
    ppermute x1, starting transfers between devices, on_device(): halo = lax.ppermute(tail, BOTH, [(i, i + 1) for i in range(devices - 1)])  3.36 us
  transfers between devices with their start and end apart: 5, of which 3 were waited for; matrix products, arithmetic and copies ran while one was open for 0% of the time, Pallas kernels for 27%

profile of v3, /device:TPU:1, one launch (start us, length us, event | category | flops | bytes accessed | tf_op | source)
XLA Modules:
  0.0 78.3 jit_solution(2352780910545202071)
XLA Ops:
  0.0 1.4 %pack.1 = (f32[4,8,512]{2,1,0:T(8,128)}, bf16[8,1024]{1,0:T(8,128)(2,1)}) custom-call(f32[4,512]{1,0:T(4,128)} %w_ref.1, f32[1,512]{1,0:T(1,128)} %bitcast.10, f32[1,8]{1,0:T(1,128)} %bitcast.11, f32[1,8]{1,0:T(1,128)} %bitcast.12, f32[1,8]{1,0:T(1,128)} %bitcast.13, bf16[512,1024]{1,0:T(8,128)(2,1)} %tok_hbm.1), custom_call_target="tpu_custom_call" | custom-call | tf_op jit(solution)/shard_map/pack/pallas_call | solution.py:121
  1.4 4.8 %all-to-all-start = ((f32[4,8,512]{2,1,0:T(8,128)}), f32[4,8,512]{2,1,0:T(8,128)S(1)}, u32[]{:S(2)}, u32[]{:S(2)}) async-start(f32[4,8,512]{2,1,0:T(8,128)} %get-tuple-element.27), calls=%async_computation | async-start | bytes 131072 | tf_op jit(solution)/shard_map/all_to_all | solution.py:592
  6.3 3.4 %collective-permute-start = (bf16[8,1024]{1,0:T(8,128)(2,1)}, bf16[8,1024]{1,0:T(8,128)(2,1)S(1)}, u32[]{:S(2)}, u32[]{:S(2)}) collective-permute-start(bf16[8,1024]{1,0:T(8,128)(2,1)} %get-tuple-element.26), channel_id=1, source_target_pairs={{0,1},{1,2},{2,3},{3,4},{4,5},{5,6},{6,7},{7,8},{8,9},{9,10},{10,1... | collective-permute-start | bytes 49160 | tf_op jit(solution)/shard_map/ppermute | solution.py:593
  9.7 4.0 %collective-permute-done.halo_ref = bf16[8,1024]{1,0:T(8,128)(2,1)S(1)} collective-permute-done((bf16[8,1024]{1,0:T(8,128)(2,1)}, bf16[8,1024]{1,0:T(8,128)(2,1)S(1)}, u32[]{:S(2)}, u32[]{:S(2)}) %collective-permute-start) | collective-permute-done | bytes 16416 | tf_op jit(solution)/shard_map/ppermute | solution.py:593
  13.6 0.0 all-to-all-done.par
  13.6 13.4 %local_state.1 = (bf16[512,2048]{1,0:T(8,128)(2,1)}, bf16[512,2048]{1,0:T(8,128)(2,1)}, bf16[512,128]{1,0:T(8,128)(2,1)}, f32[512,32]{1,0:T(8,128)}, f32[512,32]...) custom-call(bf16[512,1024]{1,0:T(8,128)(2,1)} %tok_hbm.1, ...), custom_call_target="tpu_custom_call" | custom-call | tf_op jit(solution)/shard_map/local_state/pallas_call | solution.py:66
  27.0 5.3 %all-to-all-start.1 = ((bf16[16,72,128]{2,1,0:T(8,128)(2,1)}), bf16[16,72,128]{2,1,0:T(8,128)(2,1)S(1)}, u32[]{:S(2)}, u32[]{:S(2)}) async-start(bf16[16,72,128]{2,1,0:T(8,128)(2,1)} %get-tuple-element.29), calls=%async_computation.1 | async-start | bytes 589824 | tf_op jit(solution)/shard_map/all_to_all | solution.py:597
  32.3 6.0 %intra.3 = (f32[512,512]{1,0:T(8,128)}, bf16[512,512]{1,0:T(8,128)(2,1)}) custom-call(bf16[512,2048]{1,0:T(8,128)(2,1)} %get-tuple-element.30.xc_ref, bf16[512,2048]{1,0:T(8,128)(2,1)} %get-tuple-element.42.z_ref, bf16[512,128]{1,0:T(8,128)(2,1)} %get-tuple-element.28.bc_ref.c_ref, f32[512,32]{1,0:T(8,128)} %get-tuple-element.32.dt_ref, ...), custom_call_target="tpu_custom_call" | custom-call | tf_op jit(solution)/shard_map/intra/pallas_call | solution.py:431
  38.3 1.5 %all-to-all-done.1.in_ref.near_ref = bf16[16,72,128]{2,1,0:T(8,128)(2,1)S(1)} async-done(((bf16[16,72,128]{2,1,0:T(8,128)(2,1)}), bf16[16,72,128]{2,1,0:T(8,128)(2,1)S(1)}, u32[]{:S(2)}, u32[]{:S(2)}) %all-to-all-start.1) | async-done | bytes 294944 | tf_op jit(solution)/shard_map/all_to_all | solution.py:597
  39.8 0.7 fold.1
  40.6 7.4 %all-to-all-start.2 = ((bf16[8,72,128]{2,1,0:T(8,128)(2,1)}), bf16[8,72,128]{2,1,0:T(8,128)(2,1)S(1)}, u32[]{:S(2)}, u32[]{:S(2)}) async-start(bf16[8,72,128]{2,1,0:T(8,128)(2,1)} %fold.1), calls=%async_computation.2 | async-start | bytes 294912 | tf_op jit(solution)/shard_map/all_to_all | solution.py:603
  48.0 9.1 %intra.4 = (f32[512,1024]{1,0:T(8,128)}, bf16[512,1024]{1,0:T(8,128)(2,1)}) custom-call(bf16[512,2048]{1,0:T(8,128)(2,1)} %get-tuple-element.30.xc_ref, bf16[512,2048]{1,0:T(8,128)(2,1)} %get-tuple-element.42.z_ref, bf16[512,128]{1,0:T(8,128)(2,1)} %get-tuple-element.28.bc_ref.c_ref, f32[512,32]{1,0:T(8,128)} %get-tuple-element.32.dt_ref, ...), custom_call_target="tpu_custom_call" | custom-call | tf_op jit(solution)/shard_map/intra/pallas_call | solution.py:431
  57.0 0.0 all-to-all-done.2.far_ref
  57.0 0.8 unfold.1
  57.8 4.4 %all-to-all-start.3 = ((bf16[16,64,128]{2,1,0:T(8,128)(2,1)}), bf16[16,64,128]{2,1,0:T(8,128)(2,1)S(1)}, u32[]{:S(2)}, u32[]{:S(2)}) async-start(bf16[16,64,128]{2,1,0:T(8,128)(2,1)} %unfold.1), calls=%async_computation.3 | async-start | bytes 524288 | tf_op jit(solution)/shard_map/all_to_all | solution.py:608
  62.2 6.0 %intra.5 = (f32[512,512]{1,0:T(8,128)}, bf16[512,512]{1,0:T(8,128)(2,1)}) custom-call(bf16[512,2048]{1,0:T(8,128)(2,1)} %get-tuple-element.30.xc_ref, bf16[512,2048]{1,0:T(8,128)(2,1)} %get-tuple-element.42.z_ref, bf16[512,128]{1,0:T(8,128)(2,1)} %get-tuple-element.28.bc_ref.c_ref, f32[512,32]{1,0:T(8,128)} %get-tuple-element.32.dt_ref, ...), custom_call_target="tpu_custom_call" | custom-call | tf_op jit(solution)/shard_map/intra/pallas_call | solution.py:431
  68.2 1.3 %all-to-all-done.3.in_ref = bf16[16,64,128]{2,1,0:T(8,128)(2,1)S(1)} async-done(((bf16[16,64,128]{2,1,0:T(8,128)(2,1)}), bf16[16,64,128]{2,1,0:T(8,128)(2,1)S(1)}, u32[]{:S(2)}, u32[]{:S(2)}) %all-to-all-start.3) | async-done | bytes 262176 | tf_op jit(solution)/shard_map/all_to_all | solution.py:608
  69.5 8.7 %finish.1 = bf16[512,1024]{1,0:T(8,128)(2,1)} custom-call(bf16[512,128]{1,0:T(8,128)(2,1)} %get-tuple-element.28.bc_ref.c_ref, bf16[16,64,128]{2,1,0:T(8,128)(2,1)S(1)} %all-to-all-done.3.in_ref, f32[1,2048]{1,0:T(1,128)} %bitcast.9, bf16[2048,1024]{1,0:T(8,128)(2,1)} %w_hbm.3, f32[512,512]{1,0:T(8,128)} %get-tuple-element.40.refs_0_, ...), custom_call_target="tpu_custom_call" | custom-call | tf_op jit(solution)/shard_map/finish/pallas_call | solution.py:66
Async XLA Ops:
  1.4 12.2 %all-to-all-start = ((f32[4,8,512]{2,1,0:T(8,128)}), f32[4,8,512]{2,1,0:T(8,128)S(1)}, u32[]{:S(2)}, u32[]{:S(2)}) async-start(f32[4,8,512]{2,1,0:T(8,128)} %get-tuple-element.27), calls=%async_computation | async-start | bytes 131072 | tf_op jit(solution)/shard_map/all_to_all | solution.py:592
  6.3 7.3 %collective-permute-start = (bf16[8,1024]{1,0:T(8,128)(2,1)}, bf16[8,1024]{1,0:T(8,128)(2,1)S(1)}, u32[]{:S(2)}, u32[]{:S(2)}) collective-permute-start(bf16[8,1024]{1,0:T(8,128)(2,1)} %get-tuple-element.26), channel_id=1, source_target_pairs={{0,1},{1,2},{2,3},{3,4},{4,5},{5,6},{6,7},{7,8},{8,9},{9,10},{10,1... | collective-permute-start | bytes 49160 | tf_op jit(solution)/shard_map/ppermute | solution.py:593
  27.0 12.8 %all-to-all-start.1 = ((bf16[16,72,128]{2,1,0:T(8,128)(2,1)}), bf16[16,72,128]{2,1,0:T(8,128)(2,1)S(1)}, u32[]{:S(2)}, u32[]{:S(2)}) async-start(bf16[16,72,128]{2,1,0:T(8,128)(2,1)} %get-tuple-element.29), calls=%async_computation.1 | async-start | bytes 589824 | tf_op jit(solution)/shard_map/all_to_all | solution.py:597
  40.6 16.4 %all-to-all-start.2 = ((bf16[8,72,128]{2,1,0:T(8,128)(2,1)}), bf16[8,72,128]{2,1,0:T(8,128)(2,1)S(1)}, u32[]{:S(2)}, u32[]{:S(2)}) async-start(bf16[8,72,128]{2,1,0:T(8,128)(2,1)} %fold.1), calls=%async_computation.2 | async-start | bytes 294912 | tf_op jit(solution)/shard_map/all_to_all | solution.py:603
  57.8 11.7 %all-to-all-start.3 = ((bf16[16,64,128]{2,1,0:T(8,128)(2,1)}), bf16[16,64,128]{2,1,0:T(8,128)(2,1)S(1)}, u32[]{:S(2)}, u32[]{:S(2)}) async-start(bf16[16,64,128]{2,1,0:T(8,128)(2,1)} %unfold.1), calls=%async_computation.3 | async-start | bytes 524288 | tf_op jit(solution)/shard_map/all_to_all | solution.py:608

commit v4 on v3

--- a/solution.py
+++ b/solution.py
@@ -23,10 +23,13 @@
 WIDTH = 256
 OWNED = 128
 TOGETHER = 1
-SPLIT = (2, 4, 2)
+SPLIT = (3, 3, 2)
+FINE = 256
+SEND = 512
+CHUNKS = 2
 F32 = jnp.float32
 BF16 = jnp.bfloat16
-OWN = jnp.float32
+OWN = jnp.bfloat16
 LIMIT = 60 * 1024 * 1024
 LOG2E = 1.4426950408889634
 FAR_AWAY = pl.BlockSpec(memory_space=pltpu.HBM)
@@ -100,7 +103,8 @@
     return ((row % HEADS) == (chan // HEAD_DIM)).astype(F32).astype(BF16)
 
 
-def pack_kernel(w_ref, b_ref, dt_ref, a_ref, skip_ref, tok_ref, out_ref, tail_ref):
+def pack_kernel(w_ref, b_ref, dt_ref, a_ref, skip_ref, wbc_ref, bbc_ref, gain_ref,
+                tok_ref, out_ref, tail_ref, gain_out):
     out_ref[...] = jnp.zeros_like(out_ref)
     here = dt_ref.shape[1]
     for k in range(out_ref.shape[0]):
@@ -108,12 +112,24 @@
         out_ref[k, CONV : CONV + 1] = b_ref[...]
         for row, ref in ((5, dt_ref), (6, a_ref), (7, skip_ref)):
             out_ref[k, row : row + 1, 0:here] = ref[...]
+        for tap in range(CONV):
+            row, cols = bc_slot(tap)
+            out_ref[k, row : row + 1, cols] = wbc_ref[tap : tap + 1]
+        row, cols = bc_slot(CONV)
+        out_ref[k, row : row + 1, cols] = bbc_ref[...]
     tail_ref[...] = tok_ref[...]
-
-
-def pack(weight, bias, dt_bias, a_log, skip_d, tokens, copies):
+    gain_out[...] = jnp.broadcast_to(gain_ref[...], gain_out.shape)
+
+
+def bc_slot(k):
+    at = 128 * (1 + k % 3)
+    return 5 + k // 3, slice(at, at + BC)
+
+
+def pack(small, tokens, copies):
     rows, depth = tokens.shape
-    small = (weight, bias[None], dt_bias[None], a_log[None], skip_d[None])
+    small = [a if a.ndim == 2 else a[None] for a in small]
+    wide = small[0].shape[1]
 
     def whole(a):
         return pl.BlockSpec(a.shape, lambda g: (0, 0))
@@ -124,12 +140,14 @@
         in_specs=[whole(a) for a in small]
         + [pl.BlockSpec((8, depth), lambda g: (rows // 8 - 1, 0))],
         out_specs=[
-            pl.BlockSpec((copies, 8, weight.shape[1]), lambda g: (0, 0, 0)),
+            pl.BlockSpec((copies, 8, wide), lambda g: (0, 0, 0)),
             pl.BlockSpec((8, depth), lambda g: (0, 0)),
+            pl.BlockSpec((8, DINNER), lambda g: (0, 0)),
         ],
         out_shape=[
-            jax.ShapeDtypeStruct((copies, 8, weight.shape[1]), F32),
+            jax.ShapeDtypeStruct((copies, 8, wide), F32),
             jax.ShapeDtypeStruct((8, depth), BF16),
+            jax.ShapeDtypeStruct((8, DINNER), F32),
         ],
         compiler_params=params(),
         name="pack",
@@ -164,13 +182,13 @@
 
 
 def state_kernel(
-    tok_hbm, halo_ref, w_hbm, wsmall_hbm, par, wbc_ref, bbc_ref,
-    xc_hbm, z_hbm, bc_hbm, dt_hbm, cum_hbm, skip_hbm, slab_ref,
-    raw, tok, w_ref, wsmall, xc_ref, z_ref, bc_ref, dt_ref, cum_ref, skip_ref,
+    tok_hbm, halo_ref, w_hbm, wsmall_hbm, par,
+    xc_hbm, mine_hbm, bc_hbm, dt_hbm, cum_hbm, skip_hbm, slab_ref,
+    raw, tok, w_ref, wsmall, xc_ref, bc_ref, dt_ref, cum_ref, skip_ref,
     wgt, bt, in_sem, out_sem,
 ):
     rows = tok_hbm.shape[0]
-    groups = DINNER // WIDTH
+    groups = DINNER // FINE
     half = DINNER
     fetch_tok = start(tok_hbm, raw, in_sem.at[0])
     fetch_small = start(wsmall_hbm, wsmall, in_sem.at[1])
@@ -186,19 +204,18 @@
         here = slice(k * SUB, (k + 1) * SUB)
         tok[PAD + k * SUB : PAD + (k + 1) * SUB] = dot(order, raw[here]).astype(BF16)
     fetch_small.wait()
-    begin(tok, wsmall, par, wbc_ref, bbc_ref, bc_ref, dt_ref, cum_ref, wgt, bt)
+    begin(tok, wsmall, par, bc_ref, dt_ref, cum_ref, wgt, bt)
     sends = [
+        start(tok.at[PAD:], mine_hbm, out_sem.at[4]),
         start(bc_ref, bc_hbm, out_sem.at[0]),
         start(dt_ref, dt_hbm, out_sem.at[1]),
         start(cum_ref, cum_hbm, out_sem.at[2]),
     ]
 
     def project(g):
-        at = 2 * g * WIDTH % half
-        both = dot(tok[...], w_ref[2 * g * WIDTH // half, :, at : at + 2 * WIDTH])
-        both = both.astype(BF16)
-        z_ref[:, g * WIDTH : (g + 1) * WIDTH] = half_lanes(both[PAD:], 0)
-        return half_lanes(both, 1).astype(F32)
+        at = 2 * g * FINE % half
+        w = half_lanes(w_ref[2 * g * FINE // half, :, at : at + 2 * FINE], 1)
+        return dot(tok[...], w).astype(BF16).astype(F32)
 
     wide = par.shape[2]
     for part in range(2):
@@ -209,10 +226,10 @@
             x = ahead
             if g + 1 in mine_groups:
                 ahead = project(g + 1)
-            cols = slice(g * WIDTH, (g + 1) * WIDTH)
-            spread = dot(wgt[...], one_hot(g * WIDTH, WIDTH))
-            at = g * WIDTH % wide
-            mine = par[g * WIDTH // wide, :, at : at + WIDTH]
+            cols = slice(g * FINE, (g + 1) * FINE)
+            spread = dot(wgt[...], one_hot(g * FINE, FINE))
+            at = g * FINE % wide
+            mine = par[g * FINE // wide, :, at : at + FINE]
             blocks = convolve(x, mine[0:CONV], mine[CONV : CONV + 1])
             xc = jnp.concatenate([block.astype(BF16) for block in blocks], axis=0)
             xc_ref[:, cols] = xc
@@ -220,22 +237,21 @@
             state = dot(bt[...], weighted)
             extra = spread[rows : rows + 8]
             skip_ref[:, cols] = extra
-            for i in range(WIDTH // OWNED):
+            for i in range(FINE // OWNED):
                 own = slice(i * OWNED, (i + 1) * OWNED)
-                owner = g * WIDTH // OWNED + i
+                owner = g * FINE // OWNED + i
                 slab_ref[owner, 0:STATE] = state[:, own].astype(BF16)
                 slab_ref[owner, STATE : STATE + 8] = extra[:, own].astype(BF16)
-        cols = slice(part * DINNER // 2, (part + 1) * DINNER // 2)
-        for k, (ref, hbm) in enumerate(((xc_ref, xc_hbm), (z_ref, z_hbm))):
-            sends.append(
-                start(ref.at[:, cols], hbm.at[:, cols], out_sem.at[3 + 2 * part + k])
-            )
-    sends.append(start(skip_ref, skip_hbm, out_sem.at[7]))
+            if (g + 1) * FINE % SEND == 0:
+                cols = slice((g + 1) * FINE - SEND, (g + 1) * FINE)
+                sem = out_sem.at[5 + cols.start // SEND]
+                sends.append(start(xc_ref.at[:, cols], xc_hbm.at[:, cols], sem))
+    sends.append(start(skip_ref, skip_hbm, out_sem.at[3]))
     for copy in sends:
         copy.wait()
 
 
-def begin(tok, wsmall_ref, par, wbc_ref, bbc_ref, bc_ref, dt_ref, cum_ref, wgt, bt):
+def begin(tok, wsmall_ref, par, bc_ref, dt_ref, cum_ref, wgt, bt):
     rows = dt_ref.shape[0]
     blocks = par.shape[0]
     each = HEADS // blocks
@@ -282,18 +298,19 @@
         ],
         axis=0,
     )
-    conved = jnp.concatenate(
-        convolve(small[:, :BC], wbc_ref[...], bbc_ref[...]), axis=0
-    )
+    slots = [bc_slot(k) for k in range(CONV + 1)]
+    taps = [par[0, row : row + 1, cols] for row, cols in slots]
+    weights = jnp.concatenate(taps[:CONV], axis=0)
+    conved = jnp.concatenate(convolve(small[:, :BC], weights, taps[CONV]), axis=0)
     bc_ref[...] = conved.astype(BF16)
     bt[...] = conved.T[:STATE].astype(BF16)
 
 
-def local_state(tokens, halo, w_gate_x, w_small, packed, conv_w, conv_b):
+def local_state(tokens, halo, w_gate_x, w_small, packed):
     rows, depth = tokens.shape
     outs = [
         ((rows, DINNER), BF16),
-        ((rows, DINNER), BF16),
+        ((rows, depth), BF16),
         ((rows, BC), BF16),
         ((rows, HEADS), F32),
         ((rows, HEADS), F32),
@@ -301,18 +318,18 @@
     ]
     return call(
         state_kernel,
-        [tokens, on_chip(halo), w_gate_x, w_small, on_chip(packed), conv_w, conv_b],
+        [tokens, on_chip(halo), w_gate_x, w_small, on_chip(packed)],
         outs + [((DINNER // OWNED, STATE + 8, OWNED), BF16)],
         [
             pltpu.VMEM((rows, depth), BF16),
             pltpu.VMEM((PAD + rows, depth), BF16),
             pltpu.VMEM((2, depth, DINNER), BF16),
             pltpu.VMEM(w_small.shape, BF16),
-            *(pltpu.VMEM(shape, dtype) for shape, dtype in outs),
+            *(pltpu.VMEM(shape, dtype) for shape, dtype in outs[:1] + outs[2:]),
             pltpu.VMEM((rows + 8, 2 * HEADS), BF16),
             pltpu.VMEM((STATE, rows), BF16),
             pltpu.SemaphoreType.DMA((4,)),
-            pltpu.SemaphoreType.DMA((8,)),
+            pltpu.SemaphoreType.DMA((5 + DINNER // SEND,)),
         ],
         "local_state",
         far=(0, 2, 3),
@@ -351,7 +368,7 @@
 
 
 def intra_kernel(
-    first_group, xc_ref, z_ref, bc_ref, dt_ref, cum_ref, skip_ref,
+    first_group, xc_ref, tok_ref, w_ref, bc_ref, dt_ref, cum_ref, skip_ref,
     own_ref, scale_ref, scores, left, rowlog, bt, wgt,
 ):
     rows = xc_ref.shape[0]
@@ -375,6 +392,8 @@
         spread = one_hot(g * WIDTH, WIDTH)
         pick = (pr % HEADS == g * heads + pc // SUB).astype(F32).astype(BF16)
         skip = skip_ref[2:3, mine]
+        w = half_lanes(w_ref[:, 2 * i * WIDTH : 2 * (i + 1) * WIDTH], 0)
+        z = dot(tok_ref[...], w).astype(BF16).astype(F32)
         state = jnp.zeros((STATE, WIDTH), F32)
         for k in range(blocks):
             here = slice(k * SUB, (k + 1) * SUB)
@@ -413,14 +432,14 @@
                 shrink = dot(wgt[here], spread)
                 fresh = dot(bt[:, here], (xf * shrink).astype(BF16))
                 state = state * grow[SUB - 1 : SUB] + fresh
-            gate = silu(z_ref[here, mine].astype(F32))
+            gate = silu(z[here])
             own_ref[here, mine] = ((y + skip * xf) * gate).astype(own_ref.dtype)
             full = dot(wgt[2 * rows + k * SUB : 2 * rows + (k + 1) * SUB], spread)
             scale_ref[here, mine] = (full * gate).astype(BF16)
 
 
-def intra(first_group, groups, xc, z, bc, dt, cum, skips):
-    rows = xc.shape[0]
+def intra(first_group, groups, xc, tokens, w_gate_x, bc, dt, cum, skips):
+    rows, depth = tokens.shape
     together = TOGETHER
     group = first_group // together
     wide = together * WIDTH
@@ -433,7 +452,8 @@
         grid=(groups // together,),
         in_specs=[
             pl.BlockSpec((rows, wide), lambda i: (0, i + group)),
-            pl.BlockSpec((rows, wide), lambda i: (0, i + group)),
+            whole(tokens),
+            pl.BlockSpec((depth, 2 * wide), lambda i: (0, i + group)),
             whole(bc),
             whole(dt),
             whole(cum),
@@ -456,7 +476,7 @@
         ],
         compiler_params=params(),
         name="intra",
-    )(xc, z, bc, dt, cum, skips)
+    )(xc, tokens, w_gate_x, bc, dt, cum, skips)
 
 
 def through(state, slab):
@@ -504,79 +524,93 @@
     return call(unfold_kernel, operands, [out], [], "unfold", scalars=(me,))[0]
 
 
-def finish_kernel(parts, c_ref, in_ref, gain_ref, w_hbm, *refs):
+def finish_kernel(parts, bc_hbm, in_ref, gain_hbm, w_hbm, *refs):
     own_hbm, scale_hbm = refs[:parts], refs[parts : 2 * parts]
-    out_ref, w_ref, own_all, scale_all, acc, in_sem, w_sem = refs[2 * parts :]
-    rows = c_ref.shape[0]
-    halves = 2
-    span = DINNER // halves
-    fetches = []
-    fetch_w = []
-    for k in range(halves):
+    out_hbm, bc_ref, gain_ref, w_ref, own_all, scale_all = refs[2 * parts : 2 * parts + 6]
+    acc, out_ref, in_sem, w_sem = refs[2 * parts + 6 :]
+    rows = bc_hbm.shape[0]
+    span = DINNER // CHUNKS
+    small = [
+        start(bc_hbm, bc_ref, w_sem.at[CHUNKS + rows // SUB]),
+        start(gain_hbm, gain_ref, w_sem.at[CHUNKS + rows // SUB + 1]),
+    ]
+    fetches, fetch_w = [], []
+    for k in range(CHUNKS):
         fetches.append([])
         at = 0
         for p in range(parts):
             low, high = max(at, k * span), min(at + own_hbm[p].shape[1], (k + 1) * span)
             if low < high:
                 there, here = slice(low - at, high - at), slice(low, high)
-                for i, (hbm, ref) in enumerate(
-                    ((own_hbm[p], own_all), (scale_hbm[p], scale_all))
-                ):
+                pairs = ((own_hbm[p], own_all), (scale_hbm[p], scale_all))
+                for i, (hbm, ref) in enumerate(pairs):
                     source, target = hbm.at[:, there], ref.at[:, here]
                     fetches[k].append(start(source, target, in_sem.at[k, p, i]))
             at += own_hbm[p].shape[1]
         part = slice(k * span, (k + 1) * span)
         fetch_w.append(start(w_hbm.at[part], w_ref.at[part], w_sem.at[k]))
-    total = jnp.zeros((rows, 128), F32)
 
     def gate(k, total):
         sides = []
         for g in range(k * span // WIDTH, (k + 1) * span // WIDTH):
             cols = slice(g * WIDTH, (g + 1) * WIDTH)
             slabs = [in_ref[2 * g], in_ref[2 * g + 1]]
-            carried = dot(c_ref[:, STATE:], jnp.concatenate(slabs, axis=1))
-            gated = own_all[:, cols] + scale_all[:, cols].astype(F32) * carried
+            carried = dot(bc_ref[:, STATE:], jnp.concatenate(slabs, axis=1))
+            scale = scale_all[:, cols].astype(F32)
+            gated = own_all[:, cols].astype(F32) + scale * carried
             gated = gated.astype(BF16).astype(F32)
             square = gated * gated
             total = total + square[:, :128] + square[:, 128:]
-            sides.append((gated * gain_ref[:, cols]).astype(BF16))
+            sides.append((gated * gain_ref[0:1, cols]).astype(BF16))
         return jnp.concatenate(sides, axis=1), total
 
-    for copy in fetches[0]:
+    total = jnp.zeros((rows, 128), F32)
+    for copy in small:
         copy.wait()
-    left, total = gate(0, total)
-    for copy in fetches[1] + fetch_w[:1]:
-        copy.wait()
-    acc[...] = dot(left, w_ref[:span])
-    right, total = gate(1, total)
-    fetch_w[1].wait()
+    for k in range(CHUNKS):
+        for copy in fetches[k]:
+            copy.wait()
+        side, total = gate(k, total)
+        fetch_w[k].wait()
+        product = dot(side, w_ref[k * span : (k + 1) * span])
+        if k > 0:
+            product = acc[...] + product
+        if k + 1 < CHUNKS:
+            acc[...] = product
     mean = jnp.sum(total, axis=1, keepdims=True) * (1.0 / DINNER)
-    product = (acc[...] + dot(right, w_ref[span:])) * lax.rsqrt(mean + EPSILON)
-    product = product.astype(BF16)
+    product = (product * lax.rsqrt(mean + EPSILON)).astype(BF16)
     order = reorder(back=True)
+    sends = []
     for k in range(rows // SUB):
         here = slice(k * SUB, (k + 1) * SUB)
         out_ref[here] = dot(order, product[here]).astype(BF16)
-
-
-def finish(bc, incoming, owns, scales, norm_gain, w_out):
+        sends.append(start(out_ref.at[here], out_hbm.at[here], w_sem.at[CHUNKS + k]))
+    for copy in sends:
+        copy.wait()
+
+
+def finish(bc, incoming, owns, scales, gain, w_out):
     rows = bc.shape[0]
     columns = w_out.shape[1]
     parts = len(owns)
     return call(
         functools.partial(finish_kernel, parts),
-        [bc, on_chip(incoming), norm_gain, w_out, *owns, *scales],
+        [bc, on_chip(incoming), gain, w_out, *owns, *scales],
         [((rows, columns), BF16)],
         [
+            pltpu.VMEM(bc.shape, BF16),
+            pltpu.VMEM(gain.shape, F32),
             pltpu.VMEM(w_out.shape, BF16),
-            pltpu.VMEM((rows, DINNER), F32),
+            pltpu.VMEM((rows, DINNER), OWN),
             pltpu.VMEM((rows, DINNER), BF16),
             pltpu.VMEM((rows, columns), F32),
-            pltpu.SemaphoreType.DMA((2, parts, 2)),
-            pltpu.SemaphoreType.DMA((2,)),
+            pltpu.VMEM((rows, columns), BF16),
+            pltpu.SemaphoreType.DMA((CHUNKS, parts, 2)),
+            pltpu.SemaphoreType.DMA((CHUNKS + rows // SUB + 2,)),
         ],
         "finish",
-        far=range(3, 4 + 2 * parts),
+        far=(0, *range(2, 4 + 2 * parts)),
+        far_out=(0,),
     )[0]
 
 
@@ -588,28 +622,30 @@
     blocks = lax.axis_size(FAR)
     devices = blocks * lax.axis_size(NEAR)
     my_block = lax.axis_index(FAR)[None]
-    packed, tail = pack(conv_x_weight, conv_x_bias, dt_bias, a_log, skip_d, tokens, n)
+    small = [conv_x_weight, conv_x_bias, dt_bias, a_log, skip_d]
+    small += [conv_bc_weight, conv_bc_bias, norm_gain]
+    packed, tail, gain = pack(small, tokens, n)
     packed = lax.all_to_all(packed, "head", 0, 0, tiled=True)
     halo = lax.ppermute(tail, BOTH, [(i, i + 1) for i in range(devices - 1)])
-    xc, z, bc, dt, cum, skips, slabs = local_state(
-        tokens, halo, w_gate_x, w_bc_dt.T, packed, conv_bc_weight, conv_bc_bias[None]
+    xc, mine, bc, dt, cum, skips, slabs = local_state(
+        tokens, halo, w_gate_x, w_bc_dt.T, packed
     )
     near = lax.all_to_all(slabs, NEAR, 0, 0, tiled=True)
     rest = (bc, dt, cum, skips)
     first, second, third = SPLIT
-    own0, scale0 = intra(0, first, xc, z, *rest)
+    own0, scale0 = intra(0, first, xc, mine, w_gate_x, *rest)
     near, own0 = lax.optimization_barrier((near, own0))
     copies = fold(near, blocks)
     far = lax.all_to_all(copies, FAR, 0, 0, tiled=True)
-    z, copies = lax.optimization_barrier((z, copies))
-    own1, scale1 = intra(first, second, xc, z, *rest)
+    xc, copies = lax.optimization_barrier((xc, copies))
+    own1, scale1 = intra(first, second, xc, mine, w_gate_x, *rest)
     far, own1 = lax.optimization_barrier((far, own1))
     incoming = unfold(my_block, near, far)
     back = lax.all_to_all(incoming, NEAR, 0, 0, tiled=True)
-    z, incoming = lax.optimization_barrier((z, incoming))
-    own2, scale2 = intra(first + second, third, xc, z, *rest)
+    xc, incoming = lax.optimization_barrier((xc, incoming))
+    own2, scale2 = intra(first + second, third, xc, mine, w_gate_x, *rest)
     owns, scales = (own0, own1, own2), (scale0, scale1, scale2)
-    return finish(bc, back, owns, scales, norm_gain[None], w_out)
+    return finish(bc, back, owns, scales, gain, w_out)
 
 
 def solution(mesh):

time: 79 us -> 76.3 us (0.966)
  waiting for transfers between devices: 6.73 us -> 4.12 us
  Pallas kernels: 46.1 us -> 44.8 us
  starting transfers between devices: 25.3 us -> 26.3 us
    pallas_call x4, Pallas kernels: 23.6 us -> 18.6 us  [call(): pl.pallas_call(kernel, in_specs=specs, out_specs=[FAR_AWAY if i in far_ou...]
    pallas_call x3, Pallas kernels: 21.1 us -> 24.6 us  [intra(): pl.pallas_call(functools.partial(intra_kernel, first_group), grid=(groups...]
    all_to_all x1, waiting for transfers between devices: 1.51 us -> 0.01 us  [on_device(): near = lax.all_to_all(slabs, NEAR, 0, 0, tiled=True)]
    all_to_all x1, waiting for transfers between devices: 1.27 us -> 0.16 us  [on_device(): back = lax.all_to_all(incoming, NEAR, 0, 0, tiled=True)]
    all_to_all x1, starting transfers between devices: 4.43 us -> 5.37 us  [on_device(): back = lax.all_to_all(incoming, NEAR, 0, 0, tiled=True)]
  transfers between devices with their start and end apart: 5 -> 5, of which waited for: 3 -> 2; matrix products, arithmetic and copies ran while one was open for 0% -> 0% of each run, Pallas kernels for 27% -> 33%
where the time goes in v4:
time: 76.3 us; the launch traced here: 75.4 us
  Pallas kernels  44.8 us (59%)
  starting transfers between devices  26.3 us (34%)
  waiting for transfers between devices  4.12 us (5%)
    pallas_call x3, Pallas kernels, intra(): pl.pallas_call(functools.partial(intra_kernel, first_group), grid=(groups...  24.6 us
    pallas_call x4, Pallas kernels, call(): pl.pallas_call(kernel, in_specs=specs, out_specs=[FAR_AWAY if i in far_ou...  18.6 us
    all_to_all x1, starting transfers between devices, on_device(): far = lax.all_to_all(copies, FAR, 0, 0, tiled=True)  7.4 us
    all_to_all x1, starting transfers between devices, on_device(): back = lax.all_to_all(incoming, NEAR, 0, 0, tiled=True)  5.37 us
    all_to_all x1, starting transfers between devices, on_device(): near = lax.all_to_all(slabs, NEAR, 0, 0, tiled=True)  5.31 us
    all_to_all x1, starting transfers between devices, on_device(): packed = lax.all_to_all(packed, 'head', 0, 0, tiled=True)  4.84 us
    ppermute x1, waiting for transfers between devices, on_device(): halo = lax.ppermute(tail, BOTH, [(i, i + 1) for i in range(devices - 1)])  3.95 us
    ppermute x1, starting transfers between devices, on_device(): halo = lax.ppermute(tail, BOTH, [(i, i + 1) for i in range(devices - 1)])  3.36 us
  transfers between devices with their start and end apart: 5, of which 2 were waited for; matrix products, arithmetic and copies ran while one was open for 0% of the time, Pallas kernels for 33%

profile of v4, /device:TPU:1, one launch (start us, length us, event | category | flops | bytes accessed | tf_op | source)
XLA Modules:
  0.0 75.4 jit_solution(1517250532565550218)
XLA Ops:
  0.0 1.5 %pack.1 = (f32[4,8,512]{2,1,0:T(8,128)}, bf16[8,1024]{1,0:T(8,128)(2,1)}, f32[8,2048]{1,0:T(8,128)}) custom-call(f32[4,512]{1,0:T(4,128)} %w_ref.4, f32[1,512]{1,0:T(1,128)} %bitcast.10, f32[1,8]{1,0:T(1,128)} %bitcast.11, f32[1,8]{1,0:T(1,128)} %bitcast.12, f32[1,8]{1,0:T(1,128)} %bitcast.13, f32[4,128]{1,0:T(4,128)} %wbc_ref.1, f32[1,128]{1,0:T(1,128)} %bitcast.14, ...), custom_call_target="tpu_custom_call" | custom-call | tf_op jit(solution)/shard_map/pack/pallas_call | solution.py:137
  1.5 4.8 %all-to-all-start = ((f32[4,8,512]{2,1,0:T(8,128)}), f32[4,8,512]{2,1,0:T(8,128)S(1)}, u32[]{:S(2)}, u32[]{:S(2)}) async-start(f32[4,8,512]{2,1,0:T(8,128)} %get-tuple-element.28), calls=%async_computation | async-start | bytes 131072 | tf_op jit(solution)/shard_map/all_to_all | solution.py:628
  6.3 3.4 %collective-permute-start = (bf16[8,1024]{1,0:T(8,128)(2,1)}, bf16[8,1024]{1,0:T(8,128)(2,1)S(1)}, u32[]{:S(2)}, u32[]{:S(2)}) collective-permute-start(bf16[8,1024]{1,0:T(8,128)(2,1)} %get-tuple-element.27), channel_id=1, source_target_pairs={{0,1},{1,2},{2,3},{3,4},{4,5},{5,6},{6,7},{7,8},{8,9},{9,10},{10,1... | collective-permute-start | bytes 49160 | tf_op jit(solution)/shard_map/ppermute | solution.py:629
  9.7 4.0 %collective-permute-done.halo_ref = bf16[8,1024]{1,0:T(8,128)(2,1)S(1)} collective-permute-done((bf16[8,1024]{1,0:T(8,128)(2,1)}, bf16[8,1024]{1,0:T(8,128)(2,1)S(1)}, u32[]{:S(2)}, u32[]{:S(2)}) %collective-permute-start) | collective-permute-done | bytes 16416 | tf_op jit(solution)/shard_map/ppermute | solution.py:629
  13.7 0.0 all-to-all-done.par
  13.7 9.9 %local_state.1 = (bf16[512,2048]{1,0:T(8,128)(2,1)}, bf16[512,1024]{1,0:T(8,128)(2,1)}, bf16[512,128]{1,0:T(8,128)(2,1)}, f32[512,32]{1,0:T(8,128)}, f32[512,32]...) custom-call(bf16[512,1024]{1,0:T(8,128)(2,1)} %tok_hbm.1, ...), custom_call_target="tpu_custom_call" | custom-call | tf_op jit(solution)/shard_map/local_state/pallas_call | solution.py:69
  23.6 5.3 %all-to-all-start.1 = ((bf16[16,72,128]{2,1,0:T(8,128)(2,1)}), bf16[16,72,128]{2,1,0:T(8,128)(2,1)S(1)}, u32[]{:S(2)}, u32[]{:S(2)}) async-start(bf16[16,72,128]{2,1,0:T(8,128)(2,1)} %get-tuple-element.30), calls=%async_computation.1 | async-start | bytes 589824 | tf_op jit(solution)/shard_map/all_to_all | solution.py:633
  28.9 8.8 %intra.3 = (bf16[512,768]{1,0:T(8,128)(2,1)}, bf16[512,768]{1,0:T(8,128)(2,1)}) custom-call(bf16[512,2048]{1,0:T(8,128)(2,1)} %get-tuple-element.44.xc_ref, bf16[512,1024]{1,0:T(8,128)(2,1)} %get-tuple-element.32.tok_ref, bf16[1024,4096]{1,0:T(8,128)(2,1)} %w_ref.7, bf16[512,128]{1,0:T(8,128)(2,1)} %get-tuple-element.29.bc_ref.bc_hbm, ...), custom_call_target="tpu_custom_call" | custom-call | tf_op jit(solution)/shard_map/intra/pallas_call | solution.py:450
  37.7 0.0 all-to-all-done.1.in_ref.near_ref
  37.7 0.8 %fold.1 = bf16[8,72,128]{2,1,0:T(8,128)(2,1)} custom-call(bf16[16,72,128]{2,1,0:T(8,128)(2,1)S(1)} %all-to-all-done.1.in_ref.near_ref), custom_call_target="tpu_custom_call" | custom-call | tf_op jit(solution)/shard_map/fold/pallas_call | solution.py:69
  38.5 7.4 %all-to-all-start.2 = ((bf16[8,72,128]{2,1,0:T(8,128)(2,1)}), bf16[8,72,128]{2,1,0:T(8,128)(2,1)S(1)}, u32[]{:S(2)}, u32[]{:S(2)}) async-start(bf16[8,72,128]{2,1,0:T(8,128)(2,1)} %fold.1), calls=%async_computation.2 | async-start | bytes 294912 | tf_op jit(solution)/shard_map/all_to_all | solution.py:639
  45.9 8.8 %intra.4 = (bf16[512,768]{1,0:T(8,128)(2,1)}, bf16[512,768]{1,0:T(8,128)(2,1)}) custom-call(bf16[512,2048]{1,0:T(8,128)(2,1)} %get-tuple-element.44.xc_ref, bf16[512,1024]{1,0:T(8,128)(2,1)} %get-tuple-element.32.tok_ref, bf16[1024,4096]{1,0:T(8,128)(2,1)} %w_ref.7, bf16[512,128]{1,0:T(8,128)(2,1)} %get-tuple-element.29.bc_ref.bc_hbm, ...), custom_call_target="tpu_custom_call" | custom-call | tf_op jit(solution)/shard_map/intra/pallas_call | solution.py:450
  54.7 0.0 all-to-all-done.2.far_ref
  54.7 0.8 %unfold.1 = bf16[16,64,128]{2,1,0:T(8,128)(2,1)} custom-call(s32[1]{0:T(128)} %bitcast.7.me_ref, bf16[16,72,128]{2,1,0:T(8,128)(2,1)S(1)} %all-to-all-done.1.in_ref.near_ref, bf16[8,72,128]{2,1,0:T(8,128)(2,1)S(1)} %all-to-all-done.2.far_ref), custom_call_target="tpu_custom_call" | custom-call | tf_op jit(solution)/shard_map/unfold/pallas_call | solution.py:69
  55.4 5.4 %all-to-all-start.3 = ((bf16[16,64,128]{2,1,0:T(8,128)(2,1)}), bf16[16,64,128]{2,1,0:T(8,128)(2,1)S(1)}, u32[]{:S(2)}, u32[]{:S(2)}) async-start(bf16[16,64,128]{2,1,0:T(8,128)(2,1)} %unfold.1), calls=%async_computation.3 | async-start | bytes 524288 | tf_op jit(solution)/shard_map/all_to_all | solution.py:644
  60.8 7.1 %intra.5 = (bf16[512,512]{1,0:T(8,128)(2,1)}, bf16[512,512]{1,0:T(8,128)(2,1)}) custom-call(bf16[512,2048]{1,0:T(8,128)(2,1)} %get-tuple-element.44.xc_ref, bf16[512,1024]{1,0:T(8,128)(2,1)} %get-tuple-element.32.tok_ref, bf16[1024,4096]{1,0:T(8,128)(2,1)} %w_ref.7, bf16[512,128]{1,0:T(8,128)(2,1)} %get-tuple-element.29.bc_ref.bc_hbm, ...), custom_call_target="tpu_custom_call" | custom-call | tf_op jit(solution)/shard_map/intra/pallas_call | solution.py:450
  67.9 0.2 all-to-all-done.3.in_ref
  68.0 7.2 %finish.1 = bf16[512,1024]{1,0:T(8,128)(2,1)} custom-call(bf16[512,128]{1,0:T(8,128)(2,1)} %get-tuple-element.29.bc_ref.bc_hbm, bf16[16,64,128]{2,1,0:T(8,128)(2,1)S(1)} %all-to-all-done.3.in_ref, f32[8,2048]{1,0:T(8,128)} %get-tuple-element.41.gain_hbm, bf16[2048,1024]{1,0:T(8,128)(2,1)} %w_hbm.3, bf16[512,768]{1,0:T(8,128)(2,1)} %get-tuple-element.42.refs_0_, ...), custom_call_target="tpu_custom_call" | custom-call | tf_op jit(solution)/shard_map/finish/pallas_call | solution.py:69
Async XLA Ops:
  1.5 12.2 %all-to-all-start = ((f32[4,8,512]{2,1,0:T(8,128)}), f32[4,8,512]{2,1,0:T(8,128)S(1)}, u32[]{:S(2)}, u32[]{:S(2)}) async-start(f32[4,8,512]{2,1,0:T(8,128)} %get-tuple-element.28), calls=%async_computation | async-start | bytes 131072 | tf_op jit(solution)/shard_map/all_to_all | solution.py:628
  6.3 7.3 %collective-permute-start = (bf16[8,1024]{1,0:T(8,128)(2,1)}, bf16[8,1024]{1,0:T(8,128)(2,1)S(1)}, u32[]{:S(2)}, u32[]{:S(2)}) collective-permute-start(bf16[8,1024]{1,0:T(8,128)(2,1)} %get-tuple-element.27), channel_id=1, source_target_pairs={{0,1},{1,2},{2,3},{3,4},{4,5},{5,6},{6,7},{7,8},{8,9},{9,10},{10,1... | collective-permute-start | bytes 49160 | tf_op jit(solution)/shard_map/ppermute | solution.py:629
  23.6 14.1 %all-to-all-start.1 = ((bf16[16,72,128]{2,1,0:T(8,128)(2,1)}), bf16[16,72,128]{2,1,0:T(8,128)(2,1)S(1)}, u32[]{:S(2)}, u32[]{:S(2)}) async-start(bf16[16,72,128]{2,1,0:T(8,128)(2,1)} %get-tuple-element.30), calls=%async_computation.1 | async-start | bytes 589824 | tf_op jit(solution)/shard_map/all_to_all | solution.py:633
  38.5 16.2 %all-to-all-start.2 = ((bf16[8,72,128]{2,1,0:T(8,128)(2,1)}), bf16[8,72,128]{2,1,0:T(8,128)(2,1)S(1)}, u32[]{:S(2)}, u32[]{:S(2)}) async-start(bf16[8,72,128]{2,1,0:T(8,128)(2,1)} %fold.1), calls=%async_computation.2 | async-start | bytes 294912 | tf_op jit(solution)/shard_map/all_to_all | solution.py:639
  55.4 12.6 %all-to-all-start.3 = ((bf16[16,64,128]{2,1,0:T(8,128)(2,1)}), bf16[16,64,128]{2,1,0:T(8,128)(2,1)S(1)}, u32[]{:S(2)}, u32[]{:S(2)}) async-start(bf16[16,64,128]{2,1,0:T(8,128)(2,1)} %unfold.1), calls=%async_computation.3 | async-start | bytes 524288 | tf_op jit(solution)/shard_map/all_to_all | solution.py:644

commit v5 on v4

--- a/solution.py
+++ b/solution.py
@@ -33,6 +33,7 @@
 LIMIT = 60 * 1024 * 1024
 LOG2E = 1.4426950408889634
 FAR_AWAY = pl.BlockSpec(memory_space=pltpu.HBM)
+HERE = pl.BlockSpec(memory_space=pltpu.VMEM)
 
 
 def params(steps=1):
@@ -63,14 +64,20 @@
     return [hi, mid, (rest - mid.astype(F32)).astype(BF16)]
 
 
-def call(kernel, args, outs, scratch, name, far=(), far_out=(), scalars=()):
+def call(kernel, args, outs, scratch, name, far=(), far_out=(), near_out=(), scalars=()):
     specs = [pl.BlockSpec(memory_space=pltpu.SMEM)] * len(scalars)
     specs += [FAR_AWAY if i in far else pl.BlockSpec() for i in range(len(args))]
     return pl.pallas_call(
         kernel,
         in_specs=specs,
-        out_specs=[FAR_AWAY if i in far_out else pl.BlockSpec() for i in range(len(outs))],
-        out_shape=[jax.ShapeDtypeStruct(shape, dtype) for shape, dtype in outs],
+        out_specs=[
+            FAR_AWAY if i in far_out else HERE if i in near_out else pl.BlockSpec()
+            for i in range(len(outs))
+        ],
+        out_shape=[
+            pltpu.VMEM(*out) if i in near_out else jax.ShapeDtypeStruct(*out)
+            for i, out in enumerate(outs)
+        ],
         scratch_shapes=scratch,
         compiler_params=params(0),
         name=name,
@@ -334,6 +341,7 @@
         "local_state",
         far=(0, 2, 3),
         far_out=range(6),
+        near_out=(6,),
     )
 
 
@@ -347,13 +355,6 @@
     cum = cum_ref[...]
     step = dt_ref[...]
     ones = jnp.ones((rows, HEADS), BF16)
-    left[...] = jnp.concatenate(split3(cum * LOG2E) + [ones], axis=1)
-    by_row = (jnp.log(jnp.maximum(step, 1e-37)) - cum) * LOG2E
-    by_row = jnp.concatenate([p.astype(F32) for p in split3(by_row)] + [cum], axis=1).T
-    for g in range(HEADS // heads):
-        for p in range(3):
-            first = p * HEADS + g * heads
-            rowlog[g, p, 0:heads] = by_row[first : first + heads]
     starts, ends = [], []
     before = jnp.zeros((1, HEADS), F32)
     for k in range(rows // SUB):
@@ -362,8 +363,16 @@
         ends.append(jnp.broadcast_to(before, (SUB, HEADS)))
     starts = jnp.concatenate(starts, axis=0)
     ends = jnp.concatenate(ends, axis=0)
+    passed = cum - starts
+    left[...] = jnp.concatenate(split3(passed * LOG2E) + [ones], axis=1)
+    by_row = (jnp.log(jnp.maximum(step, 1e-37)) - passed) * LOG2E
+    by_row = jnp.concatenate([p.astype(F32) for p in split3(by_row)] + [cum], axis=1).T
+    for g in range(HEADS // heads):
+        for p in range(3):
+            first = p * HEADS + g * heads
+            rowlog[g, p, 0:heads] = by_row[first : first + heads]
     wgt[0:rows] = hi_lo(step * jnp.exp(ends - cum), 1)
-    wgt[rows : 2 * rows] = hi_lo(jnp.exp(cum - starts), 1)
+    wgt[rows : 2 * rows] = hi_lo(jnp.exp(passed), 1)
     wgt[2 * rows : 3 * rows] = hi_lo(jnp.exp(cum), 1)
 
 
@@ -389,7 +398,7 @@
     for i in range(together):
         g = first_group + pl.program_id(0) * together + i
         mine = slice(i * WIDTH, (i + 1) * WIDTH)
-        spread = one_hot(g * WIDTH, WIDTH)
+        expanded = dot(wgt[...], one_hot(g * WIDTH, WIDTH))
         pick = (pr % HEADS == g * heads + pc // SUB).astype(F32).astype(BF16)
         skip = skip_ref[2:3, mine]
         w = half_lanes(w_ref[:, 2 * i * WIDTH : 2 * (i + 1) * WIDTH], 0)
@@ -425,16 +434,16 @@
                 pieces.append(dot(jnp.concatenate(both, axis=1), right))
             y = jnp.concatenate(pieces, axis=1)
             xf = xc.astype(F32)
-            grow = dot(wgt[rows + k * SUB : rows + (k + 1) * SUB], spread)
+            grow = expanded[rows + k * SUB : rows + (k + 1) * SUB]
             if k > 0:
                 y = y + grow * dot(bc_ref[here, STATE:], state.astype(BF16))
             if k + 1 < blocks:
-                shrink = dot(wgt[here], spread)
+                shrink = expanded[here]
                 fresh = dot(bt[:, here], (xf * shrink).astype(BF16))
                 state = state * grow[SUB - 1 : SUB] + fresh
             gate = silu(z[here])
             own_ref[here, mine] = ((y + skip * xf) * gate).astype(own_ref.dtype)
-            full = dot(wgt[2 * rows + k * SUB : 2 * rows + (k + 1) * SUB], spread)
+            full = expanded[2 * rows + k * SUB : 2 * rows + (k + 1) * SUB]
             scale_ref[here, mine] = (full * gate).astype(BF16)
 
 
@@ -503,7 +512,7 @@
 
 def fold(near, blocks):
     out = ((blocks, *near.shape[1:]), BF16)
-    return call(fold_kernel, [on_chip(near)], [out], [], "fold")[0]
+    return call(fold_kernel, [on_chip(near)], [out], [], "fold", near_out=(0,))[0]
 
 
 def unfold_kernel(me_ref, near_ref, far_ref, out_ref):
@@ -521,7 +530,9 @@
     count = near.shape[0]
     out = ((count, STATE, OWNED), BF16)
     operands = [on_chip(near), on_chip(far)]
-    return call(unfold_kernel, operands, [out], [], "unfold", scalars=(me,))[0]
+    return call(
+        unfold_kernel, operands, [out], [], "unfold", near_out=(0,), scalars=(me,)
+    )[0]
 
 
 def finish_kernel(parts, bc_hbm, in_ref, gain_hbm, w_hbm, *refs):

time: 76.3 us -> 74.6 us (0.978)
  Pallas kernels: 44.8 us -> 42.5 us
    pallas_call x3, Pallas kernels: 24.6 us -> 22.4 us  [intra(): pl.pallas_call(functools.partial(intra_kernel, first_group), grid=(groups...]
  transfers between devices with their start and end apart: 5 -> 5, of which waited for: 2 -> 2; matrix products, arithmetic and copies ran while one was open for 0% -> 0% of each run, Pallas kernels for 33% -> 30%
where the time goes in v5:
time: 74.6 us; the launch traced here: 74 us
  Pallas kernels  42.5 us (57%)
  starting transfers between devices  26.6 us (36%)
  waiting for transfers between devices  4.69 us (6%)
    pallas_call x3, Pallas kernels, intra(): pl.pallas_call(functools.partial(intra_kernel, first_group), grid=(groups...  22.4 us
    pallas_call x4, Pallas kernels, call(): pl.pallas_call(kernel, in_specs=specs, out_specs=[FAR_AWAY if i in far_ou...  18.6 us
    all_to_all x1, starting transfers between devices, on_device(): far = lax.all_to_all(copies, FAR, 0, 0, tiled=True)  7.37 us
    all_to_all x1, starting transfers between devices, on_device(): back = lax.all_to_all(incoming, NEAR, 0, 0, tiled=True)  5.74 us
    all_to_all x1, starting transfers between devices, on_device(): near = lax.all_to_all(slabs, NEAR, 0, 0, tiled=True)  5.31 us
    all_to_all x1, starting transfers between devices, on_device(): packed = lax.all_to_all(packed, 'head', 0, 0, tiled=True)  4.84 us
    ppermute x1, waiting for transfers between devices, on_device(): halo = lax.ppermute(tail, BOTH, [(i, i + 1) for i in range(devices - 1)])  3.95 us
    ppermute x1, starting transfers between devices, on_device(): halo = lax.ppermute(tail, BOTH, [(i, i + 1) for i in range(devices - 1)])  3.36 us
  transfers between devices with their start and end apart: 5, of which 2 were waited for; matrix products, arithmetic and copies ran while one was open for 0% of the time, Pallas kernels for 30%

profile of v5, /device:TPU:1, one launch (start us, length us, event | category | flops | bytes accessed | tf_op | source)
XLA Modules:
  0.0 74.0 jit_solution(9709306311654031904)
XLA Ops:
  0.0 1.5 %pack.1 = (f32[4,8,512]{2,1,0:T(8,128)}, bf16[8,1024]{1,0:T(8,128)(2,1)}, f32[8,2048]{1,0:T(8,128)}) custom-call(f32[4,512]{1,0:T(4,128)} %w_ref.4, f32[1,512]{1,0:T(1,128)} %bitcast.10, f32[1,8]{1,0:T(1,128)} %bitcast.11, f32[1,8]{1,0:T(1,128)} %bitcast.12, f32[1,8]{1,0:T(1,128)} %bitcast.13, f32[4,128]{1,0:T(4,128)} %wbc_ref.1, f32[1,128]{1,0:T(1,128)} %bitcast.14, ...), custom_call_target="tpu_custom_call" | custom-call | tf_op jit(solution)/shard_map/pack/pallas_call | solution.py:144
  1.5 4.8 %all-to-all-start = ((f32[4,8,512]{2,1,0:T(8,128)}), f32[4,8,512]{2,1,0:T(8,128)S(1)}, u32[]{:S(2)}, u32[]{:S(2)}) async-start(f32[4,8,512]{2,1,0:T(8,128)} %get-tuple-element.28), calls=%async_computation | async-start | bytes 131072 | tf_op jit(solution)/shard_map/all_to_all | solution.py:639
  6.3 3.4 %collective-permute-start = (bf16[8,1024]{1,0:T(8,128)(2,1)}, bf16[8,1024]{1,0:T(8,128)(2,1)S(1)}, u32[]{:S(2)}, u32[]{:S(2)}) collective-permute-start(bf16[8,1024]{1,0:T(8,128)(2,1)} %get-tuple-element.27), channel_id=1, source_target_pairs={{0,1},{1,2},{2,3},{3,4},{4,5},{5,6},{6,7},{7,8},{8,9},{9,10},{10,1... | collective-permute-start | bytes 49160 | tf_op jit(solution)/shard_map/ppermute | solution.py:640
  9.7 4.0 %collective-permute-done.halo_ref = bf16[8,1024]{1,0:T(8,128)(2,1)S(1)} collective-permute-done((bf16[8,1024]{1,0:T(8,128)(2,1)}, bf16[8,1024]{1,0:T(8,128)(2,1)S(1)}, u32[]{:S(2)}, u32[]{:S(2)}) %collective-permute-start) | collective-permute-done | bytes 16416 | tf_op jit(solution)/shard_map/ppermute | solution.py:640
  13.7 0.0 all-to-all-done.par
  13.7 9.9 %local_state.1 = (bf16[512,2048]{1,0:T(8,128)(2,1)}, bf16[512,1024]{1,0:T(8,128)(2,1)}, bf16[512,128]{1,0:T(8,128)(2,1)}, f32[512,32]{1,0:T(8,128)}, f32[512,32]...) custom-call(bf16[512,1024]{1,0:T(8,128)(2,1)} %tok_hbm.1, ...), custom_call_target="tpu_custom_call" | custom-call | tf_op jit(solution)/shard_map/local_state/pallas_call | solution.py:70
  23.6 5.3 %all-to-all-start.1 = ((bf16[16,72,128]{2,1,0:T(8,128)(2,1)}), bf16[16,72,128]{2,1,0:T(8,128)(2,1)S(1)}, u32[]{:S(2)}, u32[]{:S(2)}) async-start(bf16[16,72,128]{2,1,0:T(8,128)(2,1)} %get-tuple-element.30), calls=%async_computation.1 | async-start | bytes 589824 | tf_op jit(solution)/shard_map/all_to_all | solution.py:644
  28.9 8.0 %intra.3 = (bf16[512,768]{1,0:T(8,128)(2,1)}, bf16[512,768]{1,0:T(8,128)(2,1)}) custom-call(bf16[512,2048]{1,0:T(8,128)(2,1)} %get-tuple-element.44.xc_ref, bf16[512,1024]{1,0:T(8,128)(2,1)} %get-tuple-element.32.tok_ref, bf16[1024,4096]{1,0:T(8,128)(2,1)} %w_ref.7, bf16[512,128]{1,0:T(8,128)(2,1)} %get-tuple-element.29.bc_ref.bc_hbm, ...), custom_call_target="tpu_custom_call" | custom-call | tf_op jit(solution)/shard_map/intra/pallas_call | solution.py:459
  36.9 0.0 all-to-all-done.1.in_ref.near_ref
  36.9 0.8 %fold.1 = bf16[8,72,128]{2,1,0:T(8,128)(2,1)} custom-call(bf16[16,72,128]{2,1,0:T(8,128)(2,1)S(1)} %all-to-all-done.1.in_ref.near_ref), custom_call_target="tpu_custom_call" | custom-call | tf_op jit(solution)/shard_map/fold/pallas_call | solution.py:70
  37.7 7.4 %all-to-all-start.2 = ((bf16[8,72,128]{2,1,0:T(8,128)(2,1)}), bf16[8,72,128]{2,1,0:T(8,128)(2,1)S(1)}, u32[]{:S(2)}, u32[]{:S(2)}) async-start(bf16[8,72,128]{2,1,0:T(8,128)(2,1)} %fold.1), calls=%async_computation.2 | async-start | bytes 294912 | tf_op jit(solution)/shard_map/all_to_all | solution.py:650
  45.0 7.9 %intra.4 = (bf16[512,768]{1,0:T(8,128)(2,1)}, bf16[512,768]{1,0:T(8,128)(2,1)}) custom-call(bf16[512,2048]{1,0:T(8,128)(2,1)} %get-tuple-element.44.xc_ref, bf16[512,1024]{1,0:T(8,128)(2,1)} %get-tuple-element.32.tok_ref, bf16[1024,4096]{1,0:T(8,128)(2,1)} %w_ref.7, bf16[512,128]{1,0:T(8,128)(2,1)} %get-tuple-element.29.bc_ref.bc_hbm, ...), custom_call_target="tpu_custom_call" | custom-call | tf_op jit(solution)/shard_map/intra/pallas_call | solution.py:459
  52.9 0.0 all-to-all-done.2.far_ref
  52.9 0.8 %unfold.1 = bf16[16,64,128]{2,1,0:T(8,128)(2,1)} custom-call(s32[1]{0:T(128)} %bitcast.7.me_ref, bf16[16,72,128]{2,1,0:T(8,128)(2,1)S(1)} %all-to-all-done.1.in_ref.near_ref, bf16[8,72,128]{2,1,0:T(8,128)(2,1)S(1)} %all-to-all-done.2.far_ref), custom_call_target="tpu_custom_call" | custom-call | tf_op jit(solution)/shard_map/unfold/pallas_call | solution.py:70
  53.7 5.7 %all-to-all-start.3 = ((bf16[16,64,128]{2,1,0:T(8,128)(2,1)}), bf16[16,64,128]{2,1,0:T(8,128)(2,1)S(1)}, u32[]{:S(2)}, u32[]{:S(2)}) async-start(bf16[16,64,128]{2,1,0:T(8,128)(2,1)} %unfold.1), calls=%async_computation.3 | async-start | bytes 524288 | tf_op jit(solution)/shard_map/all_to_all | solution.py:655
  59.5 6.5 %intra.5 = (bf16[512,512]{1,0:T(8,128)(2,1)}, bf16[512,512]{1,0:T(8,128)(2,1)}) custom-call(bf16[512,2048]{1,0:T(8,128)(2,1)} %get-tuple-element.44.xc_ref, bf16[512,1024]{1,0:T(8,128)(2,1)} %get-tuple-element.32.tok_ref, bf16[1024,4096]{1,0:T(8,128)(2,1)} %w_ref.7, bf16[512,128]{1,0:T(8,128)(2,1)} %get-tuple-element.29.bc_ref.bc_hbm, ...), custom_call_target="tpu_custom_call" | custom-call | tf_op jit(solution)/shard_map/intra/pallas_call | solution.py:459
  66.0 0.7 all-to-all-done.3.in_ref
  66.7 7.2 %finish.1 = bf16[512,1024]{1,0:T(8,128)(2,1)} custom-call(bf16[512,128]{1,0:T(8,128)(2,1)} %get-tuple-element.29.bc_ref.bc_hbm, bf16[16,64,128]{2,1,0:T(8,128)(2,1)S(1)} %all-to-all-done.3.in_ref, f32[8,2048]{1,0:T(8,128)} %get-tuple-element.41.gain_hbm, bf16[2048,1024]{1,0:T(8,128)(2,1)} %w_hbm.3, bf16[512,768]{1,0:T(8,128)(2,1)} %get-tuple-element.42.refs_0_, ...), custom_call_target="tpu_custom_call" | custom-call | tf_op jit(solution)/shard_map/finish/pallas_call | solution.py:70
Async XLA Ops:
  1.5 12.2 %all-to-all-start = ((f32[4,8,512]{2,1,0:T(8,128)}), f32[4,8,512]{2,1,0:T(8,128)S(1)}, u32[]{:S(2)}, u32[]{:S(2)}) async-start(f32[4,8,512]{2,1,0:T(8,128)} %get-tuple-element.28), calls=%async_computation | async-start | bytes 131072 | tf_op jit(solution)/shard_map/all_to_all | solution.py:639
  6.3 7.3 %collective-permute-start = (bf16[8,1024]{1,0:T(8,128)(2,1)}, bf16[8,1024]{1,0:T(8,128)(2,1)S(1)}, u32[]{:S(2)}, u32[]{:S(2)}) collective-permute-start(bf16[8,1024]{1,0:T(8,128)(2,1)} %get-tuple-element.27), channel_id=1, source_target_pairs={{0,1},{1,2},{2,3},{3,4},{4,5},{5,6},{6,7},{7,8},{8,9},{9,10},{10,1... | collective-permute-start | bytes 49160 | tf_op jit(solution)/shard_map/ppermute | solution.py:640
  23.6 13.3 %all-to-all-start.1 = ((bf16[16,72,128]{2,1,0:T(8,128)(2,1)}), bf16[16,72,128]{2,1,0:T(8,128)(2,1)S(1)}, u32[]{:S(2)}, u32[]{:S(2)}) async-start(bf16[16,72,128]{2,1,0:T(8,128)(2,1)} %get-tuple-element.30), calls=%async_computation.1 | async-start | bytes 589824 | tf_op jit(solution)/shard_map/all_to_all | solution.py:644
  37.7 15.3 %all-to-all-start.2 = ((bf16[8,72,128]{2,1,0:T(8,128)(2,1)}), bf16[8,72,128]{2,1,0:T(8,128)(2,1)S(1)}, u32[]{:S(2)}, u32[]{:S(2)}) async-start(bf16[8,72,128]{2,1,0:T(8,128)(2,1)} %fold.1), calls=%async_computation.2 | async-start | bytes 294912 | tf_op jit(solution)/shard_map/all_to_all | solution.py:650
  53.7 13.0 %all-to-all-start.3 = ((bf16[16,64,128]{2,1,0:T(8,128)(2,1)}), bf16[16,64,128]{2,1,0:T(8,128)(2,1)S(1)}, u32[]{:S(2)}, u32[]{:S(2)}) async-start(bf16[16,64,128]{2,1,0:T(8,128)(2,1)} %unfold.1), calls=%async_computation.3 | async-start | bytes 524288 | tf_op jit(solution)/shard_map/all_to_all | solution.py:655

commit v6 on v5

--- a/solution.py
+++ b/solution.py
@@ -147,13 +147,13 @@
         in_specs=[whole(a) for a in small]
         + [pl.BlockSpec((8, depth), lambda g: (rows // 8 - 1, 0))],
         out_specs=[
-            pl.BlockSpec((copies, 8, wide), lambda g: (0, 0, 0)),
-            pl.BlockSpec((8, depth), lambda g: (0, 0)),
+            HERE,
+            HERE,
             pl.BlockSpec((8, DINNER), lambda g: (0, 0)),
         ],
         out_shape=[
-            jax.ShapeDtypeStruct((copies, 8, wide), F32),
-            jax.ShapeDtypeStruct((8, depth), BF16),
+            pltpu.VMEM((copies, 8, wide), F32),
+            pltpu.VMEM((8, depth), BF16),
             jax.ShapeDtypeStruct((8, DINNER), F32),
         ],
         compiler_params=params(),

time: 74.6 us -> 74.4 us (level)
  no operation moved by 1% of the time
where the time goes in v6:
time: 74.4 us; the launch traced here: 73.8 us
  Pallas kernels  42.5 us (57%)
  starting transfers between devices  26.6 us (36%)
  waiting for transfers between devices  4.48 us (6%)
    pallas_call x3, Pallas kernels, intra(): pl.pallas_call(functools.partial(intra_kernel, first_group), grid=(groups...  22.4 us
    pallas_call x4, Pallas kernels, call(): pl.pallas_call(kernel, in_specs=specs, out_specs=[FAR_AWAY if i in far_ou...  18.6 us
    all_to_all x1, starting transfers between devices, on_device(): far = lax.all_to_all(copies, FAR, 0, 0, tiled=True)  7.39 us
    all_to_all x1, starting transfers between devices, on_device(): back = lax.all_to_all(incoming, NEAR, 0, 0, tiled=True)  5.74 us
    all_to_all x1, starting transfers between devices, on_device(): near = lax.all_to_all(slabs, NEAR, 0, 0, tiled=True)  5.31 us
    all_to_all x1, starting transfers between devices, on_device(): packed = lax.all_to_all(packed, 'head', 0, 0, tiled=True)  4.84 us
    ppermute x1, waiting for transfers between devices, on_device(): halo = lax.ppermute(tail, BOTH, [(i, i + 1) for i in range(devices - 1)])  3.74 us
    ppermute x1, starting transfers between devices, on_device(): halo = lax.ppermute(tail, BOTH, [(i, i + 1) for i in range(devices - 1)])  3.36 us
  transfers between devices with their start and end apart: 5, of which 2 were waited for; matrix products, arithmetic and copies ran while one was open for 0% of the time, Pallas kernels for 30%

profile of v6, /device:TPU:1, one launch (start us, length us, event | category | flops | bytes accessed | tf_op | source)
XLA Modules:
  0.0 73.8 jit_solution(9749492796160406880)
XLA Ops:
  0.0 1.5 %pack.1 = (f32[4,8,512]{2,1,0:T(8,128)}, bf16[8,1024]{1,0:T(8,128)(2,1)S(1)}, f32[8,2048]{1,0:T(8,128)}) custom-call(f32[4,512]{1,0:T(4,128)} %w_ref.4, f32[1,512]{1,0:T(1,128)} %bitcast.10, f32[1,8]{1,0:T(1,128)} %bitcast.11, f32[1,8]{1,0:T(1,128)} %bitcast.12, f32[1,8]{1,0:T(1,128)} %bitcast.13, f32[4,128]{1,0:T(4,128)} %wbc_ref.1, f32[1,128]{1,0:T(1,128)} %bitcast.14, ...), custom_call_target="tpu_custom_call" | custom-call | tf_op jit(solution)/shard_map/pack/pallas_call | solution.py:144
  1.5 4.8 %all-to-all-start = ((f32[4,8,512]{2,1,0:T(8,128)}), f32[4,8,512]{2,1,0:T(8,128)S(1)}, u32[]{:S(2)}, u32[]{:S(2)}) async-start(f32[4,8,512]{2,1,0:T(8,128)} %get-tuple-element.28), calls=%async_computation | async-start | bytes 131072 | tf_op jit(solution)/shard_map/all_to_all | solution.py:639
  6.3 3.4 %collective-permute-start = (bf16[8,1024]{1,0:T(8,128)(2,1)S(1)}, bf16[8,1024]{1,0:T(8,128)(2,1)S(1)}, u32[]{:S(2)}, u32[]{:S(2)}) collective-permute-start(bf16[8,1024]{1,0:T(8,128)(2,1)S(1)} %get-tuple-element.27), channel_id=1, source_target_pairs={{0,1},{1,2},{2,3},{3,4},{4,5},{5,6},{6,7},{7,8},{8,9},{9,10},{10,1... | collective-permute-start | bytes 49160 | tf_op jit(solution)/shard_map/ppermute | solution.py:640
  9.7 3.7 %collective-permute-done.halo_ref = bf16[8,1024]{1,0:T(8,128)(2,1)S(1)} collective-permute-done((bf16[8,1024]{1,0:T(8,128)(2,1)S(1)}, bf16[8,1024]{1,0:T(8,128)(2,1)S(1)}, u32[]{:S(2)}, u32[]{:S(2)}) %collective-permute-start) | collective-permute-done | bytes 16416 | tf_op jit(solution)/shard_map/ppermute | solution.py:640
  13.5 0.0 all-to-all-done.par
  13.5 9.9 %local_state.1 = (bf16[512,2048]{1,0:T(8,128)(2,1)}, bf16[512,1024]{1,0:T(8,128)(2,1)}, bf16[512,128]{1,0:T(8,128)(2,1)}, f32[512,32]{1,0:T(8,128)}, f32[512,32]...) custom-call(bf16[512,1024]{1,0:T(8,128)(2,1)} %tok_hbm.1, ...), custom_call_target="tpu_custom_call" | custom-call | tf_op jit(solution)/shard_map/local_state/pallas_call | solution.py:70
  23.4 5.3 %all-to-all-start.1 = ((bf16[16,72,128]{2,1,0:T(8,128)(2,1)}), bf16[16,72,128]{2,1,0:T(8,128)(2,1)S(1)}, u32[]{:S(2)}, u32[]{:S(2)}) async-start(bf16[16,72,128]{2,1,0:T(8,128)(2,1)} %get-tuple-element.30), calls=%async_computation.1 | async-start | bytes 589824 | tf_op jit(solution)/shard_map/all_to_all | solution.py:644
  28.7 8.0 %intra.3 = (bf16[512,768]{1,0:T(8,128)(2,1)}, bf16[512,768]{1,0:T(8,128)(2,1)}) custom-call(bf16[512,2048]{1,0:T(8,128)(2,1)} %get-tuple-element.44.xc_ref, bf16[512,1024]{1,0:T(8,128)(2,1)} %get-tuple-element.32.tok_ref, bf16[1024,4096]{1,0:T(8,128)(2,1)} %w_ref.7, bf16[512,128]{1,0:T(8,128)(2,1)} %get-tuple-element.29.bc_ref.bc_hbm, ...), custom_call_target="tpu_custom_call" | custom-call | tf_op jit(solution)/shard_map/intra/pallas_call | solution.py:459
  36.7 0.0 all-to-all-done.1.in_ref.near_ref
  36.7 0.8 %fold.1 = bf16[8,72,128]{2,1,0:T(8,128)(2,1)} custom-call(bf16[16,72,128]{2,1,0:T(8,128)(2,1)S(1)} %all-to-all-done.1.in_ref.near_ref), custom_call_target="tpu_custom_call" | custom-call | tf_op jit(solution)/shard_map/fold/pallas_call | solution.py:70
  37.4 7.4 %all-to-all-start.2 = ((bf16[8,72,128]{2,1,0:T(8,128)(2,1)}), bf16[8,72,128]{2,1,0:T(8,128)(2,1)S(1)}, u32[]{:S(2)}, u32[]{:S(2)}) async-start(bf16[8,72,128]{2,1,0:T(8,128)(2,1)} %fold.1), calls=%async_computation.2 | async-start | bytes 294912 | tf_op jit(solution)/shard_map/all_to_all | solution.py:650
  44.8 7.9 %intra.4 = (bf16[512,768]{1,0:T(8,128)(2,1)}, bf16[512,768]{1,0:T(8,128)(2,1)}) custom-call(bf16[512,2048]{1,0:T(8,128)(2,1)} %get-tuple-element.44.xc_ref, bf16[512,1024]{1,0:T(8,128)(2,1)} %get-tuple-element.32.tok_ref, bf16[1024,4096]{1,0:T(8,128)(2,1)} %w_ref.7, bf16[512,128]{1,0:T(8,128)(2,1)} %get-tuple-element.29.bc_ref.bc_hbm, ...), custom_call_target="tpu_custom_call" | custom-call | tf_op jit(solution)/shard_map/intra/pallas_call | solution.py:459
  52.7 0.0 all-to-all-done.2.far_ref
  52.7 0.8 %unfold.1 = bf16[16,64,128]{2,1,0:T(8,128)(2,1)} custom-call(s32[1]{0:T(128)} %bitcast.7.me_ref, bf16[16,72,128]{2,1,0:T(8,128)(2,1)S(1)} %all-to-all-done.1.in_ref.near_ref, bf16[8,72,128]{2,1,0:T(8,128)(2,1)S(1)} %all-to-all-done.2.far_ref), custom_call_target="tpu_custom_call" | custom-call | tf_op jit(solution)/shard_map/unfold/pallas_call | solution.py:70
  53.5 5.7 %all-to-all-start.3 = ((bf16[16,64,128]{2,1,0:T(8,128)(2,1)}), bf16[16,64,128]{2,1,0:T(8,128)(2,1)S(1)}, u32[]{:S(2)}, u32[]{:S(2)}) async-start(bf16[16,64,128]{2,1,0:T(8,128)(2,1)} %unfold.1), calls=%async_computation.3 | async-start | bytes 524288 | tf_op jit(solution)/shard_map/all_to_all | solution.py:655
  59.2 6.5 %intra.5 = (bf16[512,512]{1,0:T(8,128)(2,1)}, bf16[512,512]{1,0:T(8,128)(2,1)}) custom-call(bf16[512,2048]{1,0:T(8,128)(2,1)} %get-tuple-element.44.xc_ref, bf16[512,1024]{1,0:T(8,128)(2,1)} %get-tuple-element.32.tok_ref, bf16[1024,4096]{1,0:T(8,128)(2,1)} %w_ref.7, bf16[512,128]{1,0:T(8,128)(2,1)} %get-tuple-element.29.bc_ref.bc_hbm, ...), custom_call_target="tpu_custom_call" | custom-call | tf_op jit(solution)/shard_map/intra/pallas_call | solution.py:459
  65.7 0.7 all-to-all-done.3.in_ref
  66.5 7.2 %finish.1 = bf16[512,1024]{1,0:T(8,128)(2,1)} custom-call(bf16[512,128]{1,0:T(8,128)(2,1)} %get-tuple-element.29.bc_ref.bc_hbm, bf16[16,64,128]{2,1,0:T(8,128)(2,1)S(1)} %all-to-all-done.3.in_ref, f32[8,2048]{1,0:T(8,128)} %get-tuple-element.41.gain_hbm, bf16[2048,1024]{1,0:T(8,128)(2,1)} %w_hbm.3, bf16[512,768]{1,0:T(8,128)(2,1)} %get-tuple-element.42.refs_0_, ...), custom_call_target="tpu_custom_call" | custom-call | tf_op jit(solution)/shard_map/finish/pallas_call | solution.py:70
Async XLA Ops:
  1.5 12.0 %all-to-all-start = ((f32[4,8,512]{2,1,0:T(8,128)}), f32[4,8,512]{2,1,0:T(8,128)S(1)}, u32[]{:S(2)}, u32[]{:S(2)}) async-start(f32[4,8,512]{2,1,0:T(8,128)} %get-tuple-element.28), calls=%async_computation | async-start | bytes 131072 | tf_op jit(solution)/shard_map/all_to_all | solution.py:639
  6.3 7.1 %collective-permute-start = (bf16[8,1024]{1,0:T(8,128)(2,1)S(1)}, bf16[8,1024]{1,0:T(8,128)(2,1)S(1)}, u32[]{:S(2)}, u32[]{:S(2)}) collective-permute-start(bf16[8,1024]{1,0:T(8,128)(2,1)S(1)} %get-tuple-element.27), channel_id=1, source_target_pairs={{0,1},{1,2},{2,3},{3,4},{4,5},{5,6},{6,7},{7,8},{8,9},{9,10},{10,1... | collective-permute-start | bytes 49160 | tf_op jit(solution)/shard_map/ppermute | solution.py:640
  23.4 13.3 %all-to-all-start.1 = ((bf16[16,72,128]{2,1,0:T(8,128)(2,1)}), bf16[16,72,128]{2,1,0:T(8,128)(2,1)S(1)}, u32[]{:S(2)}, u32[]{:S(2)}) async-start(bf16[16,72,128]{2,1,0:T(8,128)(2,1)} %get-tuple-element.30), calls=%async_computation.1 | async-start | bytes 589824 | tf_op jit(solution)/shard_map/all_to_all | solution.py:644
  37.4 15.3 %all-to-all-start.2 = ((bf16[8,72,128]{2,1,0:T(8,128)(2,1)}), bf16[8,72,128]{2,1,0:T(8,128)(2,1)S(1)}, u32[]{:S(2)}, u32[]{:S(2)}) async-start(bf16[8,72,128]{2,1,0:T(8,128)(2,1)} %fold.1), calls=%async_computation.2 | async-start | bytes 294912 | tf_op jit(solution)/shard_map/all_to_all | solution.py:650
  53.5 13.0 %all-to-all-start.3 = ((bf16[16,64,128]{2,1,0:T(8,128)(2,1)}), bf16[16,64,128]{2,1,0:T(8,128)(2,1)S(1)}, u32[]{:S(2)}, u32[]{:S(2)}) async-start(bf16[16,64,128]{2,1,0:T(8,128)(2,1)} %unfold.1), calls=%async_computation.3 | async-start | bytes 524288 | tf_op jit(solution)/shard_map/all_to_all | solution.py:655

commit v7 on v6

--- a/solution.py
+++ b/solution.py
@@ -23,8 +23,8 @@
 WIDTH = 256
 OWNED = 128
 TOGETHER = 1
-SPLIT = (3, 3, 2)
-FINE = 256
+SPLIT = (2, 3, 3)
+FINE = 512
 SEND = 512
 CHUNKS = 2
 F32 = jnp.float32

time: 74.4 us -> 73.7 us (level)
  starting transfers between devices: 26.6 us -> 25.6 us
    all_to_all x1, starting transfers between devices: 5.74 us -> 4.72 us  [on_device(): back = lax.all_to_all(incoming, NEAR, 0, 0, tiled=True)]
    all_to_all x1, waiting for transfers between devices: 0.01 us -> 1.02 us  [on_device(): near = lax.all_to_all(slabs, NEAR, 0, 0, tiled=True)]
  transfers between devices with their start and end apart: 5 -> 5, of which waited for: 2 -> 2; matrix products, arithmetic and copies ran while one was open for 0% -> 0% of each run, Pallas kernels for 30% -> 31%
where the time goes in v7:
time: 73.7 us; the launch traced here: 72.9 us
  Pallas kernels  42.3 us (57%)
  starting transfers between devices  25.6 us (35%)
  waiting for transfers between devices  4.77 us (6%)
    pallas_call x3, Pallas kernels, intra(): pl.pallas_call(functools.partial(intra_kernel, first_group), grid=(groups...  22.4 us
    pallas_call x4, Pallas kernels, call(): pl.pallas_call(kernel, in_specs=specs, out_specs=[FAR_AWAY if i in far_ou...  18.5 us
    all_to_all x1, starting transfers between devices, on_device(): far = lax.all_to_all(copies, FAR, 0, 0, tiled=True)  7.37 us
    all_to_all x1, starting transfers between devices, on_device(): near = lax.all_to_all(slabs, NEAR, 0, 0, tiled=True)  5.31 us
    all_to_all x1, starting transfers between devices, on_device(): packed = lax.all_to_all(packed, 'head', 0, 0, tiled=True)  4.84 us
    all_to_all x1, starting transfers between devices, on_device(): back = lax.all_to_all(incoming, NEAR, 0, 0, tiled=True)  4.72 us
    ppermute x1, waiting for transfers between devices, on_device(): halo = lax.ppermute(tail, BOTH, [(i, i + 1) for i in range(devices - 1)])  3.74 us
    ppermute x1, starting transfers between devices, on_device(): halo = lax.ppermute(tail, BOTH, [(i, i + 1) for i in range(devices - 1)])  3.36 us
  transfers between devices with their start and end apart: 5, of which 2 were waited for; matrix products, arithmetic and copies ran while one was open for 0% of the time, Pallas kernels for 31%

profile of v7, /device:TPU:1, one launch (start us, length us, event | category | flops | bytes accessed | tf_op | source)
XLA Modules:
  0.0 72.9 jit_solution(17916047302420054875)
XLA Ops:
  0.0 1.5 %pack.1 = (f32[4,8,512]{2,1,0:T(8,128)}, bf16[8,1024]{1,0:T(8,128)(2,1)S(1)}, f32[8,2048]{1,0:T(8,128)}) custom-call(f32[4,512]{1,0:T(4,128)} %w_ref.4, f32[1,512]{1,0:T(1,128)} %bitcast.10, f32[1,8]{1,0:T(1,128)} %bitcast.11, f32[1,8]{1,0:T(1,128)} %bitcast.12, f32[1,8]{1,0:T(1,128)} %bitcast.13, f32[4,128]{1,0:T(4,128)} %wbc_ref.1, f32[1,128]{1,0:T(1,128)} %bitcast.14, ...), custom_call_target="tpu_custom_call" | custom-call | tf_op jit(solution)/shard_map/pack/pallas_call | solution.py:144
  1.5 4.8 %all-to-all-start = ((f32[4,8,512]{2,1,0:T(8,128)}), f32[4,8,512]{2,1,0:T(8,128)S(1)}, u32[]{:S(2)}, u32[]{:S(2)}) async-start(f32[4,8,512]{2,1,0:T(8,128)} %get-tuple-element.28), calls=%async_computation | async-start | bytes 131072 | tf_op jit(solution)/shard_map/all_to_all | solution.py:639
  6.3 3.4 %collective-permute-start = (bf16[8,1024]{1,0:T(8,128)(2,1)S(1)}, bf16[8,1024]{1,0:T(8,128)(2,1)S(1)}, u32[]{:S(2)}, u32[]{:S(2)}) collective-permute-start(bf16[8,1024]{1,0:T(8,128)(2,1)S(1)} %get-tuple-element.27), channel_id=1, source_target_pairs={{0,1},{1,2},{2,3},{3,4},{4,5},{5,6},{6,7},{7,8},{8,9},{9,10},{10,1... | collective-permute-start | bytes 49160 | tf_op jit(solution)/shard_map/ppermute | solution.py:640
  9.7 3.7 %collective-permute-done.halo_ref = bf16[8,1024]{1,0:T(8,128)(2,1)S(1)} collective-permute-done((bf16[8,1024]{1,0:T(8,128)(2,1)S(1)}, bf16[8,1024]{1,0:T(8,128)(2,1)S(1)}, u32[]{:S(2)}, u32[]{:S(2)}) %collective-permute-start) | collective-permute-done | bytes 16416 | tf_op jit(solution)/shard_map/ppermute | solution.py:640
  13.5 0.0 all-to-all-done.par
  13.5 10.0 %local_state.1 = (bf16[512,2048]{1,0:T(8,128)(2,1)}, bf16[512,1024]{1,0:T(8,128)(2,1)}, bf16[512,128]{1,0:T(8,128)(2,1)}, f32[512,32]{1,0:T(8,128)}, f32[512,32]...) custom-call(bf16[512,1024]{1,0:T(8,128)(2,1)} %tok_hbm.1, ...), custom_call_target="tpu_custom_call" | custom-call | tf_op jit(solution)/shard_map/local_state/pallas_call | solution.py:70
  23.4 5.3 %all-to-all-start.1 = ((bf16[16,72,128]{2,1,0:T(8,128)(2,1)}), bf16[16,72,128]{2,1,0:T(8,128)(2,1)S(1)}, u32[]{:S(2)}, u32[]{:S(2)}) async-start(bf16[16,72,128]{2,1,0:T(8,128)(2,1)} %get-tuple-element.30), calls=%async_computation.1 | async-start | bytes 589824 | tf_op jit(solution)/shard_map/all_to_all | solution.py:644
  28.7 6.5 %intra.3 = (bf16[512,512]{1,0:T(8,128)(2,1)}, bf16[512,512]{1,0:T(8,128)(2,1)}) custom-call(bf16[512,2048]{1,0:T(8,128)(2,1)} %get-tuple-element.44.xc_ref, bf16[512,1024]{1,0:T(8,128)(2,1)} %get-tuple-element.32.tok_ref, bf16[1024,4096]{1,0:T(8,128)(2,1)} %w_ref.7, bf16[512,128]{1,0:T(8,128)(2,1)} %get-tuple-element.29.bc_ref.bc_hbm, ...), custom_call_target="tpu_custom_call" | custom-call | tf_op jit(solution)/shard_map/intra/pallas_call | solution.py:459
  35.2 1.0 %all-to-all-done.1.in_ref.near_ref = bf16[16,72,128]{2,1,0:T(8,128)(2,1)S(1)} async-done(((bf16[16,72,128]{2,1,0:T(8,128)(2,1)}), bf16[16,72,128]{2,1,0:T(8,128)(2,1)S(1)}, u32[]{:S(2)}, u32[]{:S(2)}) %all-to-all-start.1) | async-done | bytes 294944 | tf_op jit(solution)/shard_map/all_to_all | solution.py:644
  36.2 0.7 fold.1
  37.0 7.4 %all-to-all-start.2 = ((bf16[8,72,128]{2,1,0:T(8,128)(2,1)}), bf16[8,72,128]{2,1,0:T(8,128)(2,1)S(1)}, u32[]{:S(2)}, u32[]{:S(2)}) async-start(bf16[8,72,128]{2,1,0:T(8,128)(2,1)} %fold.1), calls=%async_computation.2 | async-start | bytes 294912 | tf_op jit(solution)/shard_map/all_to_all | solution.py:650
  44.3 8.0 %intra.4 = (bf16[512,768]{1,0:T(8,128)(2,1)}, bf16[512,768]{1,0:T(8,128)(2,1)}) custom-call(bf16[512,2048]{1,0:T(8,128)(2,1)} %get-tuple-element.44.xc_ref, bf16[512,1024]{1,0:T(8,128)(2,1)} %get-tuple-element.32.tok_ref, bf16[1024,4096]{1,0:T(8,128)(2,1)} %w_ref.7, bf16[512,128]{1,0:T(8,128)(2,1)} %get-tuple-element.29.bc_ref.bc_hbm, ...), custom_call_target="tpu_custom_call" | custom-call | tf_op jit(solution)/shard_map/intra/pallas_call | solution.py:459
  52.3 0.0 all-to-all-done.2.far_ref
  52.3 0.8 %unfold.1 = bf16[16,64,128]{2,1,0:T(8,128)(2,1)} custom-call(s32[1]{0:T(128)} %bitcast.7.me_ref, bf16[16,72,128]{2,1,0:T(8,128)(2,1)S(1)} %all-to-all-done.1.in_ref.near_ref, bf16[8,72,128]{2,1,0:T(8,128)(2,1)S(1)} %all-to-all-done.2.far_ref), custom_call_target="tpu_custom_call" | custom-call | tf_op jit(solution)/shard_map/unfold/pallas_call | solution.py:70
  53.1 4.7 %all-to-all-start.3 = ((bf16[16,64,128]{2,1,0:T(8,128)(2,1)}), bf16[16,64,128]{2,1,0:T(8,128)(2,1)S(1)}, u32[]{:S(2)}, u32[]{:S(2)}) async-start(bf16[16,64,128]{2,1,0:T(8,128)(2,1)} %unfold.1), calls=%async_computation.3 | async-start | bytes 524288 | tf_op jit(solution)/shard_map/all_to_all | solution.py:655
  57.8 7.9 %intra.5 = (bf16[512,768]{1,0:T(8,128)(2,1)}, bf16[512,768]{1,0:T(8,128)(2,1)}) custom-call(bf16[512,2048]{1,0:T(8,128)(2,1)} %get-tuple-element.44.xc_ref, bf16[512,1024]{1,0:T(8,128)(2,1)} %get-tuple-element.32.tok_ref, bf16[1024,4096]{1,0:T(8,128)(2,1)} %w_ref.7, bf16[512,128]{1,0:T(8,128)(2,1)} %get-tuple-element.29.bc_ref.bc_hbm, ...), custom_call_target="tpu_custom_call" | custom-call | tf_op jit(solution)/shard_map/intra/pallas_call | solution.py:459
  65.7 0.0 all-to-all-done.3.in_ref
  65.7 7.0 %finish.1 = bf16[512,1024]{1,0:T(8,128)(2,1)} custom-call(bf16[512,128]{1,0:T(8,128)(2,1)} %get-tuple-element.29.bc_ref.bc_hbm, bf16[16,64,128]{2,1,0:T(8,128)(2,1)S(1)} %all-to-all-done.3.in_ref, f32[8,2048]{1,0:T(8,128)} %get-tuple-element.41.gain_hbm, bf16[2048,1024]{1,0:T(8,128)(2,1)} %w_hbm.3, bf16[512,512]{1,0:T(8,128)(2,1)} %get-tuple-element.42.refs_0_, ...), custom_call_target="tpu_custom_call" | custom-call | tf_op jit(solution)/shard_map/finish/pallas_call | solution.py:70
Async XLA Ops:
  1.5 12.0 %all-to-all-start = ((f32[4,8,512]{2,1,0:T(8,128)}), f32[4,8,512]{2,1,0:T(8,128)S(1)}, u32[]{:S(2)}, u32[]{:S(2)}) async-start(f32[4,8,512]{2,1,0:T(8,128)} %get-tuple-element.28), calls=%async_computation | async-start | bytes 131072 | tf_op jit(solution)/shard_map/all_to_all | solution.py:639
  6.3 7.1 %collective-permute-start = (bf16[8,1024]{1,0:T(8,128)(2,1)S(1)}, bf16[8,1024]{1,0:T(8,128)(2,1)S(1)}, u32[]{:S(2)}, u32[]{:S(2)}) collective-permute-start(bf16[8,1024]{1,0:T(8,128)(2,1)S(1)} %get-tuple-element.27), channel_id=1, source_target_pairs={{0,1},{1,2},{2,3},{3,4},{4,5},{5,6},{6,7},{7,8},{8,9},{9,10},{10,1... | collective-permute-start | bytes 49160 | tf_op jit(solution)/shard_map/ppermute | solution.py:640
  23.4 12.8 %all-to-all-start.1 = ((bf16[16,72,128]{2,1,0:T(8,128)(2,1)}), bf16[16,72,128]{2,1,0:T(8,128)(2,1)S(1)}, u32[]{:S(2)}, u32[]{:S(2)}) async-start(bf16[16,72,128]{2,1,0:T(8,128)(2,1)} %get-tuple-element.30), calls=%async_computation.1 | async-start | bytes 589824 | tf_op jit(solution)/shard_map/all_to_all | solution.py:644
  37.0 15.3 %all-to-all-start.2 = ((bf16[8,72,128]{2,1,0:T(8,128)(2,1)}), bf16[8,72,128]{2,1,0:T(8,128)(2,1)S(1)}, u32[]{:S(2)}, u32[]{:S(2)}) async-start(bf16[8,72,128]{2,1,0:T(8,128)(2,1)} %fold.1), calls=%async_computation.2 | async-start | bytes 294912 | tf_op jit(solution)/shard_map/all_to_all | solution.py:650
  53.1 12.6 %all-to-all-start.3 = ((bf16[16,64,128]{2,1,0:T(8,128)(2,1)}), bf16[16,64,128]{2,1,0:T(8,128)(2,1)S(1)}, u32[]{:S(2)}, u32[]{:S(2)}) async-start(bf16[16,64,128]{2,1,0:T(8,128)(2,1)} %unfold.1), calls=%async_computation.3 | async-start | bytes 524288 | tf_op jit(solution)/shard_map/all_to_all | solution.py:655

commit v8 on v7

--- a/solution.py
+++ b/solution.py
@@ -578,16 +578,15 @@
     total = jnp.zeros((rows, 128), F32)
     for copy in small:
         copy.wait()
-    for k in range(CHUNKS):
-        for copy in fetches[k]:
-            copy.wait()
-        side, total = gate(k, total)
-        fetch_w[k].wait()
-        product = dot(side, w_ref[k * span : (k + 1) * span])
-        if k > 0:
-            product = acc[...] + product
-        if k + 1 < CHUNKS:
-            acc[...] = product
+    for copy in fetches[0]:
+        copy.wait()
+    side, total = gate(0, total)
+    for copy in fetches[1] + fetch_w[:1]:
+        copy.wait()
+    acc[...] = dot(side, w_ref[:span])
+    side, total = gate(1, total)
+    fetch_w[1].wait()
+    product = acc[...] + dot(side, w_ref[span:])
     mean = jnp.sum(total, axis=1, keepdims=True) * (1.0 / DINNER)
     product = (product * lax.rsqrt(mean + EPSILON)).astype(BF16)
     order = reorder(back=True)

time: 73.7 us -> 73.9 us (level)
  no operation moved by 1% of the time
where the time goes in v8:
time: 73.9 us; the launch traced here: 73.1 us
  Pallas kernels  42.5 us (58%)
  starting transfers between devices  25.6 us (35%)
  waiting for transfers between devices  4.77 us (6%)
    pallas_call x3, Pallas kernels, intra(): pl.pallas_call(functools.partial(intra_kernel, first_group), grid=(groups...  22.4 us
    pallas_call x4, Pallas kernels, call(): pl.pallas_call(kernel, in_specs=specs, out_specs=[FAR_AWAY if i in far_ou...  18.7 us
    all_to_all x1, starting transfers between devices, on_device(): far = lax.all_to_all(copies, FAR, 0, 0, tiled=True)  7.37 us
    all_to_all x1, starting transfers between devices, on_device(): near = lax.all_to_all(slabs, NEAR, 0, 0, tiled=True)  5.31 us
    all_to_all x1, starting transfers between devices, on_device(): packed = lax.all_to_all(packed, 'head', 0, 0, tiled=True)  4.84 us
    all_to_all x1, starting transfers between devices, on_device(): back = lax.all_to_all(incoming, NEAR, 0, 0, tiled=True)  4.72 us
    ppermute x1, waiting for transfers between devices, on_device(): halo = lax.ppermute(tail, BOTH, [(i, i + 1) for i in range(devices - 1)])  3.74 us
    ppermute x1, starting transfers between devices, on_device(): halo = lax.ppermute(tail, BOTH, [(i, i + 1) for i in range(devices - 1)])  3.36 us
  transfers between devices with their start and end apart: 5, of which 2 were waited for; matrix products, arithmetic and copies ran while one was open for 0% of the time, Pallas kernels for 31%

profile of v8, /device:TPU:1, one launch (start us, length us, event | category | flops | bytes accessed | tf_op | source)
XLA Modules:
  0.0 73.1 jit_solution(14469558702472795180)
XLA Ops:
  0.0 1.5 %pack.1 = (f32[4,8,512]{2,1,0:T(8,128)}, bf16[8,1024]{1,0:T(8,128)(2,1)S(1)}, f32[8,2048]{1,0:T(8,128)}) custom-call(f32[4,512]{1,0:T(4,128)} %w_ref.4, f32[1,512]{1,0:T(1,128)} %bitcast.10, f32[1,8]{1,0:T(1,128)} %bitcast.11, f32[1,8]{1,0:T(1,128)} %bitcast.12, f32[1,8]{1,0:T(1,128)} %bitcast.13, f32[4,128]{1,0:T(4,128)} %wbc_ref.1, f32[1,128]{1,0:T(1,128)} %bitcast.14, ...), custom_call_target="tpu_custom_call" | custom-call | tf_op jit(solution)/shard_map/pack/pallas_call | solution.py:144
  1.5 4.8 %all-to-all-start = ((f32[4,8,512]{2,1,0:T(8,128)}), f32[4,8,512]{2,1,0:T(8,128)S(1)}, u32[]{:S(2)}, u32[]{:S(2)}) async-start(f32[4,8,512]{2,1,0:T(8,128)} %get-tuple-element.28), calls=%async_computation | async-start | bytes 131072 | tf_op jit(solution)/shard_map/all_to_all | solution.py:638
  6.3 3.4 %collective-permute-start = (bf16[8,1024]{1,0:T(8,128)(2,1)S(1)}, bf16[8,1024]{1,0:T(8,128)(2,1)S(1)}, u32[]{:S(2)}, u32[]{:S(2)}) collective-permute-start(bf16[8,1024]{1,0:T(8,128)(2,1)S(1)} %get-tuple-element.27), channel_id=1, source_target_pairs={{0,1},{1,2},{2,3},{3,4},{4,5},{5,6},{6,7},{7,8},{8,9},{9,10},{10,1... | collective-permute-start | bytes 49160 | tf_op jit(solution)/shard_map/ppermute | solution.py:639
  9.7 3.7 %collective-permute-done.halo_ref = bf16[8,1024]{1,0:T(8,128)(2,1)S(1)} collective-permute-done((bf16[8,1024]{1,0:T(8,128)(2,1)S(1)}, bf16[8,1024]{1,0:T(8,128)(2,1)S(1)}, u32[]{:S(2)}, u32[]{:S(2)}) %collective-permute-start) | collective-permute-done | bytes 16416 | tf_op jit(solution)/shard_map/ppermute | solution.py:639
  13.5 0.0 all-to-all-done.par
  13.5 10.0 %local_state.1 = (bf16[512,2048]{1,0:T(8,128)(2,1)}, bf16[512,1024]{1,0:T(8,128)(2,1)}, bf16[512,128]{1,0:T(8,128)(2,1)}, f32[512,32]{1,0:T(8,128)}, f32[512,32]...) custom-call(bf16[512,1024]{1,0:T(8,128)(2,1)} %tok_hbm.1, ...), custom_call_target="tpu_custom_call" | custom-call | tf_op jit(solution)/shard_map/local_state/pallas_call | solution.py:70
  23.4 5.3 %all-to-all-start.1 = ((bf16[16,72,128]{2,1,0:T(8,128)(2,1)}), bf16[16,72,128]{2,1,0:T(8,128)(2,1)S(1)}, u32[]{:S(2)}, u32[]{:S(2)}) async-start(bf16[16,72,128]{2,1,0:T(8,128)(2,1)} %get-tuple-element.30), calls=%async_computation.1 | async-start | bytes 589824 | tf_op jit(solution)/shard_map/all_to_all | solution.py:643
  28.7 6.5 %intra.3 = (bf16[512,512]{1,0:T(8,128)(2,1)}, bf16[512,512]{1,0:T(8,128)(2,1)}) custom-call(bf16[512,2048]{1,0:T(8,128)(2,1)} %get-tuple-element.44.xc_ref, bf16[512,1024]{1,0:T(8,128)(2,1)} %get-tuple-element.32.tok_ref, bf16[1024,4096]{1,0:T(8,128)(2,1)} %w_ref.7, bf16[512,128]{1,0:T(8,128)(2,1)} %get-tuple-element.29.bc_ref.bc_hbm, ...), custom_call_target="tpu_custom_call" | custom-call | tf_op jit(solution)/shard_map/intra/pallas_call | solution.py:459
  35.2 1.0 %all-to-all-done.1.in_ref.near_ref = bf16[16,72,128]{2,1,0:T(8,128)(2,1)S(1)} async-done(((bf16[16,72,128]{2,1,0:T(8,128)(2,1)}), bf16[16,72,128]{2,1,0:T(8,128)(2,1)S(1)}, u32[]{:S(2)}, u32[]{:S(2)}) %all-to-all-start.1) | async-done | bytes 294944 | tf_op jit(solution)/shard_map/all_to_all | solution.py:643
  36.2 0.7 fold.1
  37.0 7.4 %all-to-all-start.2 = ((bf16[8,72,128]{2,1,0:T(8,128)(2,1)}), bf16[8,72,128]{2,1,0:T(8,128)(2,1)S(1)}, u32[]{:S(2)}, u32[]{:S(2)}) async-start(bf16[8,72,128]{2,1,0:T(8,128)(2,1)} %fold.1), calls=%async_computation.2 | async-start | bytes 294912 | tf_op jit(solution)/shard_map/all_to_all | solution.py:649
  44.3 8.0 %intra.4 = (bf16[512,768]{1,0:T(8,128)(2,1)}, bf16[512,768]{1,0:T(8,128)(2,1)}) custom-call(bf16[512,2048]{1,0:T(8,128)(2,1)} %get-tuple-element.44.xc_ref, bf16[512,1024]{1,0:T(8,128)(2,1)} %get-tuple-element.32.tok_ref, bf16[1024,4096]{1,0:T(8,128)(2,1)} %w_ref.7, bf16[512,128]{1,0:T(8,128)(2,1)} %get-tuple-element.29.bc_ref.bc_hbm, ...), custom_call_target="tpu_custom_call" | custom-call | tf_op jit(solution)/shard_map/intra/pallas_call | solution.py:459
  52.3 0.0 all-to-all-done.2.far_ref
  52.3 0.8 %unfold.1 = bf16[16,64,128]{2,1,0:T(8,128)(2,1)} custom-call(s32[1]{0:T(128)} %bitcast.7.me_ref, bf16[16,72,128]{2,1,0:T(8,128)(2,1)S(1)} %all-to-all-done.1.in_ref.near_ref, bf16[8,72,128]{2,1,0:T(8,128)(2,1)S(1)} %all-to-all-done.2.far_ref), custom_call_target="tpu_custom_call" | custom-call | tf_op jit(solution)/shard_map/unfold/pallas_call | solution.py:70
  53.1 4.7 %all-to-all-start.3 = ((bf16[16,64,128]{2,1,0:T(8,128)(2,1)}), bf16[16,64,128]{2,1,0:T(8,128)(2,1)S(1)}, u32[]{:S(2)}, u32[]{:S(2)}) async-start(bf16[16,64,128]{2,1,0:T(8,128)(2,1)} %unfold.1), calls=%async_computation.3 | async-start | bytes 524288 | tf_op jit(solution)/shard_map/all_to_all | solution.py:654
  57.8 7.9 %intra.5 = (bf16[512,768]{1,0:T(8,128)(2,1)}, bf16[512,768]{1,0:T(8,128)(2,1)}) custom-call(bf16[512,2048]{1,0:T(8,128)(2,1)} %get-tuple-element.44.xc_ref, bf16[512,1024]{1,0:T(8,128)(2,1)} %get-tuple-element.32.tok_ref, bf16[1024,4096]{1,0:T(8,128)(2,1)} %w_ref.7, bf16[512,128]{1,0:T(8,128)(2,1)} %get-tuple-element.29.bc_ref.bc_hbm, ...), custom_call_target="tpu_custom_call" | custom-call | tf_op jit(solution)/shard_map/intra/pallas_call | solution.py:459
  65.7 0.0 all-to-all-done.3.in_ref
  65.7 7.2 %finish.1 = bf16[512,1024]{1,0:T(8,128)(2,1)} custom-call(bf16[512,128]{1,0:T(8,128)(2,1)} %get-tuple-element.29.bc_ref.bc_hbm, bf16[16,64,128]{2,1,0:T(8,128)(2,1)S(1)} %all-to-all-done.3.in_ref, f32[8,2048]{1,0:T(8,128)} %get-tuple-element.41.gain_hbm, bf16[2048,1024]{1,0:T(8,128)(2,1)} %w_hbm.3, bf16[512,512]{1,0:T(8,128)(2,1)} %get-tuple-element.42.refs_0_, ...), custom_call_target="tpu_custom_call" | custom-call | tf_op jit(solution)/shard_map/finish/pallas_call | solution.py:70
Async XLA Ops:
  1.5 12.0 %all-to-all-start = ((f32[4,8,512]{2,1,0:T(8,128)}), f32[4,8,512]{2,1,0:T(8,128)S(1)}, u32[]{:S(2)}, u32[]{:S(2)}) async-start(f32[4,8,512]{2,1,0:T(8,128)} %get-tuple-element.28), calls=%async_computation | async-start | bytes 131072 | tf_op jit(solution)/shard_map/all_to_all | solution.py:638
  6.3 7.1 %collective-permute-start = (bf16[8,1024]{1,0:T(8,128)(2,1)S(1)}, bf16[8,1024]{1,0:T(8,128)(2,1)S(1)}, u32[]{:S(2)}, u32[]{:S(2)}) collective-permute-start(bf16[8,1024]{1,0:T(8,128)(2,1)S(1)} %get-tuple-element.27), channel_id=1, source_target_pairs={{0,1},{1,2},{2,3},{3,4},{4,5},{5,6},{6,7},{7,8},{8,9},{9,10},{10,1... | collective-permute-start | bytes 49160 | tf_op jit(solution)/shard_map/ppermute | solution.py:639
  23.4 12.8 %all-to-all-start.1 = ((bf16[16,72,128]{2,1,0:T(8,128)(2,1)}), bf16[16,72,128]{2,1,0:T(8,128)(2,1)S(1)}, u32[]{:S(2)}, u32[]{:S(2)}) async-start(bf16[16,72,128]{2,1,0:T(8,128)(2,1)} %get-tuple-element.30), calls=%async_computation.1 | async-start | bytes 589824 | tf_op jit(solution)/shard_map/all_to_all | solution.py:643
  37.0 15.3 %all-to-all-start.2 = ((bf16[8,72,128]{2,1,0:T(8,128)(2,1)}), bf16[8,72,128]{2,1,0:T(8,128)(2,1)S(1)}, u32[]{:S(2)}, u32[]{:S(2)}) async-start(bf16[8,72,128]{2,1,0:T(8,128)(2,1)} %fold.1), calls=%async_computation.2 | async-start | bytes 294912 | tf_op jit(solution)/shard_map/all_to_all | solution.py:649
  53.1 12.6 %all-to-all-start.3 = ((bf16[16,64,128]{2,1,0:T(8,128)(2,1)}), bf16[16,64,128]{2,1,0:T(8,128)(2,1)S(1)}, u32[]{:S(2)}, u32[]{:S(2)}) async-start(bf16[16,64,128]{2,1,0:T(8,128)(2,1)} %unfold.1), calls=%async_computation.3 | async-start | bytes 524288 | tf_op jit(solution)/shard_map/all_to_all | solution.py:654
